TPU v7x, 256 devices: a whole 4x4x8 slice. The times are simulated.
256 devices in a mesh: pts: 64 (over z, x, core), cen: 4 (over y).
Axes of the slice: x: 4, y: 4, z: 8, core: 2. Of those that a mesh axis runs over, the one named last changes fastest.
Arguments:
- points: bfloat16 [131072, 768], P('pts'), may hold values from -16 to 16
- centroids: bfloat16 [4096, 768], P('cen'), may hold values from -1 to 1
Outputs:
- new_centroids: bfloat16 [4096, 768], P(('cen', 'pts'))
- distances: float32 [131072], P('pts')
All inputs are finite; a program needn't handle non-finite values.
Results may differ from a plain program's by a relative error of at most 0.0034.
Values may be sent and summed in bfloat16 or wider, within the bound.
No kernel may reach another device: no remote copies, remote signals or barrier semaphores. Data moves between devices by JAX's collectives and lax.ppermute only.
A program may use at most 64 MiB of HBM per device.

v0:
```python
import math

import jax
import jax.numpy as jnp
from jax import lax
from jax.sharding import PartitionSpec as P

ITERS = 3


sharpness = 4.0


def merged(value, axis, join):
    pieces = jax.tree.map(lambda part: lax.all_gather(part, axis), value)
    head = jax.tree.map(lambda part: part[0], pieces)
    tail = jax.tree.map(lambda part: part[1:], pieces)
    subtotal, _ = lax.scan(lambda subtotal, piece: (join(subtotal, piece), None), head, tail)
    return subtotal


def logits(points, centroids):
    product = lax.dot_general(
        points, centroids, (((1,), (1,)), ((), ())), preferred_element_type=jnp.float32
    )
    return sharpness * product


def combine_lse(earlier, later):
    joined_max = jnp.maximum(earlier[0], later[0])
    summed = earlier[1] * jnp.exp(earlier[0] - joined_max) + later[1] * jnp.exp(
        later[0] - joined_max
    )
    return (joined_max, summed)


def on_device(points, centroids):
    pts_devices = lax.axis_size("pts")
    total_points = points.shape[0] * pts_devices
    local_centroids = centroids.shape[0]
    total_centroids = local_centroids * lax.axis_size("cen")
    width = points.shape[1]
    stored_scores = logits(points, centroids)

    def current_scores():
        return stored_scores

    col_potential = jnp.zeros((local_centroids,), jnp.float32)
    row_potential = jnp.zeros((points.shape[0],), jnp.float32)
    for iteration in range(ITERS):
        shifted = current_scores() + col_potential[None, :]
        highest = jnp.max(shifted, axis=1)
        summed = jnp.sum(jnp.exp(shifted - highest[:, None]), axis=1)
        highest, summed = merged((highest, summed), "cen", combine_lse)
        row_potential = -math.log(total_points) - (highest + jnp.log(summed))
        shifted = current_scores() + row_potential[:, None]
        highest = lax.pmax(jnp.max(shifted, axis=0), "pts")
        summed = lax.psum(jnp.sum(jnp.exp(shifted - highest[None, :]), axis=0), "pts")
        col_potential = -math.log(total_centroids) - (highest + jnp.log(summed))
    transport = jnp.exp(current_scores() + row_potential[:, None] + col_potential[None, :])
    weights = transport.astype(jnp.bfloat16)
    rows_each = local_centroids // pts_devices
    product = lax.dot_general(
        weights, points, (((0,), (0,)), ((), ())), preferred_element_type=jnp.float32
    )
    partial_sums = total_centroids * product
    gathered_block = lax.psum(partial_sums, "pts").astype(jnp.bfloat16)
    own_rows = lax.dynamic_slice_in_dim(
        gathered_block, lax.axis_index("pts") * rows_each, rows_each, 0
    )
    block_float = gathered_block.astype(jnp.float32)
    squares = jnp.sum(block_float * block_float, axis=1)
    cross_terms = lax.dot_general(
        points, gathered_block, (((1,), (1,)), ((), ())), preferred_element_type=jnp.float32
    )
    numerator = jnp.sum(transport * (squares[None, :] - 2.0 * cross_terms), axis=1)
    row_mass = jnp.sum(transport, axis=1)
    numerator, row_mass = lax.psum((numerator, row_mass), "cen")
    distances = numerator / row_mass / width
    return (own_rows, distances)


def solution(mesh):
    in_specs = (P("pts", None), P("cen", None))
    out_specs = (P(("cen", "pts"), None), P("pts"))
    return jax.shard_map(
        on_device, mesh=mesh, in_specs=in_specs, out_specs=out_specs, check_vma=False
    )
```

profile of v0, /device:TPU:2, one launch (start us, length us, event | category | flops | bytes accessed | tf_op | source)
XLA Modules:
  0.0 1190.4 jit_solution(11087072551796998977)
XLA Ops:
  0.6 0.0 copy-start
  0.6 1.9 copy-done
  2.5 7.0 fusion.10
  9.6 12.4 %all-gather = f32[8192]{0:T(1024)S(1)} all-gather(f32[2048]{0:T(1024)S(1)} %get-tuple-element.136), channel_id=2, replica_groups=mesh['pts'=64,'cen'=4] {'cen'}, dimensions={0}, use_global_device_ids=true | all-gather | bytes 40960 | tf_op jit(solution)/shard_map/all_gather | solution.py:15
  22.0 4.6 exponential_reduce_fusion.5
  26.5 11.9 %all-gather.1 = f32[8192]{0:T(1024)S(1)} all-gather(f32[2048]{0:T(1024)S(1)} %exponential_reduce_fusion.5), channel_id=3, replica_groups=mesh['pts'=64,'cen'=4] {'cen'}, dimensions={0}, use_global_device_ids=true | all-gather | bytes 40960 | tf_op jit(solution)/shard_map/all_gather | solution.py:15
  38.5 0.2 while.36
  38.7 4.0 add_reduce_fusion.3
  42.7 121.6 %pmax.21 = f32[1024]{0:T(1024)S(1)} all-reduce(f32[1024]{0:T(1024)S(1)} %add_reduce_fusion.3), channel_id=1, replica_groups=mesh['pts'=64,'cen'=4] {'pts'}, use_global_device_ids=true, to_apply=%region_5.6 | all-reduce | flops 1024 | bytes 8192 | tf_op jit(solution)/shard_map/pmax | solution.py:57
  164.4 4.4 exponential_reduce_fusion.4
  168.7 124.4 %psum.42 = f32[1024]{0:T(1024)S(1)} all-reduce(f32[1024]{0:T(1024)S(1)} %exponential_reduce_fusion.4), channel_id=1, replica_groups=mesh['pts'=64,'cen'=4] {'pts'}, use_global_device_ids=true, to_apply=%region_7.8 | all-reduce | flops 1024 | bytes 8192 | tf_op jit(solution)/shard_map/psum | solution.py:58
  293.1 4.0 add_reduce_fusion.2
  297.1 11.9 %all-gather.2 = f32[8192]{0:T(1024)S(1)} all-gather(f32[2048]{0:T(1024)S(1)} %add_reduce_fusion.2), channel_id=4, replica_groups=mesh['pts'=64,'cen'=4] {'cen'}, dimensions={0}, use_global_device_ids=true | all-gather | bytes 40960 | tf_op jit(solution)/shard_map/all_gather | solution.py:15
  309.1 4.3 exponential_reduce_fusion.3
  313.4 11.9 %all-gather.3 = f32[8192]{0:T(1024)S(1)} all-gather(f32[2048]{0:T(1024)S(1)} %exponential_reduce_fusion.3), channel_id=5, replica_groups=mesh['pts'=64,'cen'=4] {'cen'}, dimensions={0}, use_global_device_ids=true | all-gather | bytes 40960 | tf_op jit(solution)/shard_map/all_gather | solution.py:15
  325.4 0.2 while.37
  325.6 4.0 add_reduce_fusion.1
  329.6 124.1 %pmax.22 = f32[1024]{0:T(1024)S(1)} all-reduce(f32[1024]{0:T(1024)S(1)} %add_reduce_fusion.1), channel_id=1, replica_groups=mesh['pts'=64,'cen'=4] {'pts'}, use_global_device_ids=true, to_apply=%region_13.14 | all-reduce | flops 1024 | bytes 8192 | tf_op jit(solution)/shard_map/pmax | solution.py:57
  453.6 4.4 exponential_reduce_fusion.2
  458.0 124.1 %psum.43 = f32[1024]{0:T(1024)S(1)} all-reduce(f32[1024]{0:T(1024)S(1)} %exponential_reduce_fusion.2), channel_id=1, replica_groups=mesh['pts'=64,'cen'=4] {'pts'}, use_global_device_ids=true, to_apply=%region_15.16 | all-reduce | flops 1024 | bytes 8192 | tf_op jit(solution)/shard_map/psum | solution.py:58
  582.1 4.0 add_reduce_fusion
  586.1 11.9 %all-gather.4 = f32[8192]{0:T(1024)S(1)} all-gather(f32[2048]{0:T(1024)S(1)} %add_reduce_fusion), channel_id=6, replica_groups=mesh['pts'=64,'cen'=4] {'cen'}, dimensions={0}, use_global_device_ids=true | all-gather | bytes 40960 | tf_op jit(solution)/shard_map/all_gather | solution.py:15
  598.0 4.3 exponential_reduce_fusion.1
  602.3 11.9 %all-gather.5 = f32[8192]{0:T(1024)S(1)} all-gather(f32[2048]{0:T(1024)S(1)} %exponential_reduce_fusion.1), channel_id=7, replica_groups=mesh['pts'=64,'cen'=4] {'cen'}, dimensions={0}, use_global_device_ids=true | all-gather | bytes 40960 | tf_op jit(solution)/shard_map/all_gather | solution.py:15
  614.3 0.2 while.38
  614.5 4.0 add_reduce_fusion.4
  618.5 124.1 %pmax.23 = f32[1024]{0:T(1024)S(1)} all-reduce(f32[1024]{0:T(1024)S(1)} %add_reduce_fusion.4), channel_id=1, replica_groups=mesh['pts'=64,'cen'=4] {'pts'}, use_global_device_ids=true, to_apply=%region_21.22 | all-reduce | flops 1024 | bytes 8192 | tf_op jit(solution)/shard_map/pmax | solution.py:57
  742.6 4.4 exponential_reduce_fusion
  746.9 124.2 %psum.44 = f32[1024]{0:T(1024)S(1)} all-reduce(f32[1024]{0:T(1024)S(1)} %exponential_reduce_fusion), channel_id=1, replica_groups=mesh['pts'=64,'cen'=4] {'pts'}, use_global_device_ids=true, to_apply=%region_23.24 | all-reduce | flops 1024 | bytes 8192 | tf_op jit(solution)/shard_map/psum | solution.py:58
  871.2 8.8 fusion.7
  879.9 278.9 %all-reduce.2 = bf16[1024,768]{1,0:T(8,128)(2,1)} all-reduce(f32[1024,768]{1,0:T(8,128)} %fusion.7), channel_id=1, replica_groups=mesh['pts'=64,'cen'=4] {'pts'}, use_global_device_ids=true, to_apply=%region_24.25 | all-reduce | flops 786432 | bytes 4718592 | tf_op jit(solution)/shard_map/psum | solution.py:67
  1158.8 1.3 constant_dynamic-slice_fusion.6
  1160.2 1.8 multiply_reduce_fusion
  1161.9 6.9 fusion
  1168.9 4.3 fusion.1
  1173.2 16.6 %all-reduce = (f32[2048]{0:T(1024)S(1)}, f32[2048]{0:T(1024)S(1)}) all-reduce(f32[2048]{0:T(1024)S(1)} %fusion, f32[2048]{0:T(1024)S(1)} %fusion.1), channel_id=1, replica_groups=mesh['pts'=64,'cen'=4] {'cen'}, use_global_device_ids=true, to_apply=%region_27.28 | all-reduce | flops 4096 | bytes 32768 | tf_op jit(solution)/shard_map/psum | solution.py:78
  1189.8 0.6 divide_multiply_fusion
  (42 shorter events, 0.5 us)
Async XLA Ops:
  0.6 1.9 copy-start
where the time goes:
time: 1190 us
  blocking collectives  1110 us (93%)
  other arithmetic  53.1 us (4%)
  matrix products  22.7 us (2%)
    psum x3, blocking collectives, on_device(): lax.psum(jnp.sum(jnp.exp(shifted - highest[None, :]), axis=0), 'pts')  373 us
    pmax x3, blocking collectives, on_device(): highest = lax.pmax(jnp.max(shifted, axis=0), 'pts')  370 us
    psum x1, blocking collectives, on_device(): gathered_block = lax.psum(partial_sums, 'pts').astype(jnp.bfloat16)  279 us
    all_gather x6, blocking collectives, merged(): pieces = jax.tree.map(lambda part: lax.all_gather(part, axis), value)  72 us

commit v1 on v0

v1 whole, which is shorter than its diff:
```python
import math

import jax
import jax.numpy as jnp
from jax import lax
from jax.sharding import PartitionSpec as P

ITERS = 3


sharpness = 4.0
LOG2E = math.log2(math.e)
C = 2


def other_core(value):
    size = lax.axis_size("pts")
    return lax.ppermute(value, "pts", [(i, i ^ 1) for i in range(size)])


def chip_groups():
    size = lax.axis_size("pts")
    return [[chip * C + core for chip in range(size // C)] for core in range(C)]


def exchange(value):
    return lax.all_to_all(value, "pts", 0, 0, axis_index_groups=chip_groups())


def from_chips(value):
    chips = lax.axis_size("pts") // C
    return exchange(jnp.broadcast_to(value[None], (chips,) + value.shape))


def cen_shift(value, step):
    size = lax.axis_size("cen")
    return lax.ppermute(value, "cen", [(i, (i + step) % size) for i in range(size)])


def merged_rows(value):
    one, two, three = [cen_shift(value, step) for step in (1, 2, 3)]
    top = jnp.maximum(jnp.maximum(value, two), jnp.maximum(one, three))
    even = jnp.exp2(value - top) + jnp.exp2(two - top)
    odd = jnp.exp2(one - top) + jnp.exp2(three - top)
    return top + jnp.log2(even + odd)


def merged_cols(value):
    theirs = other_core(value)
    top = jnp.maximum(value, theirs)
    value = top + jnp.log2(jnp.exp2(value - top) + jnp.exp2(theirs - top))
    values = from_chips(value)
    top = jnp.max(values, axis=0)
    return top + jnp.log2(jnp.sum(jnp.exp2(values - top[None]), axis=0))


def scattered(partial):
    core = lax.axis_index("pts") % C
    chips = lax.axis_size("pts") // C
    rows, width = partial.shape
    parts = partial.reshape(chips, C, rows // (chips * C), width)
    keep = lax.dynamic_index_in_dim(parts, core, 1, keepdims=False)
    give = lax.dynamic_index_in_dim(parts, 1 - core, 1, keepdims=False)
    theirs = other_core(give.astype(jnp.bfloat16)).astype(jnp.float32)
    pieces = exchange((keep + theirs).astype(jnp.bfloat16))
    return jnp.sum(pieces.astype(jnp.float32), axis=0)


def collected(own):
    core = lax.axis_index("pts") % C
    mine = from_chips(own)
    theirs = other_core(mine)
    first = jnp.where(core == 0, mine, theirs)
    second = jnp.where(core == 0, theirs, mine)
    return jnp.stack([first, second], axis=1).reshape(-1, own.shape[-1])


def on_device(points, centroids):
    total_points = points.shape[0] * lax.axis_size("pts")
    total_centroids = centroids.shape[0] * lax.axis_size("cen")
    width = points.shape[1]
    scores = (sharpness * LOG2E) * lax.dot_general(
        points, centroids, (((1,), (1,)), ((), ())), preferred_element_type=jnp.float32
    )
    col_potential = jnp.zeros((centroids.shape[0],), jnp.float32)
    for iteration in range(ITERS):
        shifted = scores + col_potential[None, :]
        highest = jnp.max(shifted, axis=1)
        summed = jnp.sum(jnp.exp2(shifted - highest[:, None]), axis=1)
        row_potential = -math.log2(total_points) - merged_rows(highest + jnp.log2(summed))
        shifted = scores + row_potential[:, None]
        highest = jnp.max(shifted, axis=0)
        summed = jnp.sum(jnp.exp2(shifted - highest[None, :]), axis=0)
        col_potential = -math.log2(total_centroids) - merged_cols(highest + jnp.log2(summed))
    transport = jnp.exp2(scores + row_potential[:, None] + col_potential[None, :])
    partial = lax.dot_general(
        transport.astype(jnp.bfloat16),
        points,
        (((0,), (0,)), ((), ())),
        preferred_element_type=jnp.float32,
    )
    own_rows = (total_centroids * scattered(partial)).astype(jnp.bfloat16)
    gathered = collected(own_rows)
    as_float = gathered.astype(jnp.float32)
    squares = jnp.sum(as_float * as_float, axis=1)
    cross_terms = lax.dot_general(
        points, gathered, (((1,), (1,)), ((), ())), preferred_element_type=jnp.float32
    )
    numerator = jnp.sum(transport * (squares[None, :] - 2.0 * cross_terms), axis=1)
    row_mass = jnp.sum(transport, axis=1)
    both = jnp.stack([numerator, row_mass])
    one, two, three = [cen_shift(both, step) for step in (1, 2, 3)]
    total = (both + two) + (one + three)
    distances = total[0] / total[1] / width
    return (own_rows, distances)


def solution(mesh):
    in_specs = (P("pts", None), P("cen", None))
    out_specs = (P(("cen", "pts"), None), P("pts"))
    return jax.shard_map(
        on_device, mesh=mesh, in_specs=in_specs, out_specs=out_specs, check_vma=False
    )
```

time: 1190 us -> 204 us (0.17)
  blocking collectives: 1110 us -> 89.7 us
  waiting for transfers between devices: 0 us -> 26 us
  starting transfers between devices: 0 us -> 25.2 us
  other arithmetic: 53.1 us -> 36.2 us
    psum x5 -> x0, blocking collectives: 668 us -> none  [the longest x3 373 us: on_device(): lax.psum(jnp.sum(jnp.exp(shifted - highest[None, :]), axis=0), 'pts')]
    pmax x3 -> x0, blocking collectives: 370 us -> none  [on_device(): highest = lax.pmax(jnp.max(shifted, axis=0), 'pts')]
    all_to_all x0 -> x4, blocking collectives: none -> 89.7 us  [exchange(): return lax.all_to_all(value, 'pts', 0, 0, axis_index_groups=chip_groups())]
    all_gather x6 -> x0, blocking collectives: 72 us -> none  [merged(): pieces = jax.tree.map(lambda part: lax.all_gather(part, axis), value)]
    ppermute x0 -> x17, starting transfers between devices: none -> 19.7 us  [the longest x12 19.5 us: cen_shift(): lax.ppermute(value, 'cen', [(i, (i + step) % size) for i in range(size)])]
    ppermute x0 -> x17, waiting for transfers between devices: none -> 16.7 us  [the longest x12 10.6 us: cen_shift(): lax.ppermute(value, 'cen', [(i, (i + step) % size) for i in range(size)])]
    reduce_sum x7 -> x11, other arithmetic: 28 us -> 15.6 us  [the longest x3 8.32 us: on_device(): summed = jnp.sum(jnp.exp2(shifted - highest[:, None]), axis=1)]
  transfers between devices with their start and end apart: 0 -> 18, of which waited for: 0 -> 13; matrix products, arithmetic and copies ran while one was open for 0% -> 2% of each run, Pallas kernels for 0% -> 0%
where the time goes in v1:
time: 204 us
  blocking collectives  89.7 us (44%)
  other arithmetic  36.2 us (18%)
  waiting for transfers between devices  26 us (13%)
  starting transfers between devices  25.2 us (12%)
  matrix products  18.5 us (9%)
  local copies, waits for them, and re-layouts  7.22 us (4%)
    all_to_all x4, blocking collectives, exchange(): return lax.all_to_all(value, 'pts', 0, 0, axis_index_groups=chip_groups())  89.7 us
    ppermute x12, starting transfers between devices, cen_shift(): lax.ppermute(value, 'cen', [(i, (i + step) % size) for i in range(size)])  19.5 us
    ppermute x12, waiting for transfers between devices, cen_shift(): lax.ppermute(value, 'cen', [(i, (i + step) % size) for i in range(size)])  10.6 us
    all_to_all x1, waiting for transfers between devices, exchange(): return lax.all_to_all(value, 'pts', 0, 0, axis_index_groups=chip_groups())  9.25 us
    reduce_sum x3, other arithmetic, on_device(): summed = jnp.sum(jnp.exp2(shifted - highest[:, None]), axis=1)  8.32 us
    reduce_max x2, other arithmetic, on_device(): highest = jnp.max(shifted, axis=1)  8.31 us
    dot_general x1, matrix products, on_device(): lax.dot_general(points, gathered, (((1,), (1,)), ((), ())), preferred_ele...  7.25 us
    reduce_sum x3, other arithmetic, on_device(): summed = jnp.sum(jnp.exp2(shifted - highest[None, :]), axis=0)  6.64 us
  transfers between devices with their start and end apart: 18, of which 13 were waited for; matrix products, arithmetic and copies ran while one was open for 2% of the time, Pallas kernels for 0%

profile of v1, /device:TPU:2, one launch (start us, length us, event | category | flops | bytes accessed | tf_op | source)
XLA Modules:
  0.0 203.8 jit_solution(1362470761114973780)
XLA Ops:
  0.6 1.9 copy-done
  2.5 4.9 %fusion.42 = (f32[2048]{0:T(1024)S(1)}, f32[2048,1024]{0,1:T(8,128)S(1)}) fusion(bf16[2048,768]{1,0:T(8,128)(2,1)S(1)} %copy-done, bf16[1024,768]{1,0:T(8,128)(2,1)} %param.3), kind=kOutput, calls=%fused_computation.93 | convolution fusion | flops 3225417728 | bytes 13115392 | tf_op jit(solution)/shard_map/dot_general | solution.py:82
  7.4 1.4 exponential_reduce_fusion.5
  8.8 3.3 %collective-permute-start = (f32[2048]{0:T(1024)S(1)}, f32[2048]{0:T(1024)S(1)}, u32[]{:S(2)}, u32[]{:S(2)}) collective-permute-start(f32[2048]{0:T(1024)S(1)} %multiply_add_fusion.2), channel_id=1, source_target_pairs={{0,2},{1,3},{2,0},{3,1},{4,6},{5,7},{6,4},{7,5},{8,10},{9,11},{10,... | collective-permute-start | bytes 24584 | tf_op jit(solution)/shard_map/ppermute | solution.py:37
  12.1 0.7 collective-permute-start.1
  12.8 2.6 %collective-permute-start.2 = (f32[2048]{0:T(1024)S(1)}, f32[2048]{0:T(1024)S(1)}, u32[]{:S(2)}, u32[]{:S(2)}) collective-permute-start(f32[2048]{0:T(1024)S(1)} %multiply_add_fusion.2), channel_id=1, source_target_pairs={{0,3},{1,0},{2,1},{3,2},{4,7},{5,4},{6,5},{7,6},{8,11},{9,8},{10,9... | collective-permute-start | bytes 24584 | tf_op jit(solution)/shard_map/ppermute | solution.py:37
  15.3 1.6 collective-permute-done.1
  17.0 0.6 add_reduce_fusion.3
  17.6 2.2 %exponential_reduce_fusion.4 = f32[1024]{0:T(1024)S(1)} fusion(f32[2048,1024]{0,1:T(8,128)S(1)} %get-tuple-element.5, f32[1024]{0:T(1024)S(1)} %add_reduce_fusion.3, f32[2048]{0:T(1024)S(1)} %add_subtract_fusion.2), kind=kLoop, calls=%fused_computation.7 | loop fusion | flops 8387584 | bytes 8404992 | tf_op jit(solution)/shard_map/reduce_sum | solution.py:93
  19.9 1.2 collective-permute-done.3
  21.2 20.5 %all_to_all.37 = f32[32,1,1024]{2,1,0:T(1,128)S(1)} all-to-all(f32[32,1,1024]{2,1,0:T(1,128)S(1)} %broadcast_in_dim.8), channel_id=1, replica_groups={{0,8,16,24,32,40,48,56,64,72,80,88,96,104,112,120,128,136,144,152,160,1..., dimensions={0} | all-to-all | bytes 262144 | tf_op jit(solution)/shard_map/all_to_all | solution.py:27
  41.9 4.2 %add_reduce_fusion.2 = f32[2048]{0:T(1024)S(1)} fusion(f32[2048,1024]{0,1:T(8,128)} %copy-done.1, f32[1024]{0:T(1024)S(1)} %add_subtract_fusion.5), kind=kLoop, calls=%fused_computation.11 | loop fusion | flops 4192256 | bytes 8400896 | tf_op jit(solution)/shard_map/reduce_max | solution.py:88
  46.0 1.5 copy-done.2
  47.6 2.3 %exponential_reduce_fusion.3 = f32[2048]{0:T(1024)S(1)} fusion(f32[2048,1024]{0,1:T(8,128)S(1)} %copy-done.2, f32[2048]{0:T(1024)S(1)} %add_reduce_fusion.2, f32[1024]{0:T(1024)S(1)} %add_subtract_fusion.5), kind=kLoop, calls=%fused_computation.6 | loop fusion | flops 8386560 | bytes 8409088 | tf_op jit(solution)/shard_map/reduce_sum | solution.py:89
  49.8 1.5 collective-permute-start.4
  51.4 2.6 %collective-permute-start.5 = (f32[2048]{0:T(1024)S(1)}, f32[2048]{0:T(1024)S(1)}, u32[]{:S(2)}, u32[]{:S(2)}) collective-permute-start(f32[2048]{0:T(1024)S(1)} %multiply_add_fusion.1), channel_id=1, source_target_pairs={{0,1},{1,2},{2,3},{3,0},{4,5},{5,6},{6,7},{7,4},{8,9},{9,10},{10,1... | collective-permute-start | bytes 24584 | tf_op jit(solution)/shard_map/ppermute | solution.py:37
  55.1 1.2 collective-permute-done.5
  56.3 1.4 collective-permute-done.6
  57.7 0.6 add_reduce_fusion.1
  58.3 2.2 %exponential_reduce_fusion.2 = f32[1024]{0:T(1024)S(1)} fusion(f32[2048,1024]{0,1:T(8,128)S(1)} %copy-done.2, f32[1024]{0:T(1024)S(1)} %add_reduce_fusion.1, f32[2048]{0:T(1024)S(1)} %add_subtract_fusion.1), kind=kLoop, calls=%fused_computation.5 | loop fusion | flops 8387584 | bytes 8404992 | tf_op jit(solution)/shard_map/reduce_sum | solution.py:93
  60.7 1.2 collective-permute-done.7
  61.9 14.1 %all_to_all.38 = f32[32,1,1024]{2,1,0:T(1,128)S(1)} all-to-all(f32[32,1,1024]{2,1,0:T(1,128)S(1)} %broadcast_in_dim.9), channel_id=1, replica_groups={{0,8,16,24,32,40,48,56,64,72,80,88,96,104,112,120,128,136,144,152,160,1..., dimensions={0} | all-to-all | bytes 262144 | tf_op jit(solution)/shard_map/all_to_all | solution.py:27
  76.2 4.2 %add_reduce_fusion = f32[2048]{0:T(1024)S(1)} fusion(f32[2048,1024]{0,1:T(8,128)} %copy-done.1, f32[1024]{0:T(1024)S(1)} %add_subtract_fusion.4), kind=kLoop, calls=%fused_computation.9 | loop fusion | flops 4192256 | bytes 8400896 | tf_op jit(solution)/shard_map/reduce_max | solution.py:88
  80.4 4.6 %exponential_reduce_fusion.1 = f32[2048]{0:T(1024)S(1)} fusion(f32[2048,1024]{0,1:T(8,128)} %copy-done.1, f32[2048]{0:T(1024)S(1)} %add_reduce_fusion, f32[1024]{0:T(1024)S(1)} %add_subtract_fusion.4), kind=kLoop, calls=%fused_computation.4 | loop fusion | flops 8386560 | bytes 8409088 | tf_op jit(solution)/shard_map/reduce_sum | solution.py:89
  85.0 1.9 collective-permute-start.10
  87.2 0.7 collective-permute-start.9
  87.9 0.9 collective-permute-done.10
  88.8 3.4 %collective-permute-done.8 = f32[2048]{0:T(1024)S(1)} collective-permute-done((f32[2048]{0:T(1024)S(1)}, f32[2048]{0:T(1024)S(1)}, u32[]{:S(2)}, u32[]{:S(2)}) %collective-permute-start.8) | collective-permute-done | bytes 8224 | tf_op jit(solution)/shard_map/ppermute | solution.py:37
  92.2 0.6 add_reduce_fusion.4
  92.8 2.2 %exponential_reduce_fusion = f32[1024]{0:T(1024)S(1)} fusion(f32[2048,1024]{0,1:T(8,128)S(1)} %bitcast.51, f32[1024]{0:T(1024)S(1)} %add_reduce_fusion.4, f32[2048]{0:T(1024)S(1)} %add_subtract_fusion), kind=kLoop, calls=%fused_computation.3 | loop fusion | flops 8387584 | bytes 8404992 | tf_op jit(solution)/shard_map/reduce_sum | solution.py:93
  95.2 1.2 collective-permute-done.11
  96.3 0.7 broadcast_in_dim.10
  97.1 5.5 %all-to-all-start.2 = ((f32[32,1,1024]{2,1,0:T(1,128)}), f32[32,1,1024]{2,1,0:T(1,128)S(1)}, u32[]{:S(2)}, u32[]{:S(2)}) async-start(f32[32,1,1024]{2,1,0:T(1,128)} %broadcast_in_dim.10), calls=%async_computation.2 | async-start | bytes 262144 | tf_op jit(solution)/shard_map/all_to_all | solution.py:27
  102.6 9.3 %all-to-all-done.2 = f32[32,1,1024]{2,1,0:T(1,128)S(1)} async-done(((f32[32,1,1024]{2,1,0:T(1,128)}), f32[32,1,1024]{2,1,0:T(1,128)S(1)}, u32[]{:S(2)}, u32[]{:S(2)}) %all-to-all-start.2) | async-done | bytes 131104 | tf_op jit(solution)/shard_map/all_to_all | solution.py:27
  112.0 6.4 %fusion.3 = f32[1024,768]{1,0:T(8,128)S(1)} fusion(bf16[2048,768]{1,0:T(8,128)(2,1)S(1)} %copy-done, f32[2048,1024]{0,1:T(8,128)} %copy-done.1, f32[1024]{0:T(1024)S(1)} %add_subtract_fusion.3, f32[2048]{0:T(1024)S(1)} %add_subtract_fusion), kind=kOutput, calls=%fused_computation.17 | convolution fusion | flops 3229614080 | bytes 14692352 | tf_op jit(solution)/shard_map/dot_general | solution.py:96
  118.4 1.7 copy-done.3
  120.1 1.0 fusion.9
  121.1 2.6 %collective-permute-done.12 = bf16[32,16,768]{2,1,0:T(8,128)(2,1)} collective-permute-done((bf16[32,16,768]{2,1,0:T(8,128)(2,1)}, bf16[32,16,768]{2,1,0:T(8,128)(2,1)}, u32[]{:S(2)}, u32[]{:S(2)}) %collective-permute-start.12) | collective-permute-done | bytes 786464 | tf_op jit(solution)/shard_map/ppermute | solution.py:18
  123.7 1.9 fusion.8
  125.6 28.0 %all_to_all.39 = bf16[32,16,768]{2,1,0:T(8,128)(2,1)S(1)} all-to-all(bf16[32,16,768]{2,1,0:T(8,128)(2,1)S(1)} %fusion.8), channel_id=1, replica_groups={{0,8,16,24,32,40,48,56,64,72,80,88,96,104,112,120,128,136,144,152,160,1..., dimensions={0} | all-to-all | bytes 1572864 | tf_op jit(solution)/shard_map/all_to_all | solution.py:27
  153.8 27.1 %all_to_all.40 = bf16[32,16,768]{2,1,0:T(8,128)(2,1)} all-to-all(bf16[32,16,768]{2,1,0:T(8,128)(2,1)S(1)} %broadcast_in_dim.11), channel_id=1, replica_groups={{0,8,16,24,32,40,48,56,64,72,80,88,96,104,112,120,128,136,144,152,160,1..., dimensions={0} | all-to-all | bytes 1572864 | tf_op jit(solution)/shard_map/all_to_all | solution.py:27
  181.0 4.5 %fusion.1 = f32[2048]{0:T(1024)S(1)} fusion(f32[2048,1024]{0,1:T(8,128)} %copy-done.1, f32[1024]{0:T(1024)S(1)} %add_subtract_fusion.3, f32[2048]{0:T(1024)S(1)} %add_subtract_fusion), kind=kLoop, calls=%fused_computation.14 | loop fusion | flops 8386560 | bytes 8409088 | tf_op jit(solution)/shard_map/reduce_sum | solution.py:110
  185.5 1.5 select_bitcast_fusion.1
  187.3 1.4 pad_maximum_fusion
  188.8 7.2 %fusion = f32[2048]{0:T(1024)S(1)} fusion(f32[2048,1024]{0,1:T(8,128)} %copy-done.1, bf16[1024,768]{1,0:T(8,128)(2,1)} %bitcast.54, bf16[2048,768]{1,0:T(8,128)(2,1)S(1)} %copy-done, f32[1024]{0:T(1024)S(1)} %sub.215, f32[1024]{0:T(1024)S(1)} %add_subtract_fusion.3, f32[2048]{0:T(1024)S(1)} %add_subtract_fusion), kind=kOutput, calls=%fused_computation.1 | convolution fusion | flops 3235903488 | bytes 13131776 | tf_op jit(solution)/shard_map/dot_general | solution.py:106
  196.1 2.1 %collective-permute-start.14 = (f32[2,2048]{1,0:T(2,128)S(1)}, f32[2,2048]{1,0:T(2,128)S(1)}, u32[]{:S(2)}, u32[]{:S(2)}) collective-permute-start(f32[2,2048]{1,0:T(2,128)S(1)} %pad_maximum_fusion.1), channel_id=1, source_target_pairs={{0,2},{1,3},{2,0},{3,1},{4,6},{5,7},{6,4},{7,5},{8,10},{9,11},{10,... | collective-permute-start | bytes 49160 | tf_op jit(solution)/shard_map/ppermute | solution.py:37
  198.4 3.0 %collective-permute-start.16 = (f32[2,2048]{1,0:T(2,128)S(1)}, f32[2,2048]{1,0:T(2,128)S(1)}, u32[]{:S(2)}, u32[]{:S(2)}) collective-permute-start(f32[2,2048]{1,0:T(2,128)S(1)} %pad_maximum_fusion.1), channel_id=1, source_target_pairs={{0,3},{1,0},{2,1},{3,2},{4,7},{5,4},{6,5},{7,6},{8,11},{9,8},{10,9... | collective-permute-start | bytes 49160 | tf_op jit(solution)/shard_map/ppermute | solution.py:37
  201.6 1.5 collective-permute-done.15
  (58 shorter events, 4.2 us)
Async XLA Ops:
  0.6 1.9 copy-start
  7.4 10.2 %copy-start.1 = (f32[2048,1024]{0,1:T(8,128)}, f32[2048,1024]{0,1:T(8,128)S(1)}, u32[]{:S(2)}) copy-start(f32[2048,1024]{0,1:T(8,128)S(1)} %get-tuple-element.5) | copy-start | bytes 25165828
  8.8 6.5 %collective-permute-start = (f32[2048]{0:T(1024)S(1)}, f32[2048]{0:T(1024)S(1)}, u32[]{:S(2)}, u32[]{:S(2)}) collective-permute-start(f32[2048]{0:T(1024)S(1)} %multiply_add_fusion.2), channel_id=1, source_target_pairs={{0,2},{1,3},{2,0},{3,1},{4,6},{5,7},{6,4},{7,5},{8,10},{9,11},{10,... | collective-permute-start | bytes 24584 | tf_op jit(solution)/shard_map/ppermute | solution.py:37
  12.1 4.9 %collective-permute-start.1 = (f32[2048]{0:T(1024)S(1)}, f32[2048]{0:T(1024)S(1)}, u32[]{:S(2)}, u32[]{:S(2)}) collective-permute-start(f32[2048]{0:T(1024)S(1)} %multiply_add_fusion.2), channel_id=1, source_target_pairs={{0,1},{1,2},{2,3},{3,0},{4,5},{5,6},{6,7},{7,4},{8,9},{9,10},{10,1... | collective-permute-start | bytes 24584 | tf_op jit(solution)/shard_map/ppermute | solution.py:37
  12.8 4.2 %collective-permute-start.2 = (f32[2048]{0:T(1024)S(1)}, f32[2048]{0:T(1024)S(1)}, u32[]{:S(2)}, u32[]{:S(2)}) collective-permute-start(f32[2048]{0:T(1024)S(1)} %multiply_add_fusion.2), channel_id=1, source_target_pairs={{0,3},{1,0},{2,1},{3,2},{4,7},{5,4},{6,5},{7,6},{8,11},{9,8},{10,9... | collective-permute-start | bytes 24584 | tf_op jit(solution)/shard_map/ppermute | solution.py:37
  19.8 1.3 collective-permute-start.3
  41.8 5.8 %copy-start.2 = (f32[2048,1024]{0,1:T(8,128)S(1)}, f32[2048,1024]{0,1:T(8,128)}, u32[]{:S(2)}) copy-start(f32[2048,1024]{0,1:T(8,128)} %copy-done.1) | copy-start | bytes 25165828
  49.8 5.2 %collective-permute-start.4 = (f32[2048]{0:T(1024)S(1)}, f32[2048]{0:T(1024)S(1)}, u32[]{:S(2)}, u32[]{:S(2)}) collective-permute-start(f32[2048]{0:T(1024)S(1)} %multiply_add_fusion.1), channel_id=1, source_target_pairs={{0,2},{1,3},{2,0},{3,1},{4,6},{5,7},{6,4},{7,5},{8,10},{9,11},{10,... | collective-permute-start | bytes 24584 | tf_op jit(solution)/shard_map/ppermute | solution.py:37
  51.4 4.9 %collective-permute-start.5 = (f32[2048]{0:T(1024)S(1)}, f32[2048]{0:T(1024)S(1)}, u32[]{:S(2)}, u32[]{:S(2)}) collective-permute-start(f32[2048]{0:T(1024)S(1)} %multiply_add_fusion.1), channel_id=1, source_target_pairs={{0,1},{1,2},{2,3},{3,0},{4,5},{5,6},{6,7},{7,4},{8,9},{9,10},{10,1... | collective-permute-start | bytes 24584 | tf_op jit(solution)/shard_map/ppermute | solution.py:37
  54.0 3.7 %collective-permute-start.6 = (f32[2048]{0:T(1024)S(1)}, f32[2048]{0:T(1024)S(1)}, u32[]{:S(2)}, u32[]{:S(2)}) collective-permute-start(f32[2048]{0:T(1024)S(1)} %multiply_add_fusion.1), channel_id=1, source_target_pairs={{0,3},{1,0},{2,1},{3,2},{4,7},{5,4},{6,5},{7,6},{8,11},{9,8},{10,9... | collective-permute-start | bytes 24584 | tf_op jit(solution)/shard_map/ppermute | solution.py:37
  60.6 1.3 collective-permute-start.7
  76.2 16.0 %slice-start = ((s8[8388608]{0:T(1024)(128)(4,1)}), s8[4194304]{0:T(1024)(128)(4,1)S(1)}, s32[]{:S(2)}) async-start(s8[8388608]{0:T(1024)(128)(4,1)} %bitcast.50), calls=%async_computation.5 | async-start | bytes 8388608
  80.3 11.8 %slice-start.1 = ((s8[8388608]{0:T(1024)(128)(4,1)}), s8[4194304]{0:T(1024)(128)(4,1)S(1)}, s32[]{:S(2)}) async-start(s8[8388608]{0:T(1024)(128)(4,1)} %bitcast.50), calls=%async_computation.6 | async-start | bytes 8388608
  85.0 3.7 %collective-permute-start.10 = (f32[2048]{0:T(1024)S(1)}, f32[2048]{0:T(1024)S(1)}, u32[]{:S(2)}, u32[]{:S(2)}) collective-permute-start(f32[2048]{0:T(1024)S(1)} %multiply_add_fusion), channel_id=1, source_target_pairs={{0,3},{1,0},{2,1},{3,2},{4,7},{5,4},{6,5},{7,6},{8,11},{9,8},{10,9... | collective-permute-start | bytes 24584 | tf_op jit(solution)/shard_map/ppermute | solution.py:37
  86.9 5.2 %collective-permute-start.8 = (f32[2048]{0:T(1024)S(1)}, f32[2048]{0:T(1024)S(1)}, u32[]{:S(2)}, u32[]{:S(2)}) collective-permute-start(f32[2048]{0:T(1024)S(1)} %multiply_add_fusion), channel_id=1, source_target_pairs={{0,2},{1,3},{2,0},{3,1},{4,6},{5,7},{6,4},{7,5},{8,10},{9,11},{10,... | collective-permute-start | bytes 24584 | tf_op jit(solution)/shard_map/ppermute | solution.py:37
  87.2 5.0 %collective-permute-start.9 = (f32[2048]{0:T(1024)S(1)}, f32[2048]{0:T(1024)S(1)}, u32[]{:S(2)}, u32[]{:S(2)}) collective-permute-start(f32[2048]{0:T(1024)S(1)} %multiply_add_fusion), channel_id=1, source_target_pairs={{0,1},{1,2},{2,3},{3,0},{4,5},{5,6},{6,7},{7,4},{8,9},{9,10},{10,1... | collective-permute-start | bytes 24584 | tf_op jit(solution)/shard_map/ppermute | solution.py:37
  95.1 1.3 collective-permute-start.11
  97.1 14.8 %all-to-all-start.2 = ((f32[32,1,1024]{2,1,0:T(1,128)}), f32[32,1,1024]{2,1,0:T(1,128)S(1)}, u32[]{:S(2)}, u32[]{:S(2)}) async-start(f32[32,1,1024]{2,1,0:T(1,128)} %broadcast_in_dim.10), calls=%async_computation.2 | async-start | bytes 262144 | tf_op jit(solution)/shard_map/all_to_all | solution.py:27
  118.4 1.8 copy-start.3
  121.1 2.6 %collective-permute-start.12 = (bf16[32,16,768]{2,1,0:T(8,128)(2,1)}, bf16[32,16,768]{2,1,0:T(8,128)(2,1)}, u32[]{:S(2)}, u32[]{:S(2)}) collective-permute-start(bf16[32,16,768]{2,1,0:T(8,128)(2,1)} %fusion.9), channel_id=1, source_target_pairs={{0,4},{4,0},{8,12},{12,8},{16,20},{20,16},{24,28},{28,24},{32,36},... | collective-permute-start | bytes 2359304 | tf_op jit(solution)/shard_map/ppermute | solution.py:18
  153.7 35.0 %copy-start.4 = (bf16[16,768]{1,0:T(8,128)(2,1)}, bf16[16,768]{1,0:T(8,128)(2,1)S(1)}, u32[]{:S(2)}) copy-start(bf16[16,768]{1,0:T(8,128)(2,1)S(1)} %multiply_convert_fusion) | copy-start | bytes 73732
  181.0 4.5 %collective-permute-start.13 = (bf16[32,16,768]{2,1,0:T(8,128)(2,1)}, bf16[32,16,768]{2,1,0:T(8,128)(2,1)}, u32[]{:S(2)}, u32[]{:S(2)}) collective-permute-start(bf16[32,16,768]{2,1,0:T(8,128)(2,1)} %all_to_all.40), channel_id=1, source_target_pairs={{0,4},{4,0},{8,12},{12,8},{16,20},{20,16},{24,28},{28,24},{32,36},... | collective-permute-start | bytes 2359304 | tf_op jit(solution)/shard_map/ppermute | solution.py:18
  196.1 5.5 %collective-permute-start.14 = (f32[2,2048]{1,0:T(2,128)S(1)}, f32[2,2048]{1,0:T(2,128)S(1)}, u32[]{:S(2)}, u32[]{:S(2)}) collective-permute-start(f32[2,2048]{1,0:T(2,128)S(1)} %pad_maximum_fusion.1), channel_id=1, source_target_pairs={{0,2},{1,3},{2,0},{3,1},{4,6},{5,7},{6,4},{7,5},{8,10},{9,11},{10,... | collective-permute-start | bytes 49160 | tf_op jit(solution)/shard_map/ppermute | solution.py:37
  198.2 4.9 %collective-permute-start.15 = (f32[2,2048]{1,0:T(2,128)S(1)}, f32[2,2048]{1,0:T(2,128)S(1)}, u32[]{:S(2)}, u32[]{:S(2)}) collective-permute-start(f32[2,2048]{1,0:T(2,128)S(1)} %pad_maximum_fusion.1), channel_id=1, source_target_pairs={{0,1},{1,2},{2,3},{3,0},{4,5},{5,6},{6,7},{7,4},{8,9},{9,10},{10,1... | collective-permute-start | bytes 49160 | tf_op jit(solution)/shard_map/ppermute | solution.py:37
  198.4 4.8 %collective-permute-start.16 = (f32[2,2048]{1,0:T(2,128)S(1)}, f32[2,2048]{1,0:T(2,128)S(1)}, u32[]{:S(2)}, u32[]{:S(2)}) collective-permute-start(f32[2,2048]{1,0:T(2,128)S(1)} %pad_maximum_fusion.1), channel_id=1, source_target_pairs={{0,3},{1,0},{2,1},{3,2},{4,7},{5,4},{6,5},{7,6},{8,11},{9,8},{10,9... | collective-permute-start | bytes 49160 | tf_op jit(solution)/shard_map/ppermute | solution.py:37

commit v2 on v1

v2 whole, which is shorter than its diff:
```python
import math

import jax
import jax.numpy as jnp
from jax import lax
from jax.experimental import pallas as pl
from jax.experimental.pallas import tpu as pltpu
from jax.sharding import PartitionSpec as P

ITERS = 3


sharpness = 4.0
LOG2E = math.log2(math.e)
C = 2
LANES = 128
SUB = 8
GROUP = 128
F32 = jnp.float32
BF16 = jnp.bfloat16


def other_core(value):
    size = lax.axis_size("pts")
    return lax.ppermute(value, "pts", [(i, i ^ 1) for i in range(size)])


def chip_groups():
    size = lax.axis_size("pts")
    return [[chip * C + core for chip in range(size // C)] for core in range(C)]


def exchange(value):
    return lax.all_to_all(value, "pts", 0, 0, axis_index_groups=chip_groups())


def from_chips(value):
    chips = lax.axis_size("pts") // C
    return exchange(jnp.broadcast_to(value[None], (chips,) + value.shape))


def cen_shift(value, step):
    size = lax.axis_size("cen")
    return lax.ppermute(value, "cen", [(i, (i + step) % size) for i in range(size)])


def spread_cols(value):
    theirs = jnp.roll(other_core(value), value.shape[1] // 2, axis=1)
    top = jnp.maximum(value, theirs)
    value = top + jnp.log2(jnp.exp2(value - top) + jnp.exp2(theirs - top))
    return from_chips(value)


def on_lanes(row):
    return jnp.broadcast_to(row, (LANES, row.shape[1])).T


def lane_sums(values):
    top = values[0]
    for value in values[1:]:
        top = jnp.maximum(top, value)
    total = jnp.exp2(values[0] - top)
    for value in values[1:]:
        total = total + jnp.exp2(value - top)
    return top, total


def close(top, total):
    highest = jnp.max(top, axis=0, keepdims=True)
    return highest + jnp.log2(jnp.sum(total * jnp.exp2(top - highest), axis=0, keepdims=True))


def group_pairs(scores_ref, group, cols, top_ref, total_ref):
    first = group * GROUP
    at = [slice(first + SUB * j, first + SUB * (j + 1)) for j in range(GROUP // SUB)]
    out = slice(group * SUB, (group + 1) * SUB)

    def step(block, carry):
        here = pl.ds(pl.multiple_of(block * LANES, LANES), LANES)
        values = [scores_ref[a, here] for a in at]
        if cols is not None:
            values = [v + c for v, c in zip(values, cols)]
        top, total = lane_sums(values)
        top_ref[out, here] = top
        total_ref[out, here] = total
        return carry

    lax.fori_loop(0, scores_ref.shape[1] // LANES, step, 0, unroll=2)


def score_kernel(
    core_ref, points_ref, centroids_ref, scores_ref, row_ref, split_ref, top_ref, total_ref, *, each
):
    count = points_ref.shape[0]
    rows = centroids_ref.shape[0]
    core = core_ref[0]
    blocks = rows // each // C

    def order(j, carry):
        for part in range(C):
            side = core if part == 0 else 1 - core
            start = pl.multiple_of((j * C + side) * each, each)
            here = pl.multiple_of((part * blocks + j) * each, each)
            split_ref[pl.ds(here, each), :] = centroids_ref[pl.ds(start, each), :]
        return carry

    lax.fori_loop(0, blocks, order, 0)
    chunk = 256
    for first in range(0, count, chunk):
        here = slice(first, first + chunk)
        product = lax.dot_general(
            split_ref[...],
            points_ref[here, :],
            (((1,), (1,)), ((), ())),
            preferred_element_type=F32,
        )
        scores_ref[:, here] = (sharpness * LOG2E) * product
    for group in range(rows // GROUP):
        group_pairs(scores_ref, group, None, top_ref, total_ref)
    row_ref[...] = close(top_ref[...], total_ref[...])


def col_potential(values_ref, level):
    values = values_ref[:, 0, :]
    highest = jnp.max(values, axis=0, keepdims=True)
    total = jnp.sum(jnp.exp2(values - highest), axis=0, keepdims=True)
    return level - (highest + jnp.log2(total))


def row_kernel(scores_ref, values_ref, row_ref, cols_ref, top_ref, total_ref, *, level):
    cols_ref[...] = on_lanes(col_potential(values_ref, level))
    for group in range(scores_ref.shape[0] // GROUP):
        cols = [
            cols_ref[pl.ds(group * GROUP + SUB * j, SUB), :] for j in range(GROUP // SUB)
        ]
        group_pairs(scores_ref, group, cols, top_ref, total_ref)
    row_ref[...] = close(top_ref[...], total_ref[...])


def col_kernel(
    scores_ref, own_ref, one_ref, two_ref, three_ref, col_ref, row_ref, top_ref, total_ref, *, level
):
    own, one, two, three = own_ref[...], one_ref[...], two_ref[...], three_ref[...]
    highest = jnp.maximum(jnp.maximum(own, two), jnp.maximum(one, three))
    even = jnp.exp2(own - highest) + jnp.exp2(two - highest)
    odd = jnp.exp2(one - highest) + jnp.exp2(three - highest)
    row_ref[...] = level - (highest + jnp.log2(even + odd))

    rows, count = scores_ref.shape
    at = [slice(LANES * j, LANES * (j + 1)) for j in range(count // LANES)]
    points = [jnp.broadcast_to(row_ref[:, a], (SUB, LANES)) for a in at]

    def step(block, carry):
        here = pl.ds(pl.multiple_of(block * SUB, SUB), SUB)
        top, total = lane_sums([scores_ref[here, a] + p for a, p in zip(at, points)])
        top_ref[here, :] = top
        total_ref[here, :] = total
        return carry

    lax.fori_loop(0, rows // SUB, step, 0, unroll=2)
    col_ref[...] = close(top_ref[...].T, total_ref[...].T)


def plan_of(scores_ref, first, row_ref, cols_ref):
    here = slice(first, first + GROUP)
    shift = jnp.concatenate([cols_ref[here, :]] * (scores_ref.shape[1] // LANES), axis=1)
    return jnp.exp2((scores_ref[here, :] + row_ref[...]) + shift)


def sums_of(scores_ref, row_ref, cols_ref, points_ref, sums_ref, half):
    rows = sums_ref.shape[0]
    for first in range(0, rows, GROUP):
        plan = plan_of(scores_ref, half * rows + first, row_ref, cols_ref)
        sums_ref[first : first + GROUP, :] = lax.dot_general(
            plan.astype(BF16),
            points_ref[...],
            (((1,), (0,)), ((), ())),
            preferred_element_type=F32,
        ).astype(sums_ref.dtype)


def give_kernel(scores_ref, row_ref, values_ref, points_ref, sums_ref, cols_ref, *, level):
    cols_ref[...] = on_lanes(col_potential(values_ref, level))
    sums_of(scores_ref, row_ref, cols_ref, points_ref, sums_ref, 1)


def keep_kernel(scores_ref, row_ref, cols_ref, points_ref, sums_ref):
    sums_of(scores_ref, row_ref, cols_ref, points_ref, sums_ref, 0)


def distance_kernel(scores_ref, row_ref, cols_ref, points_ref, fresh_ref, both_ref, *, half):
    rows = fresh_ref.shape[0]
    count = points_ref.shape[0]
    numerator = jnp.zeros((SUB, count), F32)
    mass = jnp.zeros((SUB, count), F32)
    for first in range(0, rows, GROUP):
        fresh = fresh_ref[first : first + GROUP, :]
        wide = fresh.astype(F32)
        squares = jnp.sum(wide * wide, axis=1, keepdims=True)
        cross = lax.dot_general(
            fresh, points_ref[...], (((1,), (1,)), ((), ())), preferred_element_type=F32
        )
        plan = plan_of(scores_ref, half * rows + first, row_ref, cols_ref)
        term = plan * (squares - 2.0 * cross)
        numerator = numerator + jnp.sum(term.reshape(GROUP // SUB, SUB, count), axis=0)
        mass = mass + jnp.sum(plan.reshape(GROUP // SUB, SUB, count), axis=0)
    both_ref[0:1, :] = jnp.sum(numerator, axis=0, keepdims=True)
    both_ref[1:2, :] = jnp.sum(mass, axis=0, keepdims=True)


VMEM = pl.BlockSpec(memory_space=pltpu.VMEM)
SCALAR = pl.BlockSpec(memory_space=pltpu.SMEM)


def call(kernel, outs, scratch, args, name, limit=24):
    return pl.pallas_call(
        kernel,
        out_shape=[jax.ShapeDtypeStruct(shape, dtype) for shape, dtype in outs],
        in_specs=[SCALAR if arg.dtype == jnp.int32 else VMEM for arg in args],
        out_specs=[VMEM] * len(outs),
        scratch_shapes=[pltpu.VMEM(shape, dtype) for shape, dtype in scratch],
        compiler_params=pltpu.CompilerParams(vmem_limit_bytes=limit << 20),
        name=name,
    )(*args)


def on_device(points, centroids):
    chips = lax.axis_size("pts") // C
    core = lax.axis_index("pts") % C
    count, width = points.shape
    rows = centroids.shape[0]
    half = rows // C
    each = rows // (chips * C)
    total_centroids = rows * lax.axis_size("cen")
    row_level = -math.log2(count * chips * C)
    col_level = -math.log2(total_centroids)

    pairs = [((rows // GROUP * SUB, count), F32)] * 2
    strip = ((rows, LANES), F32)
    line = ((1, count), F32)
    sums = (half, width)

    scores, part = call(
        lambda *refs: score_kernel(*refs, each=each),
        [((rows, count), F32), line],
        [((rows, width), BF16)] + pairs,
        [core.astype(jnp.int32).reshape(1), points, centroids],
        "scores",
    )
    for iteration in range(ITERS):
        if iteration:
            (part,) = call(
                lambda *refs: row_kernel(*refs, level=col_level),
                [line],
                [strip] + pairs,
                [scores, values],
                "rows",
            )
        others = [cen_shift(part, step) for step in (1, 2, 3)]
        col, row = call(
            lambda *refs: col_kernel(*refs, level=row_level),
            [((1, rows), F32), line],
            [strip] * 2,
            [scores, part] + others,
            "cols",
        )
        values = spread_cols(col)

    give, cols = call(
        lambda *refs: give_kernel(*refs, level=col_level),
        [(sums, BF16), strip],
        [],
        [scores, row, values, points],
        "give",
    )
    theirs = other_core(give)
    (keep,) = call(keep_kernel, [(sums, F32)], [], [scores, row, cols, points], "keep")
    pieces = exchange((keep + theirs.astype(F32)).astype(BF16).reshape(chips, each, width))
    own_rows = (total_centroids * jnp.sum(pieces.astype(F32), axis=0)).astype(BF16)
    mine = from_chips(own_rows).reshape(half, width)
    other = other_core(mine)
    terms = [
        call(
            lambda *refs: distance_kernel(*refs, half=part),
            [((2, count), F32)],
            [],
            [scores, row, cols, points, fresh],
            "terms",
        )[0]
        for part, fresh in enumerate((mine, other))
    ]
    both = terms[0] + terms[1]
    one, two, three = [cen_shift(both, step) for step in (1, 2, 3)]
    total = (both + two) + (one + three)
    distances = total[0] / total[1] / width
    return (own_rows, distances)


def solution(mesh):
    in_specs = (P("pts", None), P("cen", None))
    out_specs = (P(("cen", "pts"), None), P("pts"))
    return jax.shard_map(
        on_device, mesh=mesh, in_specs=in_specs, out_specs=out_specs, check_vma=False
    )
```

time: 204 us -> 181 us (0.89)
  Pallas kernels: 0 us -> 37.5 us
  other arithmetic: 36.2 us -> 1.09 us
  matrix products: 18.5 us -> 0 us
  blocking collectives: 89.7 us -> 104 us
  starting transfers between devices: 25.2 us -> 14.5 us
  waiting for transfers between devices: 26 us -> 19.8 us
  local copies, waits for them, and re-layouts: 7.22 us -> 3.56 us
    pallas_call x0 -> x10, Pallas kernels: none -> 37.5 us  [call(): pl.pallas_call(kernel, out_shape=[jax.ShapeDtypeStruct(shape, dtype) for...]
    reduce_sum x12 -> x1, other arithmetic: 20.1 us -> 0.12 us  [on_device(): jnp.sum(pieces.astype(F32), axis=0)]
    dot_general x3 -> x0, matrix products: 18.5 us -> none  [the longest x1 7.25 us: on_device(): lax.dot_general(points, gathered, (((1,), (1,)), ((), ())), preferred_ele...]
    all_to_all x4 -> x5, blocking collectives: 89.7 us -> 104 us  [exchange(): return lax.all_to_all(value, 'pts', 0, 0, axis_index_groups=chip_groups())]
    reduce_max x8 -> x0, other arithmetic: 10.5 us -> none  [the longest x2 8.31 us: on_device(): highest = jnp.max(shifted, axis=1)]
    all_to_all x1 -> x0, waiting for transfers between devices: 9.25 us -> none  [exchange(): return lax.all_to_all(value, 'pts', 0, 0, axis_index_groups=chip_groups())]
    all_to_all x1 -> x0, starting transfers between devices: 5.48 us -> none  [exchange(): return lax.all_to_all(value, 'pts', 0, 0, axis_index_groups=chip_groups())]
    ppermute x12, waiting for transfers between devices: 10.6 us -> 16.1 us  [cen_shift(): lax.ppermute(value, 'cen', [(i, (i + step) % size) for i in range(size)])]
  transfers between devices with their start and end apart: 18 -> 17, of which waited for: 13 -> 15; matrix products, arithmetic and copies ran while one was open for 2% -> 0% of each run, Pallas kernels for 0% -> 4%
where the time goes in v2:
time: 181 us
  blocking collectives  104 us (57%)
  Pallas kernels  37.5 us (21%)
  waiting for transfers between devices  19.8 us (11%)
  starting transfers between devices  14.5 us (8%)
  local copies, waits for them, and re-layouts  3.56 us (2%)
    all_to_all x5, blocking collectives, exchange(): return lax.all_to_all(value, 'pts', 0, 0, axis_index_groups=chip_groups())  104 us
    pallas_call x10, Pallas kernels, call(): pl.pallas_call(kernel, out_shape=[jax.ShapeDtypeStruct(shape, dtype) for...  37.5 us
    ppermute x12, waiting for transfers between devices, cen_shift(): lax.ppermute(value, 'cen', [(i, (i + step) % size) for i in range(size)])  16.1 us
    ppermute x12, starting transfers between devices, cen_shift(): lax.ppermute(value, 'cen', [(i, (i + step) % size) for i in range(size)])  14.3 us
    ppermute x5, waiting for transfers between devices, other_core(): return lax.ppermute(value, 'pts', [(i, i ^ 1) for i in range(size)])  3.76 us
  transfers between devices with their start and end apart: 17, of which 15 were waited for; matrix products, arithmetic and copies ran while one was open for 0% of the time, Pallas kernels for 4%

profile of v2, /device:TPU:2, one launch (start us, length us, event | category | flops | bytes accessed | tf_op | source)
XLA Modules:
  0.0 180.9 jit_solution(4048160418064668334)
XLA Ops:
  0.7 1.9 %copy-done = bf16[2048,768]{1,0:T(8,128)(2,1)S(1)} copy-done((bf16[2048,768]{1,0:T(8,128)(2,1)S(1)}, bf16[2048,768]{1,0:T(8,128)(2,1)}, u32[]{:S(2)}) %copy-start) | copy-done | bytes 3145752
  2.5 1.4 copy-done.1
  3.9 7.0 %scores.1 = (f32[1024,2048]{1,0:T(8,128)S(1)}, f32[1,2048]{1,0:T(1,128)S(1)}) custom-call(s32[1]{0:T(128)} %bitcast.refs_0_, bf16[2048,768]{1,0:T(8,128)(2,1)S(1)} %copy-done, bf16[1024,768]{1,0:T(8,128)(2,1)S(1)} %copy-done.1), custom_call_target="tpu_custom_call" | custom-call | tf_op jit(solution)/shard_map/scores/pallas_call | solution.py:216
  10.9 3.1 %collective-permute-start.2 = (f32[1,2048]{1,0:T(1,128)S(1)}, f32[1,2048]{1,0:T(1,128)S(1)}, u32[]{:S(2)}, u32[]{:S(2)}) collective-permute-start(f32[1,2048]{1,0:T(1,128)S(1)} %get-tuple-element.11.refs_1_), channel_id=1, source_target_pairs={{0,3},{1,0},{2,1},{3,2},{4,7},{5,4},{6,5},{7,6},{8,11},{9,8},{10,9... | collective-permute-start | bytes 24584 | tf_op jit(solution)/shard_map/ppermute | solution.py:44
  14.0 0.6 collective-permute-start.1
  14.6 1.0 collective-permute-start
  15.6 3.6 %collective-permute-done.1.refs_3_ = f32[1,2048]{1,0:T(1,128)S(1)} collective-permute-done((f32[1,2048]{1,0:T(1,128)S(1)}, f32[1,2048]{1,0:T(1,128)S(1)}, u32[]{:S(2)}, u32[]{:S(2)}) %collective-permute-start.1) | collective-permute-done | bytes 8224 | tf_op jit(solution)/shard_map/ppermute | solution.py:44
  19.2 0.3 collective-permute-done.refs_2_
  19.5 3.6 %cols.3 = (f32[1,1024]{1,0:T(1,128)S(1)}, f32[1,2048]{1,0:T(1,128)}) custom-call(f32[1024,2048]{1,0:T(8,128)S(1)} %get-tuple-element.10.refs_0_.scores_ref, f32[1,2048]{1,0:T(1,128)S(1)} %get-tuple-element.11.refs_1_, f32[1,2048]{1,0:T(1,128)S(1)} %collective-permute-done.refs_2_, f32[1,2048]{1,0:T(1,128)S(1)} %collective-permute-done.1.refs_3_, ...), custom_call_target="tpu_custom_call" | custom-call | tf_op jit(solution)/shard_map/cols/pallas_call | solution.py:216
  23.1 1.2 collective-permute-done.3
  24.4 20.5 %all_to_all.25.refs_1_ = f32[32,1,1024]{2,1,0:T(1,128)S(1)} all-to-all(f32[32,1,1024]{2,1,0:T(1,128)S(1)} %broadcast_in_dim.15), channel_id=1, replica_groups={{0,8,16,24,32,40,48,56,64,72,80,88,96,104,112,120,128,136,144,152,160,1..., dimensions={0} | all-to-all | bytes 262144 | tf_op jit(solution)/shard_map/all_to_all | solution.py:34
  44.9 3.5 %rows.2.refs_1_ = f32[1,2048]{1,0:T(1,128)S(1)} custom-call(f32[1024,2048]{1,0:T(8,128)S(1)} %get-tuple-element.10.refs_0_.scores_ref, f32[32,1,1024]{2,1,0:T(1,128)S(1)} %all_to_all.25.refs_1_), custom_call_target="tpu_custom_call" | custom-call | tf_op jit(solution)/shard_map/rows/pallas_call | solution.py:216
  48.4 0.5 collective-permute-start.6
  48.9 1.4 collective-permute-start.5
  50.3 1.3 collective-permute-start.4
  51.6 0.5 collective-permute-done.6.refs_4_
  52.1 1.9 %collective-permute-done.5.refs_3_ = f32[1,2048]{1,0:T(1,128)S(1)} collective-permute-done((f32[1,2048]{1,0:T(1,128)S(1)}, f32[1,2048]{1,0:T(1,128)S(1)}, u32[]{:S(2)}, u32[]{:S(2)}) %collective-permute-start.5) | collective-permute-done | bytes 8224 | tf_op jit(solution)/shard_map/ppermute | solution.py:44
  54.0 1.1 collective-permute-done.4.refs_2_
  55.2 3.6 %cols.4 = (f32[1,1024]{1,0:T(1,128)S(1)}, f32[1,2048]{1,0:T(1,128)}) custom-call(f32[1024,2048]{1,0:T(8,128)S(1)} %get-tuple-element.10.refs_0_.scores_ref, f32[1,2048]{1,0:T(1,128)S(1)} %rows.2.refs_1_, f32[1,2048]{1,0:T(1,128)S(1)} %collective-permute-done.4.refs_2_, f32[1,2048]{1,0:T(1,128)S(1)} %collective-permute-done.5.refs_3_, ...), custom_call_target="tpu_custom_call" | custom-call | tf_op jit(solution)/shard_map/cols/pallas_call | solution.py:216
  58.8 1.2 collective-permute-done.7
  60.1 14.1 %all_to_all.26.refs_1_ = f32[32,1,1024]{2,1,0:T(1,128)S(1)} all-to-all(f32[32,1,1024]{2,1,0:T(1,128)S(1)} %broadcast_in_dim.33), channel_id=1, replica_groups={{0,8,16,24,32,40,48,56,64,72,80,88,96,104,112,120,128,136,144,152,160,1..., dimensions={0} | all-to-all | bytes 262144 | tf_op jit(solution)/shard_map/all_to_all | solution.py:34
  74.2 3.5 %rows.3.refs_1_ = f32[1,2048]{1,0:T(1,128)S(1)} custom-call(f32[1024,2048]{1,0:T(8,128)S(1)} %get-tuple-element.10.refs_0_.scores_ref, f32[32,1,1024]{2,1,0:T(1,128)S(1)} %all_to_all.26.refs_1_), custom_call_target="tpu_custom_call" | custom-call | tf_op jit(solution)/shard_map/rows/pallas_call | solution.py:216
  77.6 1.9 %collective-permute-start.10 = (f32[1,2048]{1,0:T(1,128)S(1)}, f32[1,2048]{1,0:T(1,128)S(1)}, u32[]{:S(2)}, u32[]{:S(2)}) collective-permute-start(f32[1,2048]{1,0:T(1,128)S(1)} %rows.3.refs_1_), channel_id=1, source_target_pairs={{0,3},{1,0},{2,1},{3,2},{4,7},{5,4},{6,5},{7,6},{8,11},{9,8},{10,9... | collective-permute-start | bytes 24584 | tf_op jit(solution)/shard_map/ppermute | solution.py:44
  79.6 0.9 collective-permute-start.9
  80.5 1.0 collective-permute-done.10.refs_4_
  81.5 3.2 %collective-permute-done.9.refs_3_ = f32[1,2048]{1,0:T(1,128)S(1)} collective-permute-done((f32[1,2048]{1,0:T(1,128)S(1)}, f32[1,2048]{1,0:T(1,128)S(1)}, u32[]{:S(2)}, u32[]{:S(2)}) %collective-permute-start.9) | collective-permute-done | bytes 8224 | tf_op jit(solution)/shard_map/ppermute | solution.py:44
  84.7 0.6 collective-permute-done.8.refs_2_
  85.3 3.4 %cols.5 = (f32[1,1024]{1,0:T(1,128)S(1)}, f32[1,2048]{1,0:T(1,128)S(1)}) custom-call(f32[1024,2048]{1,0:T(8,128)S(1)} %get-tuple-element.10.refs_0_.scores_ref, f32[1,2048]{1,0:T(1,128)S(1)} %rows.3.refs_1_, f32[1,2048]{1,0:T(1,128)S(1)} %collective-permute-done.8.refs_2_, f32[1,2048]{1,0:T(1,128)S(1)} %collective-permute-done.9.refs_3_, ...), custom_call_target="tpu_custom_call" | custom-call | tf_op jit(solution)/shard_map/cols/pallas_call | solution.py:216
  88.7 0.1 collective-permute-start.11
  88.8 1.2 collective-permute-done.11
  90.1 14.1 %all_to_all.27.refs_2_ = f32[32,1,1024]{2,1,0:T(1,128)S(1)} all-to-all(f32[32,1,1024]{2,1,0:T(1,128)S(1)} %broadcast_in_dim.35), channel_id=1, replica_groups={{0,8,16,24,32,40,48,56,64,72,80,88,96,104,112,120,128,136,144,152,160,1..., dimensions={0} | all-to-all | bytes 262144 | tf_op jit(solution)/shard_map/all_to_all | solution.py:34
  104.2 2.1 %give.1 = (bf16[512,768]{1,0:T(8,128)(2,1)S(1)}, f32[1024,128]{1,0:T(8,128)S(1)}) custom-call(f32[1024,2048]{1,0:T(8,128)S(1)} %get-tuple-element.10.refs_0_.scores_ref, f32[1,2048]{1,0:T(1,128)S(1)} %get-tuple-element.14.refs_1_.row_ref, f32[32,1,1024]{2,1,0:T(1,128)S(1)} %all_to_all.27.refs_2_, bf16[2048,768]{1,0:T(8,128)(2,1)S(1)} %copy-done), custom_call_target="tpu_custom_call" | custom-call | tf_op jit(solution)/shard_map/give/pallas_call | solution.py:216
  106.3 0.1 collective-permute-start.12
  106.4 2.0 %keep.1 = f32[512,768]{1,0:T(8,128)S(1)} custom-call(f32[1024,2048]{1,0:T(8,128)S(1)} %get-tuple-element.10.refs_0_.scores_ref, f32[1,2048]{1,0:T(1,128)S(1)} %get-tuple-element.14.refs_1_.row_ref, f32[1024,128]{1,0:T(8,128)S(1)} %get-tuple-element.16.cols_ref.refs_2_, bf16[2048,768]{1,0:T(8,128)(2,1)S(1)} %copy-done), custom_call_target="tpu_custom_call" | custom-call | tf_op jit(solution)/shard_map/keep/pallas_call | solution.py:216
  108.4 0.3 collective-permute-done.12
  108.6 0.2 add_convert_fusion
  108.9 27.9 %all_to_all.28 = bf16[32,16,768]{2,1,0:T(8,128)(2,1)S(1)} all-to-all(bf16[32,16,768]{2,1,0:T(8,128)(2,1)S(1)} %bitcast.9), channel_id=1, replica_groups={{0,8,16,24,32,40,48,56,64,72,80,88,96,104,112,120,128,136,144,152,160,1..., dimensions={0} | all-to-all | bytes 1572864 | tf_op jit(solution)/shard_map/all_to_all | solution.py:34
  136.7 0.1 convert_reduce_fusion
  136.9 27.0 %all_to_all.29 = bf16[32,16,768]{2,1,0:T(8,128)(2,1)S(1)} all-to-all(bf16[32,16,768]{2,1,0:T(8,128)(2,1)S(1)} %broadcast_in_dim.36), channel_id=1, replica_groups={{0,8,16,24,32,40,48,56,64,72,80,88,96,104,112,120,128,136,144,152,160,1..., dimensions={0} | all-to-all | bytes 1572864 | tf_op jit(solution)/shard_map/all_to_all | solution.py:34
  163.9 4.5 %terms.2 = f32[2,2048]{1,0:T(2,128)S(1)} custom-call(f32[1024,2048]{1,0:T(8,128)S(1)} %get-tuple-element.10.refs_0_.scores_ref, f32[1,2048]{1,0:T(1,128)S(1)} %get-tuple-element.14.refs_1_.row_ref, f32[1024,128]{1,0:T(8,128)S(1)} %get-tuple-element.16.cols_ref.refs_2_, bf16[2048,768]{1,0:T(8,128)(2,1)S(1)} %copy-done, bf16[512,768]{1,0:T(8,128)(2,1)S(1)} %bitcast.8), custom_call_target="tpu_custom_call" | custom-call | tf_op jit(solution)/shard_map/terms/pallas_call | solution.py:216
  168.4 4.5 %terms.3 = f32[2,2048]{1,0:T(2,128)S(1)} custom-call(f32[1024,2048]{1,0:T(8,128)S(1)} %get-tuple-element.10.refs_0_.scores_ref, f32[1,2048]{1,0:T(1,128)S(1)} %get-tuple-element.14.refs_1_.row_ref, f32[1024,128]{1,0:T(8,128)S(1)} %get-tuple-element.16.cols_ref.refs_2_, bf16[2048,768]{1,0:T(8,128)(2,1)S(1)} %copy-done, ...), custom_call_target="tpu_custom_call" | custom-call | tf_op jit(solution)/shard_map/terms/pallas_call | solution.py:216
  172.9 1.0 collective-permute-start.16
  173.9 1.1 collective-permute-start.15
  175.0 1.4 collective-permute-start.14
  176.4 0.3 collective-permute-done.16
  176.7 2.1 %collective-permute-done.15 = f32[2,2048]{1,0:T(2,128)S(1)} collective-permute-done((f32[2,2048]{1,0:T(2,128)S(1)}, f32[2,2048]{1,0:T(2,128)S(1)}, u32[]{:S(2)}, u32[]{:S(2)}) %collective-permute-start.15) | collective-permute-done | bytes 16416 | tf_op jit(solution)/shard_map/ppermute | solution.py:44
  178.9 1.4 collective-permute-done.14
  180.3 0.6 fusion
  (23 shorter events, 0.5 us)
Async XLA Ops:
  0.6 1.9 %copy-start = (bf16[2048,768]{1,0:T(8,128)(2,1)S(1)}, bf16[2048,768]{1,0:T(8,128)(2,1)}, u32[]{:S(2)}) copy-start(bf16[2048,768]{1,0:T(8,128)(2,1)} %refs_3_.5) | copy-start | bytes 9437188
  2.5 1.4 copy-start.1
  10.9 4.7 %collective-permute-start.2 = (f32[1,2048]{1,0:T(1,128)S(1)}, f32[1,2048]{1,0:T(1,128)S(1)}, u32[]{:S(2)}, u32[]{:S(2)}) collective-permute-start(f32[1,2048]{1,0:T(1,128)S(1)} %get-tuple-element.11.refs_1_), channel_id=1, source_target_pairs={{0,3},{1,0},{2,1},{3,2},{4,7},{5,4},{6,5},{7,6},{8,11},{9,8},{10,9... | collective-permute-start | bytes 24584 | tf_op jit(solution)/shard_map/ppermute | solution.py:44
  14.0 5.2 %collective-permute-start.1 = (f32[1,2048]{1,0:T(1,128)S(1)}, f32[1,2048]{1,0:T(1,128)S(1)}, u32[]{:S(2)}, u32[]{:S(2)}) collective-permute-start(f32[1,2048]{1,0:T(1,128)S(1)} %get-tuple-element.11.refs_1_), channel_id=1, source_target_pairs={{0,2},{1,3},{2,0},{3,1},{4,6},{5,7},{6,4},{7,5},{8,10},{9,11},{10,... | collective-permute-start | bytes 24584 | tf_op jit(solution)/shard_map/ppermute | solution.py:44
  14.6 4.9 %collective-permute-start = (f32[1,2048]{1,0:T(1,128)S(1)}, f32[1,2048]{1,0:T(1,128)S(1)}, u32[]{:S(2)}, u32[]{:S(2)}) collective-permute-start(f32[1,2048]{1,0:T(1,128)S(1)} %get-tuple-element.11.refs_1_), channel_id=1, source_target_pairs={{0,1},{1,2},{2,3},{3,0},{4,5},{5,6},{6,7},{7,4},{8,9},{9,10},{10,1... | collective-permute-start | bytes 24584 | tf_op jit(solution)/shard_map/ppermute | solution.py:44
  23.1 1.2 collective-permute-start.3
  48.4 3.7 %collective-permute-start.6 = (f32[1,2048]{1,0:T(1,128)S(1)}, f32[1,2048]{1,0:T(1,128)S(1)}, u32[]{:S(2)}, u32[]{:S(2)}) collective-permute-start(f32[1,2048]{1,0:T(1,128)S(1)} %rows.2.refs_1_), channel_id=1, source_target_pairs={{0,3},{1,0},{2,1},{3,2},{4,7},{5,4},{6,5},{7,6},{8,11},{9,8},{10,9... | collective-permute-start | bytes 24584 | tf_op jit(solution)/shard_map/ppermute | solution.py:44
  48.9 5.2 %collective-permute-start.5 = (f32[1,2048]{1,0:T(1,128)S(1)}, f32[1,2048]{1,0:T(1,128)S(1)}, u32[]{:S(2)}, u32[]{:S(2)}) collective-permute-start(f32[1,2048]{1,0:T(1,128)S(1)} %rows.2.refs_1_), channel_id=1, source_target_pairs={{0,2},{1,3},{2,0},{3,1},{4,6},{5,7},{6,4},{7,5},{8,10},{9,11},{10,... | collective-permute-start | bytes 24584 | tf_op jit(solution)/shard_map/ppermute | solution.py:44
  50.3 4.9 %collective-permute-start.4 = (f32[1,2048]{1,0:T(1,128)S(1)}, f32[1,2048]{1,0:T(1,128)S(1)}, u32[]{:S(2)}, u32[]{:S(2)}) collective-permute-start(f32[1,2048]{1,0:T(1,128)S(1)} %rows.2.refs_1_), channel_id=1, source_target_pairs={{0,1},{1,2},{2,3},{3,0},{4,5},{5,6},{6,7},{7,4},{8,9},{9,10},{10,1... | collective-permute-start | bytes 24584 | tf_op jit(solution)/shard_map/ppermute | solution.py:44
  58.8 1.2 collective-permute-start.7
  77.6 3.9 %collective-permute-start.10 = (f32[1,2048]{1,0:T(1,128)S(1)}, f32[1,2048]{1,0:T(1,128)S(1)}, u32[]{:S(2)}, u32[]{:S(2)}) collective-permute-start(f32[1,2048]{1,0:T(1,128)S(1)} %rows.3.refs_1_), channel_id=1, source_target_pairs={{0,3},{1,0},{2,1},{3,2},{4,7},{5,4},{6,5},{7,6},{8,11},{9,8},{10,9... | collective-permute-start | bytes 24584 | tf_op jit(solution)/shard_map/ppermute | solution.py:44
  79.6 5.2 %collective-permute-start.9 = (f32[1,2048]{1,0:T(1,128)S(1)}, f32[1,2048]{1,0:T(1,128)S(1)}, u32[]{:S(2)}, u32[]{:S(2)}) collective-permute-start(f32[1,2048]{1,0:T(1,128)S(1)} %rows.3.refs_1_), channel_id=1, source_target_pairs={{0,2},{1,3},{2,0},{3,1},{4,6},{5,7},{6,4},{7,5},{8,10},{9,11},{10,... | collective-permute-start | bytes 24584 | tf_op jit(solution)/shard_map/ppermute | solution.py:44
  80.5 4.9 %collective-permute-start.8 = (f32[1,2048]{1,0:T(1,128)S(1)}, f32[1,2048]{1,0:T(1,128)S(1)}, u32[]{:S(2)}, u32[]{:S(2)}) collective-permute-start(f32[1,2048]{1,0:T(1,128)S(1)} %rows.3.refs_1_), channel_id=1, source_target_pairs={{0,1},{1,2},{2,3},{3,0},{4,5},{5,6},{6,7},{7,4},{8,9},{9,10},{10,1... | collective-permute-start | bytes 24584 | tf_op jit(solution)/shard_map/ppermute | solution.py:44
  88.7 1.3 collective-permute-start.11
  106.3 2.4 %collective-permute-start.12 = (bf16[512,768]{1,0:T(8,128)(2,1)S(1)}, bf16[512,768]{1,0:T(8,128)(2,1)S(1)}, u32[]{:S(2)}, u32[]{:S(2)}) collective-permute-start(bf16[512,768]{1,0:T(8,128)(2,1)S(1)} %get-tuple-element.17), channel_id=1, source_target_pairs={{0,4},{4,0},{8,12},{12,8},{16,20},{20,16},{24,28},{28,24},{32,36},... | collective-permute-start | bytes 2359304 | tf_op jit(solution)/shard_map/ppermute | solution.py:25
  136.8 31.5 %copy-start.2 = (bf16[16,768]{1,0:T(8,128)(2,1)}, bf16[16,768]{1,0:T(8,128)(2,1)S(1)}, u32[]{:S(2)}) copy-start(bf16[16,768]{1,0:T(8,128)(2,1)S(1)} %multiply_convert_fusion) | copy-start | bytes 73732
  163.9 4.5 %collective-permute-start.13 = (bf16[512,768]{1,0:T(8,128)(2,1)S(1)}, bf16[512,768]{1,0:T(8,128)(2,1)S(1)}, u32[]{:S(2)}, u32[]{:S(2)}) collective-permute-start(bf16[512,768]{1,0:T(8,128)(2,1)S(1)} %bitcast.7), channel_id=1, source_target_pairs={{0,4},{4,0},{8,12},{12,8},{16,20},{20,16},{24,28},{28,24},{32,36},... | collective-permute-start | bytes 2359304 | tf_op jit(solution)/shard_map/ppermute | solution.py:25
  172.9 3.8 %collective-permute-start.16 = (f32[2,2048]{1,0:T(2,128)S(1)}, f32[2,2048]{1,0:T(2,128)S(1)}, u32[]{:S(2)}, u32[]{:S(2)}) collective-permute-start(f32[2,2048]{1,0:T(2,128)S(1)} %add.45), channel_id=1, source_target_pairs={{0,3},{1,0},{2,1},{3,2},{4,7},{5,4},{6,5},{7,6},{8,11},{9,8},{10,9... | collective-permute-start | bytes 49160 | tf_op jit(solution)/shard_map/ppermute | solution.py:44
  173.9 4.9 %collective-permute-start.15 = (f32[2,2048]{1,0:T(2,128)S(1)}, f32[2,2048]{1,0:T(2,128)S(1)}, u32[]{:S(2)}, u32[]{:S(2)}) collective-permute-start(f32[2,2048]{1,0:T(2,128)S(1)} %add.45), channel_id=1, source_target_pairs={{0,1},{1,2},{2,3},{3,0},{4,5},{5,6},{6,7},{7,4},{8,9},{9,10},{10,1... | collective-permute-start | bytes 49160 | tf_op jit(solution)/shard_map/ppermute | solution.py:44
  175.0 5.2 %collective-permute-start.14 = (f32[2,2048]{1,0:T(2,128)S(1)}, f32[2,2048]{1,0:T(2,128)S(1)}, u32[]{:S(2)}, u32[]{:S(2)}) collective-permute-start(f32[2,2048]{1,0:T(2,128)S(1)} %add.45), channel_id=1, source_target_pairs={{0,2},{1,3},{2,0},{3,1},{4,6},{5,7},{6,4},{7,5},{8,10},{9,11},{10,... | collective-permute-start | bytes 49160 | tf_op jit(solution)/shard_map/ppermute | solution.py:44

commit v3 on v2

--- a/solution.py
+++ b/solution.py
@@ -55,14 +55,17 @@
     return jnp.broadcast_to(row, (LANES, row.shape[1])).T
 
 
+def tree(values, join):
+    values = list(values)
+    while len(values) > 1:
+        values = [join(*values[j : j + 2]) if j + 1 < len(values) else values[j]
+                  for j in range(0, len(values), 2)]
+    return values[0]
+
+
 def lane_sums(values):
-    top = values[0]
-    for value in values[1:]:
-        top = jnp.maximum(top, value)
-    total = jnp.exp2(values[0] - top)
-    for value in values[1:]:
-        total = total + jnp.exp2(value - top)
-    return top, total
+    top = tree(values, jnp.maximum)
+    return top, tree([jnp.exp2(value - top) for value in values], jnp.add)
 
 
 def close(top, total):
@@ -137,15 +140,18 @@
     row_ref[...] = close(top_ref[...], total_ref[...])
 
 
-def col_kernel(
-    scores_ref, own_ref, one_ref, two_ref, three_ref, col_ref, row_ref, top_ref, total_ref, *, level
-):
+def row_potential(own_ref, one_ref, two_ref, three_ref, level):
     own, one, two, three = own_ref[...], one_ref[...], two_ref[...], three_ref[...]
     highest = jnp.maximum(jnp.maximum(own, two), jnp.maximum(one, three))
     even = jnp.exp2(own - highest) + jnp.exp2(two - highest)
     odd = jnp.exp2(one - highest) + jnp.exp2(three - highest)
-    row_ref[...] = level - (highest + jnp.log2(even + odd))
-
+    return level - (highest + jnp.log2(even + odd))
+
+
+def col_kernel(
+    scores_ref, own_ref, one_ref, two_ref, three_ref, col_ref, row_ref, top_ref, total_ref, *, level
+):
+    row_ref[...] = row_potential(own_ref, one_ref, two_ref, three_ref, level)
     rows, count = scores_ref.shape
     at = [slice(LANES * j, LANES * (j + 1)) for j in range(count // LANES)]
     points = [jnp.broadcast_to(row_ref[:, a], (SUB, LANES)) for a in at]
@@ -161,46 +167,134 @@
     col_ref[...] = close(top_ref[...].T, total_ref[...].T)
 
 
-def plan_of(scores_ref, first, row_ref, cols_ref):
-    here = slice(first, first + GROUP)
-    shift = jnp.concatenate([cols_ref[here, :]] * (scores_ref.shape[1] // LANES), axis=1)
-    return jnp.exp2((scores_ref[here, :] + row_ref[...]) + shift)
-
-
-def sums_of(scores_ref, row_ref, cols_ref, points_ref, sums_ref, half):
+def sums_of(scores_ref, row_ref, points_ref, sums_ref, half):
     rows = sums_ref.shape[0]
+    width = points_ref.shape[1]
     for first in range(0, rows, GROUP):
-        plan = plan_of(scores_ref, half * rows + first, row_ref, cols_ref)
-        sums_ref[first : first + GROUP, :] = lax.dot_general(
-            plan.astype(BF16),
+        here = slice(first, first + GROUP)
+        far = slice(half * rows + first, half * rows + first + GROUP)
+        shifted = scores_ref[far, :] + row_ref[...]
+        top = jnp.max(shifted, axis=1, keepdims=True)
+        weights = jnp.exp2(shifted - top)
+        total = jnp.sum(weights, axis=1, keepdims=True)
+        sums_ref[here, :width] = lax.dot_general(
+            weights.astype(BF16),
             points_ref[...],
             (((1,), (0,)), ((), ())),
             preferred_element_type=F32,
-        ).astype(sums_ref.dtype)
-
-
-def give_kernel(scores_ref, row_ref, values_ref, points_ref, sums_ref, cols_ref, *, level):
-    cols_ref[...] = on_lanes(col_potential(values_ref, level))
-    sums_of(scores_ref, row_ref, cols_ref, points_ref, sums_ref, 1)
-
-
-def keep_kernel(scores_ref, row_ref, cols_ref, points_ref, sums_ref):
-    sums_of(scores_ref, row_ref, cols_ref, points_ref, sums_ref, 0)
-
-
-def distance_kernel(scores_ref, row_ref, cols_ref, points_ref, fresh_ref, both_ref, *, half):
-    rows = fresh_ref.shape[0]
-    count = points_ref.shape[0]
+        )
+        lane = lax.broadcasted_iota(jnp.int32, (GROUP, LANES), 1)
+        sums_ref[here, width:] = jnp.where(lane < LANES // 2, top, total)
+
+
+def give_kernel(
+    scores_ref, own_ref, one_ref, two_ref, three_ref, points_ref, sums_ref, row_ref, *, level
+):
+    row_ref[...] = row_potential(own_ref, one_ref, two_ref, three_ref, level)
+    sums_of(scores_ref, row_ref, points_ref, sums_ref, 1)
+
+
+def keep_kernel(scores_ref, row_ref, points_ref, sums_ref):
+    sums_of(scores_ref, row_ref, points_ref, sums_ref, 0)
+
+
+def thirds(value):
+    high = value.astype(BF16).astype(F32)
+    rest = value - high
+    middle = rest.astype(BF16).astype(F32)
+    return [high, middle, rest - middle]
+
+
+FIELD = 8
+SPAN = LANES // 2
+
+
+def info_tile(columns):
+    lane = lax.broadcasted_iota(jnp.int32, (SUB, LANES), 1)
+    tile = jnp.zeros((SUB, LANES), F32)
+    for n, column in enumerate(columns):
+        for m, part in enumerate(thirds(column)):
+            spot = n * FIELD + m
+            tile = jnp.where(lane == spot, part[:SUB], tile)
+            tile = jnp.where(lane == SPAN + spot, part[SUB:], tile)
+    return tile.astype(BF16)
+
+
+def info_column(tiles, n):
+    lane = lax.broadcasted_iota(jnp.int32, tiles.shape, 2)
+    halves = []
+    for base in (n * FIELD, SPAN + n * FIELD):
+        mask = (lane >= base) & (lane < base + 3)
+        halves.append(jnp.sum(jnp.where(mask, tiles, 0.0), axis=2, keepdims=True))
+    return jnp.concatenate(halves, axis=1)
+
+
+def join_kernel(mine_ref, theirs_ref, pieces_ref):
+    width = mine_ref.shape[1] - LANES
+    chips = pieces_ref.shape[0]
+    each = mine_ref.shape[0] // chips
+    for chip in range(chips):
+        here = slice(chip * each, (chip + 1) * each)
+        tops = [ref[here, width : width + 1] for ref in (mine_ref, theirs_ref)]
+        totals = [ref[here, width + SPAN : width + SPAN + 1] for ref in (mine_ref, theirs_ref)]
+        top = jnp.maximum(*tops)
+        scales = [jnp.exp2(t - top) for t in tops]
+        total = totals[0] * scales[0] + totals[1] * scales[1]
+        for b in range(width // LANES):
+            lanes = slice(b * LANES, (b + 1) * LANES)
+            both = mine_ref[here, lanes] * scales[0] + theirs_ref[here, lanes] * scales[1]
+            pieces_ref[chip, b * each : (b + 1) * each, :] = both.astype(BF16)
+        pieces_ref[chip, width // LANES * each :, :] = info_tile([top, total])
+
+
+def own_kernel(pieces_ref, own_ref, fresh_ref, *, level):
+    chips = pieces_ref.shape[0]
+    each, width = own_ref.shape
+    blocks = width // LANES
+    tiles = pieces_ref[:, blocks * each :, :].astype(F32)
+    tops = info_column(tiles, 0)
+    totals = info_column(tiles, 1)
+    top = jnp.max(tops, axis=0)
+    scales = jnp.exp2(tops - top[None])
+    total = jnp.sum(totals * scales, axis=0)
+    fresh = []
+    for b in range(blocks):
+        here = slice(b * each, (b + 1) * each)
+        parts = [pieces_ref[chip, here, :].astype(F32) * scales[chip] for chip in range(chips)]
+        fresh.append((tree(parts, jnp.add) / total).astype(BF16))
+        own_ref[:, b * LANES : (b + 1) * LANES] = fresh[-1]
+    info = info_tile([level - (top + jnp.log2(total))])
+    for chip in range(chips):
+        for b in range(blocks):
+            fresh_ref[chip, b * each : (b + 1) * each, :] = fresh[b]
+        fresh_ref[chip, blocks * each :, :] = info
+
+
+def distance_kernel(scores_ref, row_ref, points_ref, fresh_ref, both_ref, *, half):
+    chips = fresh_ref.shape[0]
+    count, width = points_ref.shape
+    blocks = width // LANES
+    each = (fresh_ref.shape[1] - SUB) // blocks
     numerator = jnp.zeros((SUB, count), F32)
     mass = jnp.zeros((SUB, count), F32)
-    for first in range(0, rows, GROUP):
-        fresh = fresh_ref[first : first + GROUP, :]
+    step = GROUP // each
+    for chip in range(0, chips, step):
+        some = slice(chip, chip + step)
+        fresh = jnp.concatenate(
+            [
+                fresh_ref[some, b * each : (b + 1) * each, :].reshape(GROUP, LANES)
+                for b in range(blocks)
+            ],
+            axis=1,
+        )
+        col = info_column(fresh_ref[some, blocks * each :, :].astype(F32), 0).reshape(GROUP, 1)
         wide = fresh.astype(F32)
         squares = jnp.sum(wide * wide, axis=1, keepdims=True)
         cross = lax.dot_general(
             fresh, points_ref[...], (((1,), (1,)), ((), ())), preferred_element_type=F32
         )
-        plan = plan_of(scores_ref, half * rows + first, row_ref, cols_ref)
+        first = (half * chips + chip) * each
+        plan = jnp.exp2((scores_ref[first : first + GROUP, :] + row_ref[...]) + col)
         term = plan * (squares - 2.0 * cross)
         numerator = numerator + jnp.sum(term.reshape(GROUP // SUB, SUB, count), axis=0)
         mass = mass + jnp.sum(plan.reshape(GROUP // SUB, SUB, count), axis=0)
@@ -238,7 +332,6 @@
     pairs = [((rows // GROUP * SUB, count), F32)] * 2
     strip = ((rows, LANES), F32)
     line = ((1, count), F32)
-    sums = (half, width)
 
     scores, part = call(
         lambda *refs: score_kernel(*refs, each=each),
@@ -256,38 +349,46 @@
                 [scores, values],
                 "rows",
             )
-        others = [cen_shift(part, step) for step in (1, 2, 3)]
-        col, row = call(
-            lambda *refs: col_kernel(*refs, level=row_level),
-            [((1, rows), F32), line],
-            [strip] * 2,
-            [scores, part] + others,
-            "cols",
-        )
-        values = spread_cols(col)
-
-    give, cols = call(
-        lambda *refs: give_kernel(*refs, level=col_level),
-        [(sums, BF16), strip],
+        partial = [part] + [cen_shift(part, step) for step in (1, 2, 3)]
+        if iteration < ITERS - 1:
+            col, row = call(
+                lambda *refs: col_kernel(*refs, level=row_level),
+                [((1, rows), F32), line],
+                [strip] * 2,
+                [scores] + partial,
+                "cols",
+            )
+            values = spread_cols(col)
+
+    wide = ((half, width + LANES), F32)
+    piece = ((chips, each * width // LANES + SUB, LANES), BF16)
+    give, row = call(
+        lambda *refs: give_kernel(*refs, level=row_level),
+        [wide, line],
         [],
-        [scores, row, values, points],
+        [scores] + partial + [points],
         "give",
     )
     theirs = other_core(give)
-    (keep,) = call(keep_kernel, [(sums, F32)], [], [scores, row, cols, points], "keep")
-    pieces = exchange((keep + theirs.astype(F32)).astype(BF16).reshape(chips, each, width))
-    own_rows = (total_centroids * jnp.sum(pieces.astype(F32), axis=0)).astype(BF16)
-    mine = from_chips(own_rows).reshape(half, width)
-    other = other_core(mine)
+    (keep,) = call(keep_kernel, [wide], [], [scores, row, points], "keep")
+    (pieces,) = call(join_kernel, [piece], [], [keep, theirs], "join")
+    own_rows, fresh = call(
+        lambda *refs: own_kernel(*refs, level=col_level),
+        [((each, width), BF16), piece],
+        [],
+        [exchange(pieces)],
+        "own",
+    )
+    mine = exchange(fresh)
     terms = [
         call(
             lambda *refs: distance_kernel(*refs, half=part),
             [((2, count), F32)],
             [],
-            [scores, row, cols, points, fresh],
+            [scores, row, points, new],
             "terms",
         )[0]
-        for part, fresh in enumerate((mine, other))
+        for part, new in enumerate((mine, other_core(mine)))
     ]
     both = terms[0] + terms[1]
     one, two, three = [cen_shift(both, step) for step in (1, 2, 3)]

time: 181 us -> 169 us (0.934)
  blocking collectives: 104 us -> 92.4 us
  starting transfers between devices: 14.5 us -> 18.8 us
  waiting for transfers between devices: 19.8 us -> 15.5 us
    all_to_all x5 -> x4, blocking collectives: 104 us -> 92.4 us  [exchange(): return lax.all_to_all(value, 'pts', 0, 0, axis_index_groups=chip_groups())]
    ppermute x12, starting transfers between devices: 14.3 us -> 18.7 us  [cen_shift(): lax.ppermute(value, 'cen', [(i, (i + step) % size) for i in range(size)])]
    ppermute x12, waiting for transfers between devices: 16.1 us -> 11.9 us  [cen_shift(): lax.ppermute(value, 'cen', [(i, (i + step) % size) for i in range(size)])]
    pallas_call x10 -> x11, Pallas kernels: 37.5 us -> 36.7 us  [call(): pl.pallas_call(kernel, out_shape=[jax.ShapeDtypeStruct(shape, dtype) for...]
    ppermute x5 -> x4, waiting for transfers between devices: 3.76 us -> 3.62 us  [other_core(): return lax.ppermute(value, 'pts', [(i, i ^ 1) for i in range(size)])]
  transfers between devices with their start and end apart: 17 -> 16, of which waited for: 15 -> 14; matrix products, arithmetic and copies ran while one was open for 0% -> 0% of each run, Pallas kernels for 4% -> 4%
where the time goes in v3:
time: 169 us; the launch traced here: 168 us
  blocking collectives  92.4 us (55%)
  Pallas kernels  36.7 us (22%)
  starting transfers between devices  18.8 us (11%)
  waiting for transfers between devices  15.5 us (9%)
  local copies, waits for them, and re-layouts  3.44 us (2%)
    all_to_all x4, blocking collectives, exchange(): return lax.all_to_all(value, 'pts', 0, 0, axis_index_groups=chip_groups())  92.4 us
    pallas_call x11, Pallas kernels, call(): pl.pallas_call(kernel, out_shape=[jax.ShapeDtypeStruct(shape, dtype) for...  36.7 us
    ppermute x12, starting transfers between devices, cen_shift(): lax.ppermute(value, 'cen', [(i, (i + step) % size) for i in range(size)])  18.7 us
    ppermute x12, waiting for transfers between devices, cen_shift(): lax.ppermute(value, 'cen', [(i, (i + step) % size) for i in range(size)])  11.9 us
    ppermute x4, waiting for transfers between devices, other_core(): return lax.ppermute(value, 'pts', [(i, i ^ 1) for i in range(size)])  3.62 us
  transfers between devices with their start and end apart: 16, of which 14 were waited for; matrix products, arithmetic and copies ran while one was open for 0% of the time, Pallas kernels for 4%

profile of v3, /device:TPU:2, one launch (start us, length us, event | category | flops | bytes accessed | tf_op | source)
XLA Modules:
  0.0 168.4 jit_solution(5669217388225064833)
XLA Ops:
  0.7 1.9 %copy-done = bf16[2048,768]{1,0:T(8,128)(2,1)S(1)} copy-done((bf16[2048,768]{1,0:T(8,128)(2,1)S(1)}, bf16[2048,768]{1,0:T(8,128)(2,1)}, u32[]{:S(2)}) %copy-start) | copy-done | bytes 3145752
  2.5 1.4 copy-done.2
  3.9 6.6 %scores.1 = (f32[1024,2048]{1,0:T(8,128)S(1)}, f32[1,2048]{1,0:T(1,128)S(1)}) custom-call(s32[1]{0:T(128)} %bitcast.refs_0_, bf16[2048,768]{1,0:T(8,128)(2,1)S(1)} %copy-done, bf16[1024,768]{1,0:T(8,128)(2,1)S(1)} %copy-done.2), custom_call_target="tpu_custom_call" | custom-call | tf_op jit(solution)/shard_map/scores/pallas_call | solution.py:310
  10.6 1.7 collective-permute-start
  12.2 2.9 %collective-permute-start.1 = (f32[1,2048]{1,0:T(1,128)S(1)}, f32[1,2048]{1,0:T(1,128)S(1)}, u32[]{:S(2)}, u32[]{:S(2)}) collective-permute-start(f32[1,2048]{1,0:T(1,128)S(1)} %get-tuple-element.11.refs_1_), channel_id=1, source_target_pairs={{0,2},{1,3},{2,0},{3,1},{4,6},{5,7},{6,4},{7,5},{8,10},{9,11},{10,... | collective-permute-start | bytes 24584 | tf_op jit(solution)/shard_map/ppermute | solution.py:44
  15.1 1.3 collective-permute-start.2
  16.5 0.9 collective-permute-done.1.refs_3_
  17.4 1.4 collective-permute-done.2.refs_4_
  18.8 3.1 %cols.2 = (f32[1,1024]{1,0:T(1,128)S(1)}, f32[1,2048]{1,0:T(1,128)}) custom-call(f32[1024,2048]{1,0:T(8,128)S(1)} %get-tuple-element.10.refs_0_.scores_ref, f32[1,2048]{1,0:T(1,128)S(1)} %get-tuple-element.11.refs_1_, f32[1,2048]{1,0:T(1,128)S(1)} %collective-permute-done.refs_2_, f32[1,2048]{1,0:T(1,128)S(1)} %collective-permute-done.1.refs_3_, ...), custom_call_target="tpu_custom_call" | custom-call | tf_op jit(solution)/shard_map/cols/pallas_call | solution.py:310
  21.9 1.2 collective-permute-done.3
  23.1 0.1 broadcast_in_dim.17
  23.2 20.5 %all_to_all.20.refs_1_ = f32[32,1,1024]{2,1,0:T(1,128)S(1)} all-to-all(f32[32,1,1024]{2,1,0:T(1,128)S(1)} %broadcast_in_dim.17), channel_id=1, replica_groups={{0,8,16,24,32,40,48,56,64,72,80,88,96,104,112,120,128,136,144,152,160,1..., dimensions={0} | all-to-all | bytes 262144 | tf_op jit(solution)/shard_map/all_to_all | solution.py:34
  43.7 3.2 %rows.2.refs_1_ = f32[1,2048]{1,0:T(1,128)S(1)} custom-call(f32[1024,2048]{1,0:T(8,128)S(1)} %get-tuple-element.10.refs_0_.scores_ref, f32[32,1,1024]{2,1,0:T(1,128)S(1)} %all_to_all.20.refs_1_), custom_call_target="tpu_custom_call" | custom-call | tf_op jit(solution)/shard_map/rows/pallas_call | solution.py:310
  46.9 0.3 collective-permute-start.4
  47.2 3.8 %collective-permute-start.5 = (f32[1,2048]{1,0:T(1,128)S(1)}, f32[1,2048]{1,0:T(1,128)S(1)}, u32[]{:S(2)}, u32[]{:S(2)}) collective-permute-start(f32[1,2048]{1,0:T(1,128)S(1)} %rows.2.refs_1_), channel_id=1, source_target_pairs={{0,2},{1,3},{2,0},{3,1},{4,6},{5,7},{6,4},{7,5},{8,10},{9,11},{10,... | collective-permute-start | bytes 24584 | tf_op jit(solution)/shard_map/ppermute | solution.py:44
  51.0 0.1 collective-permute-start.6
  51.1 0.7 collective-permute-done.4.refs_2_
  51.8 0.9 collective-permute-done.5.refs_3_
  52.7 1.9 %collective-permute-done.6.refs_4_ = f32[1,2048]{1,0:T(1,128)S(1)} collective-permute-done((f32[1,2048]{1,0:T(1,128)S(1)}, f32[1,2048]{1,0:T(1,128)S(1)}, u32[]{:S(2)}, u32[]{:S(2)}) %collective-permute-start.6) | collective-permute-done | bytes 8224 | tf_op jit(solution)/shard_map/ppermute | solution.py:44
  54.6 3.1 %cols.3 = (f32[1,1024]{1,0:T(1,128)S(1)}, f32[1,2048]{1,0:T(1,128)}) custom-call(f32[1024,2048]{1,0:T(8,128)S(1)} %get-tuple-element.10.refs_0_.scores_ref, f32[1,2048]{1,0:T(1,128)S(1)} %rows.2.refs_1_, f32[1,2048]{1,0:T(1,128)S(1)} %collective-permute-done.4.refs_2_, f32[1,2048]{1,0:T(1,128)S(1)} %collective-permute-done.5.refs_3_, ...), custom_call_target="tpu_custom_call" | custom-call | tf_op jit(solution)/shard_map/cols/pallas_call | solution.py:310
  57.7 1.2 collective-permute-done.7
  58.9 0.1 broadcast_in_dim.19
  59.0 14.1 %all_to_all.21.refs_1_ = f32[32,1,1024]{2,1,0:T(1,128)S(1)} all-to-all(f32[32,1,1024]{2,1,0:T(1,128)S(1)} %broadcast_in_dim.19), channel_id=1, replica_groups={{0,8,16,24,32,40,48,56,64,72,80,88,96,104,112,120,128,136,144,152,160,1..., dimensions={0} | all-to-all | bytes 262144 | tf_op jit(solution)/shard_map/all_to_all | solution.py:34
  73.1 3.2 %rows.3.refs_1_ = f32[1,2048]{1,0:T(1,128)S(1)} custom-call(f32[1024,2048]{1,0:T(8,128)S(1)} %get-tuple-element.10.refs_0_.scores_ref, f32[32,1,1024]{2,1,0:T(1,128)S(1)} %all_to_all.21.refs_1_), custom_call_target="tpu_custom_call" | custom-call | tf_op jit(solution)/shard_map/rows/pallas_call | solution.py:310
  76.4 1.6 collective-permute-start.10
  77.9 0.7 collective-permute-start.8
  78.6 1.5 collective-permute-start.9
  80.1 0.1 collective-permute-done.10.refs_4_
  80.3 2.5 %collective-permute-done.8.refs_2_ = f32[1,2048]{1,0:T(1,128)S(1)} collective-permute-done((f32[1,2048]{1,0:T(1,128)S(1)}, f32[1,2048]{1,0:T(1,128)S(1)}, u32[]{:S(2)}, u32[]{:S(2)}) %collective-permute-start.8) | collective-permute-done | bytes 8224 | tf_op jit(solution)/shard_map/ppermute | solution.py:44
  82.8 1.0 collective-permute-done.9.refs_3_
  83.8 2.5 %give.1 = (f32[512,896]{1,0:T(8,128)S(1)}, f32[1,2048]{1,0:T(1,128)S(1)}) custom-call(f32[1024,2048]{1,0:T(8,128)S(1)} %get-tuple-element.10.refs_0_.scores_ref, f32[1,2048]{1,0:T(1,128)S(1)} %rows.3.refs_1_, f32[1,2048]{1,0:T(1,128)S(1)} %collective-permute-done.8.refs_2_, f32[1,2048]{1,0:T(1,128)S(1)} %collective-permute-done.9.refs_3_, ...), custom_call_target="tpu_custom_call" | custom-call | tf_op jit(solution)/shard_map/give/pallas_call | solution.py:310
  86.3 0.1 collective-permute-start.11
  86.4 2.5 %keep.1.mine_ref = f32[512,896]{1,0:T(8,128)S(1)} custom-call(f32[1024,2048]{1,0:T(8,128)S(1)} %get-tuple-element.10.refs_0_.scores_ref, f32[1,2048]{1,0:T(1,128)S(1)} %get-tuple-element.14.row_ref.refs_1_, bf16[2048,768]{1,0:T(8,128)(2,1)S(1)} %copy-done), custom_call_target="tpu_custom_call" | custom-call | tf_op jit(solution)/shard_map/keep/pallas_call | solution.py:310
  88.9 1.3 collective-permute-done.11.theirs_ref
  90.2 2.4 %join.1 = bf16[32,104,128]{2,1,0:T(8,128)(2,1)S(1)} custom-call(f32[512,896]{1,0:T(8,128)S(1)} %keep.1.mine_ref, f32[512,896]{1,0:T(8,128)S(1)} %collective-permute-done.11.theirs_ref), custom_call_target="tpu_custom_call" | custom-call | tf_op jit(solution)/shard_map/join/pallas_call | solution.py:310
  92.6 0.0 copy-start.1
  92.6 29.4 %all_to_all.22.refs_0_ = bf16[32,104,128]{2,1,0:T(8,128)(2,1)S(1)} all-to-all(bf16[32,104,128]{2,1,0:T(8,128)(2,1)S(1)} %join.1), channel_id=1, replica_groups={{0,8,16,24,32,40,48,56,64,72,80,88,96,104,112,120,128,136,144,152,160,1..., dimensions={0} | all-to-all | bytes 1703936 | tf_op jit(solution)/shard_map/all_to_all | solution.py:34
  122.1 1.1 own.1
  123.1 28.4 %all_to_all.23.refs_3_ = bf16[32,104,128]{2,1,0:T(8,128)(2,1)S(1)} all-to-all(bf16[32,104,128]{2,1,0:T(8,128)(2,1)S(1)} %get-tuple-element.17), channel_id=1, replica_groups={{0,8,16,24,32,40,48,56,64,72,80,88,96,104,112,120,128,136,144,152,160,1..., dimensions={0} | all-to-all | bytes 1703936 | tf_op jit(solution)/shard_map/all_to_all | solution.py:34
  151.5 4.5 %terms.2 = f32[2,2048]{1,0:T(2,128)S(1)} custom-call(f32[1024,2048]{1,0:T(8,128)S(1)} %get-tuple-element.10.refs_0_.scores_ref, f32[1,2048]{1,0:T(1,128)S(1)} %get-tuple-element.14.row_ref.refs_1_, bf16[2048,768]{1,0:T(8,128)(2,1)S(1)} %copy-done.1, bf16[32,104,128]{2,1,0:T(8,128)(2,1)S(1)} %all_to_all.23.refs_3_), custom_call_target="tpu_custom_call" | custom-call | tf_op jit(solution)/shard_map/terms/pallas_call | solution.py:310
  156.0 4.4 %terms.3 = f32[2,2048]{1,0:T(2,128)S(1)} custom-call(f32[1024,2048]{1,0:T(8,128)S(1)} %get-tuple-element.10.refs_0_.scores_ref, f32[1,2048]{1,0:T(1,128)S(1)} %get-tuple-element.14.row_ref.refs_1_, bf16[2048,768]{1,0:T(8,128)(2,1)S(1)} %copy-done.1, bf16[32,104,128]{2,1,0:T(8,128)(2,1)S(1)} %collective-permute-done.12.refs_3_), custom_call_target="tpu_custom_call" | custom-call | tf_op jit(solution)/shard_map/terms/pallas_call | solution.py:310
  160.5 1.6 collective-permute-start.13
  162.1 1.9 %collective-permute-start.14 = (f32[2,2048]{1,0:T(2,128)S(1)}, f32[2,2048]{1,0:T(2,128)S(1)}, u32[]{:S(2)}, u32[]{:S(2)}) collective-permute-start(f32[2,2048]{1,0:T(2,128)S(1)} %add.33), channel_id=1, source_target_pairs={{0,1},{1,2},{2,3},{3,0},{4,5},{5,6},{6,7},{7,4},{8,9},{9,10},{10,1... | collective-permute-start | bytes 49160 | tf_op jit(solution)/shard_map/ppermute | solution.py:44
  164.0 1.3 collective-permute-start.15
  165.3 0.6 collective-permute-done.13
  165.9 1.1 collective-permute-done.14
  167.1 0.7 collective-permute-done.15
  167.8 0.6 fusion
  (14 shorter events, 0.1 us)
Async XLA Ops:
  0.6 1.9 %copy-start = (bf16[2048,768]{1,0:T(8,128)(2,1)S(1)}, bf16[2048,768]{1,0:T(8,128)(2,1)}, u32[]{:S(2)}) copy-start(bf16[2048,768]{1,0:T(8,128)(2,1)} %refs_2_.5) | copy-start | bytes 9437188
  2.5 1.4 copy-start.2
  10.6 5.9 %collective-permute-start = (f32[1,2048]{1,0:T(1,128)S(1)}, f32[1,2048]{1,0:T(1,128)S(1)}, u32[]{:S(2)}, u32[]{:S(2)}) collective-permute-start(f32[1,2048]{1,0:T(1,128)S(1)} %get-tuple-element.11.refs_1_), channel_id=1, source_target_pairs={{0,1},{1,2},{2,3},{3,0},{4,5},{5,6},{6,7},{7,4},{8,9},{9,10},{10,1... | collective-permute-start | bytes 24584 | tf_op jit(solution)/shard_map/ppermute | solution.py:44
  12.2 5.2 %collective-permute-start.1 = (f32[1,2048]{1,0:T(1,128)S(1)}, f32[1,2048]{1,0:T(1,128)S(1)}, u32[]{:S(2)}, u32[]{:S(2)}) collective-permute-start(f32[1,2048]{1,0:T(1,128)S(1)} %get-tuple-element.11.refs_1_), channel_id=1, source_target_pairs={{0,2},{1,3},{2,0},{3,1},{4,6},{5,7},{6,4},{7,5},{8,10},{9,11},{10,... | collective-permute-start | bytes 24584 | tf_op jit(solution)/shard_map/ppermute | solution.py:44
  15.1 3.7 %collective-permute-start.2 = (f32[1,2048]{1,0:T(1,128)S(1)}, f32[1,2048]{1,0:T(1,128)S(1)}, u32[]{:S(2)}, u32[]{:S(2)}) collective-permute-start(f32[1,2048]{1,0:T(1,128)S(1)} %get-tuple-element.11.refs_1_), channel_id=1, source_target_pairs={{0,3},{1,0},{2,1},{3,2},{4,7},{5,4},{6,5},{7,6},{8,11},{9,8},{10,9... | collective-permute-start | bytes 24584 | tf_op jit(solution)/shard_map/ppermute | solution.py:44
  21.9 1.2 collective-permute-start.3
  46.9 4.9 %collective-permute-start.4 = (f32[1,2048]{1,0:T(1,128)S(1)}, f32[1,2048]{1,0:T(1,128)S(1)}, u32[]{:S(2)}, u32[]{:S(2)}) collective-permute-start(f32[1,2048]{1,0:T(1,128)S(1)} %rows.2.refs_1_), channel_id=1, source_target_pairs={{0,1},{1,2},{2,3},{3,0},{4,5},{5,6},{6,7},{7,4},{8,9},{9,10},{10,1... | collective-permute-start | bytes 24584 | tf_op jit(solution)/shard_map/ppermute | solution.py:44
  47.2 5.6 %collective-permute-start.5 = (f32[1,2048]{1,0:T(1,128)S(1)}, f32[1,2048]{1,0:T(1,128)S(1)}, u32[]{:S(2)}, u32[]{:S(2)}) collective-permute-start(f32[1,2048]{1,0:T(1,128)S(1)} %rows.2.refs_1_), channel_id=1, source_target_pairs={{0,2},{1,3},{2,0},{3,1},{4,6},{5,7},{6,4},{7,5},{8,10},{9,11},{10,... | collective-permute-start | bytes 24584 | tf_op jit(solution)/shard_map/ppermute | solution.py:44
  51.0 3.7 %collective-permute-start.6 = (f32[1,2048]{1,0:T(1,128)S(1)}, f32[1,2048]{1,0:T(1,128)S(1)}, u32[]{:S(2)}, u32[]{:S(2)}) collective-permute-start(f32[1,2048]{1,0:T(1,128)S(1)} %rows.2.refs_1_), channel_id=1, source_target_pairs={{0,3},{1,0},{2,1},{3,2},{4,7},{5,4},{6,5},{7,6},{8,11},{9,8},{10,9... | collective-permute-start | bytes 24584 | tf_op jit(solution)/shard_map/ppermute | solution.py:44
  57.7 1.2 collective-permute-start.7
  76.4 3.9 %collective-permute-start.10 = (f32[1,2048]{1,0:T(1,128)S(1)}, f32[1,2048]{1,0:T(1,128)S(1)}, u32[]{:S(2)}, u32[]{:S(2)}) collective-permute-start(f32[1,2048]{1,0:T(1,128)S(1)} %rows.3.refs_1_), channel_id=1, source_target_pairs={{0,3},{1,0},{2,1},{3,2},{4,7},{5,4},{6,5},{7,6},{8,11},{9,8},{10,9... | collective-permute-start | bytes 24584 | tf_op jit(solution)/shard_map/ppermute | solution.py:44
  77.9 4.9 %collective-permute-start.8 = (f32[1,2048]{1,0:T(1,128)S(1)}, f32[1,2048]{1,0:T(1,128)S(1)}, u32[]{:S(2)}, u32[]{:S(2)}) collective-permute-start(f32[1,2048]{1,0:T(1,128)S(1)} %rows.3.refs_1_), channel_id=1, source_target_pairs={{0,1},{1,2},{2,3},{3,0},{4,5},{5,6},{6,7},{7,4},{8,9},{9,10},{10,1... | collective-permute-start | bytes 24584 | tf_op jit(solution)/shard_map/ppermute | solution.py:44
  78.6 5.2 %collective-permute-start.9 = (f32[1,2048]{1,0:T(1,128)S(1)}, f32[1,2048]{1,0:T(1,128)S(1)}, u32[]{:S(2)}, u32[]{:S(2)}) collective-permute-start(f32[1,2048]{1,0:T(1,128)S(1)} %rows.3.refs_1_), channel_id=1, source_target_pairs={{0,2},{1,3},{2,0},{3,1},{4,6},{5,7},{6,4},{7,5},{8,10},{9,11},{10,... | collective-permute-start | bytes 24584 | tf_op jit(solution)/shard_map/ppermute | solution.py:44
  86.3 3.9 %collective-permute-start.11 = (f32[512,896]{1,0:T(8,128)S(1)}, f32[512,896]{1,0:T(8,128)S(1)}, u32[]{:S(2)}, u32[]{:S(2)}) collective-permute-start(f32[512,896]{1,0:T(8,128)S(1)} %get-tuple-element.15), channel_id=1, source_target_pairs={{0,4},{4,0},{8,12},{12,8},{16,20},{20,16},{24,28},{28,24},{32,36},... | collective-permute-start | bytes 5505032 | tf_op jit(solution)/shard_map/ppermute | solution.py:25
  92.6 58.9 %copy-start.1 = (bf16[2048,768]{1,0:T(8,128)(2,1)S(1)}, bf16[2048,768]{1,0:T(8,128)(2,1)}, u32[]{:S(2)}) copy-start(bf16[2048,768]{1,0:T(8,128)(2,1)} %refs_2_.5) | copy-start | bytes 9437188
  151.5 4.5 %collective-permute-start.12 = (bf16[32,104,128]{2,1,0:T(8,128)(2,1)S(1)}, bf16[32,104,128]{2,1,0:T(8,128)(2,1)S(1)}, u32[]{:S(2)}, u32[]{:S(2)}) collective-permute-start(bf16[32,104,128]{2,1,0:T(8,128)(2,1)S(1)} %all_to_all.23.refs_3_), channel_id=1, source_target_pairs={{0,4},{4,0},{8,12},{12,8},{16,20},{20,16},{24,28},{28,24},{32,36},... | collective-permute-start | bytes 2555912 | tf_op jit(solution)/shard_map/ppermute | solution.py:25
  160.5 5.4 %collective-permute-start.13 = (f32[2,2048]{1,0:T(2,128)S(1)}, f32[2,2048]{1,0:T(2,128)S(1)}, u32[]{:S(2)}, u32[]{:S(2)}) collective-permute-start(f32[2,2048]{1,0:T(2,128)S(1)} %add.33), channel_id=1, source_target_pairs={{0,2},{1,3},{2,0},{3,1},{4,6},{5,7},{6,4},{7,5},{8,10},{9,11},{10,... | collective-permute-start | bytes 49160 | tf_op jit(solution)/shard_map/ppermute | solution.py:44
  162.1 4.9 %collective-permute-start.14 = (f32[2,2048]{1,0:T(2,128)S(1)}, f32[2,2048]{1,0:T(2,128)S(1)}, u32[]{:S(2)}, u32[]{:S(2)}) collective-permute-start(f32[2,2048]{1,0:T(2,128)S(1)} %add.33), channel_id=1, source_target_pairs={{0,1},{1,2},{2,3},{3,0},{4,5},{5,6},{6,7},{7,4},{8,9},{9,10},{10,1... | collective-permute-start | bytes 49160 | tf_op jit(solution)/shard_map/ppermute | solution.py:44
  164.0 3.7 %collective-permute-start.15 = (f32[2,2048]{1,0:T(2,128)S(1)}, f32[2,2048]{1,0:T(2,128)S(1)}, u32[]{:S(2)}, u32[]{:S(2)}) collective-permute-start(f32[2,2048]{1,0:T(2,128)S(1)} %add.33), channel_id=1, source_target_pairs={{0,3},{1,0},{2,1},{3,2},{4,7},{5,4},{6,5},{7,6},{8,11},{9,8},{10,9... | collective-permute-start | bytes 49160 | tf_op jit(solution)/shard_map/ppermute | solution.py:44

commit v4 on v3

--- a/solution.py
+++ b/solution.py
@@ -16,6 +16,7 @@
 LANES = 128
 SUB = 8
 GROUP = 128
+UNROLL = 16
 F32 = jnp.float32
 BF16 = jnp.bfloat16
 
@@ -80,19 +81,16 @@
 
     def step(block, carry):
         here = pl.ds(pl.multiple_of(block * LANES, LANES), LANES)
-        values = [scores_ref[a, here] for a in at]
-        if cols is not None:
-            values = [v + c for v, c in zip(values, cols)]
-        top, total = lane_sums(values)
+        top, total = lane_sums([scores_ref[a, here] + c[...] for a, c in zip(at, cols)])
         top_ref[out, here] = top
         total_ref[out, here] = total
         return carry
 
-    lax.fori_loop(0, scores_ref.shape[1] // LANES, step, 0, unroll=2)
+    lax.fori_loop(0, scores_ref.shape[1] // LANES, step, 0, unroll=UNROLL)
 
 
 def score_kernel(
-    core_ref, points_ref, centroids_ref, scores_ref, row_ref, split_ref, top_ref, total_ref, *, each
+    core_ref, points_ref, centroids_ref, scores_ref, row_ref, turned_ref, split_ref, *, each
 ):
     count = points_ref.shape[0]
     rows = centroids_ref.shape[0]
@@ -107,20 +105,20 @@
             split_ref[pl.ds(here, each), :] = centroids_ref[pl.ds(start, each), :]
         return carry
 
-    lax.fori_loop(0, blocks, order, 0)
+    lax.fori_loop(0, blocks, order, 0, unroll=4)
     chunk = 256
     for first in range(0, count, chunk):
         here = slice(first, first + chunk)
+        turned = points_ref[here, :].T
+        turned_ref[:, here] = turned
         product = lax.dot_general(
-            split_ref[...],
-            points_ref[here, :],
-            (((1,), (1,)), ((), ())),
-            preferred_element_type=F32,
+            split_ref[...], turned, (((1,), (0,)), ((), ())), preferred_element_type=F32
         )
-        scores_ref[:, here] = (sharpness * LOG2E) * product
-    for group in range(rows // GROUP):
-        group_pairs(scores_ref, group, None, top_ref, total_ref)
-    row_ref[...] = close(top_ref[...], total_ref[...])
+        score = (sharpness * LOG2E) * product
+        scores_ref[:, here] = score
+        top = jnp.max(score, axis=0, keepdims=True)
+        total = jnp.sum(jnp.exp2(score - top), axis=0, keepdims=True)
+        row_ref[:, here] = top + jnp.log2(total)
 
 
 def col_potential(values_ref, level):
@@ -134,7 +132,7 @@
     cols_ref[...] = on_lanes(col_potential(values_ref, level))
     for group in range(scores_ref.shape[0] // GROUP):
         cols = [
-            cols_ref[pl.ds(group * GROUP + SUB * j, SUB), :] for j in range(GROUP // SUB)
+            cols_ref.at[pl.ds(group * GROUP + SUB * j, SUB), :] for j in range(GROUP // SUB)
         ]
         group_pairs(scores_ref, group, cols, top_ref, total_ref)
     row_ref[...] = close(top_ref[...], total_ref[...])
@@ -154,16 +152,15 @@
     row_ref[...] = row_potential(own_ref, one_ref, two_ref, three_ref, level)
     rows, count = scores_ref.shape
     at = [slice(LANES * j, LANES * (j + 1)) for j in range(count // LANES)]
-    points = [jnp.broadcast_to(row_ref[:, a], (SUB, LANES)) for a in at]
 
     def step(block, carry):
         here = pl.ds(pl.multiple_of(block * SUB, SUB), SUB)
-        top, total = lane_sums([scores_ref[here, a] + p for a, p in zip(at, points)])
+        top, total = lane_sums([scores_ref[here, a] + row_ref[:, a] for a in at])
         top_ref[here, :] = top
         total_ref[here, :] = total
         return carry
 
-    lax.fori_loop(0, rows // SUB, step, 0, unroll=2)
+    lax.fori_loop(0, rows // SUB, step, 0, unroll=UNROLL)
     col_ref[...] = close(top_ref[...].T, total_ref[...].T)
 
 
@@ -209,15 +206,14 @@
 SPAN = LANES // 2
 
 
-def info_tile(columns):
-    lane = lax.broadcasted_iota(jnp.int32, (SUB, LANES), 1)
-    tile = jnp.zeros((SUB, LANES), F32)
+def info_tiles(columns):
+    lane = lax.broadcasted_iota(jnp.int32, columns[0][:, :SUB].shape, 2)
+    tiles = jnp.zeros(lane.shape, F32)
     for n, column in enumerate(columns):
-        for m, part in enumerate(thirds(column)):
-            spot = n * FIELD + m
-            tile = jnp.where(lane == spot, part[:SUB], tile)
-            tile = jnp.where(lane == SPAN + spot, part[SUB:], tile)
-    return tile.astype(BF16)
+        both = jnp.where(lane < SPAN, column[:, :SUB], column[:, SUB:])
+        for m, part in enumerate(thirds(both)):
+            tiles = jnp.where(lane % SPAN == n * FIELD + m, part, tiles)
+    return tiles.astype(BF16)
 
 
 def info_column(tiles, n):
@@ -233,18 +229,24 @@
     width = mine_ref.shape[1] - LANES
     chips = pieces_ref.shape[0]
     each = mine_ref.shape[0] // chips
-    for chip in range(chips):
-        here = slice(chip * each, (chip + 1) * each)
-        tops = [ref[here, width : width + 1] for ref in (mine_ref, theirs_ref)]
-        totals = [ref[here, width + SPAN : width + SPAN + 1] for ref in (mine_ref, theirs_ref)]
-        top = jnp.maximum(*tops)
-        scales = [jnp.exp2(t - top) for t in tops]
-        total = totals[0] * scales[0] + totals[1] * scales[1]
-        for b in range(width // LANES):
-            lanes = slice(b * LANES, (b + 1) * LANES)
-            both = mine_ref[here, lanes] * scales[0] + theirs_ref[here, lanes] * scales[1]
-            pieces_ref[chip, b * each : (b + 1) * each, :] = both.astype(BF16)
-        pieces_ref[chip, width // LANES * each :, :] = info_tile([top, total])
+    lane = lax.broadcasted_iota(jnp.int32, (mine_ref.shape[0], LANES), 1)
+    tops, totals = [], []
+    for ref in (mine_ref, theirs_ref):
+        straight = ref[:, width:]
+        swapped = pltpu.roll(straight, SPAN, 1)
+        tops.append(jnp.where(lane < SPAN, straight, swapped))
+        totals.append(jnp.where(lane < SPAN, swapped, straight))
+    top = jnp.maximum(*tops)
+    scales = [jnp.exp2(t - top) for t in tops]
+    total = totals[0] * scales[0] + totals[1] * scales[1]
+    for b in range(width // LANES):
+        lanes = slice(b * LANES, (b + 1) * LANES)
+        both = mine_ref[:, lanes] * scales[0] + theirs_ref[:, lanes] * scales[1]
+        here = slice(b * each, (b + 1) * each)
+        pieces_ref[:, here, :] = both.astype(BF16).reshape(chips, each, LANES)
+    shape = (chips, each, LANES)
+    tiles = info_tiles([top.reshape(shape), total.reshape(shape)])
+    pieces_ref[:, width // LANES * each :, :] = tiles
 
 
 def own_kernel(pieces_ref, own_ref, fresh_ref, *, level):
@@ -263,16 +265,17 @@
         parts = [pieces_ref[chip, here, :].astype(F32) * scales[chip] for chip in range(chips)]
         fresh.append((tree(parts, jnp.add) / total).astype(BF16))
         own_ref[:, b * LANES : (b + 1) * LANES] = fresh[-1]
-    info = info_tile([level - (top + jnp.log2(total))])
+    col = jnp.broadcast_to(level - (top + jnp.log2(total)), (each, LANES))
+    info = info_tiles([col[None]])[0]
     for chip in range(chips):
         for b in range(blocks):
             fresh_ref[chip, b * each : (b + 1) * each, :] = fresh[b]
         fresh_ref[chip, blocks * each :, :] = info
 
 
-def distance_kernel(scores_ref, row_ref, points_ref, fresh_ref, both_ref, *, half):
+def distance_kernel(scores_ref, row_ref, turned_ref, fresh_ref, both_ref, *, half):
     chips = fresh_ref.shape[0]
-    count, width = points_ref.shape
+    width, count = turned_ref.shape
     blocks = width // LANES
     each = (fresh_ref.shape[1] - SUB) // blocks
     numerator = jnp.zeros((SUB, count), F32)
@@ -291,7 +294,7 @@
         wide = fresh.astype(F32)
         squares = jnp.sum(wide * wide, axis=1, keepdims=True)
         cross = lax.dot_general(
-            fresh, points_ref[...], (((1,), (1,)), ((), ())), preferred_element_type=F32
+            fresh, turned_ref[...], (((1,), (0,)), ((), ())), preferred_element_type=F32
         )
         first = (half * chips + chip) * each
         plan = jnp.exp2((scores_ref[first : first + GROUP, :] + row_ref[...]) + col)
@@ -333,10 +336,10 @@
     strip = ((rows, LANES), F32)
     line = ((1, count), F32)
 
-    scores, part = call(
+    scores, part, turned = call(
         lambda *refs: score_kernel(*refs, each=each),
-        [((rows, count), F32), line],
-        [((rows, width), BF16)] + pairs,
+        [((rows, count), F32), line, ((width, count), BF16)],
+        [((rows, width), BF16)],
         [core.astype(jnp.int32).reshape(1), points, centroids],
         "scores",
     )
@@ -385,7 +388,7 @@
             lambda *refs: distance_kernel(*refs, half=part),
             [((2, count), F32)],
             [],
-            [scores, row, points, new],
+            [scores, row, turned, new],
             "terms",
         )[0]
         for part, new in enumerate((mine, other_core(mine)))

time: 169 us -> 156 us (0.923)
  Pallas kernels: 36.7 us -> 24.3 us
    pallas_call x11, Pallas kernels: 36.7 us -> 24.3 us  [call(): pl.pallas_call(kernel, out_shape=[jax.ShapeDtypeStruct(shape, dtype) for...]
  transfers between devices with their start and end apart: 16 -> 16, of which waited for: 14 -> 14; matrix products, arithmetic and copies ran while one was open for 0% -> 0% of each run, Pallas kernels for 4% -> 3%
where the time goes in v4:
time: 156 us; the launch traced here: 155 us
  blocking collectives  92.1 us (59%)
  Pallas kernels  24.3 us (16%)
  starting transfers between devices  18.7 us (12%)
  waiting for transfers between devices  15.5 us (10%)
  local copies, waits for them, and re-layouts  3.43 us (2%)
    all_to_all x4, blocking collectives, exchange(): return lax.all_to_all(value, 'pts', 0, 0, axis_index_groups=chip_groups())  92.1 us
    pallas_call x11, Pallas kernels, call(): pl.pallas_call(kernel, out_shape=[jax.ShapeDtypeStruct(shape, dtype) for...  24.3 us
    ppermute x12, starting transfers between devices, cen_shift(): lax.ppermute(value, 'cen', [(i, (i + step) % size) for i in range(size)])  18.6 us
    ppermute x12, waiting for transfers between devices, cen_shift(): lax.ppermute(value, 'cen', [(i, (i + step) % size) for i in range(size)])  11.9 us
    ppermute x4, waiting for transfers between devices, other_core(): return lax.ppermute(value, 'pts', [(i, i ^ 1) for i in range(size)])  3.62 us
    unnamed x4, local copies, waits for them, and re-layouts  3.29 us
  transfers between devices with their start and end apart: 16, of which 14 were waited for; matrix products, arithmetic and copies ran while one was open for 0% of the time, Pallas kernels for 3%

profile of v4, /device:TPU:2, one launch (start us, length us, event | category | flops | bytes accessed | tf_op | source)
XLA Modules:
  0.0 155.5 jit_solution(1143921368622994384)
XLA Ops:
  0.6 1.9 %copy-done = bf16[2048,768]{1,0:T(8,128)(2,1)S(1)} copy-done((bf16[2048,768]{1,0:T(8,128)(2,1)S(1)}, bf16[2048,768]{1,0:T(8,128)(2,1)}, u32[]{:S(2)}) %copy-start) | copy-done | bytes 3145752
  2.5 1.4 copy-done.1
  3.9 4.9 %scores.1 = (f32[1024,2048]{1,0:T(8,128)S(1)}, f32[1,2048]{1,0:T(1,128)S(1)}, bf16[768,2048]{1,0:T(8,128)(2,1)S(1)}) custom-call(s32[1]{0:T(128)} %bitcast.refs_0_, bf16[2048,768]{1,0:T(8,128)(2,1)S(1)} %copy-done, bf16[1024,768]{1,0:T(8,128)(2,1)S(1)} %copy-done.1), custom_call_target="tpu_custom_call" | custom-call | tf_op jit(solution)/shard_map/scores/pallas_call | solution.py:313
  8.8 1.7 %collective-permute-start = (f32[1,2048]{1,0:T(1,128)S(1)}, f32[1,2048]{1,0:T(1,128)S(1)}, u32[]{:S(2)}, u32[]{:S(2)}) collective-permute-start(f32[1,2048]{1,0:T(1,128)S(1)} %get-tuple-element.12.refs_1_), channel_id=1, source_target_pairs={{0,1},{1,2},{2,3},{3,0},{4,5},{5,6},{6,7},{7,4},{8,9},{9,10},{10,1... | collective-permute-start | bytes 24584 | tf_op jit(solution)/shard_map/ppermute | solution.py:45
  10.5 2.9 %collective-permute-start.1 = (f32[1,2048]{1,0:T(1,128)S(1)}, f32[1,2048]{1,0:T(1,128)S(1)}, u32[]{:S(2)}, u32[]{:S(2)}) collective-permute-start(f32[1,2048]{1,0:T(1,128)S(1)} %get-tuple-element.12.refs_1_), channel_id=1, source_target_pairs={{0,2},{1,3},{2,0},{3,1},{4,6},{5,7},{6,4},{7,5},{8,10},{9,11},{10,... | collective-permute-start | bytes 24584 | tf_op jit(solution)/shard_map/ppermute | solution.py:45
  13.4 1.3 collective-permute-start.2
  14.7 0.9 collective-permute-done.1.refs_3_
  15.6 1.4 collective-permute-done.2.refs_4_
  17.0 2.0 %cols.2 = (f32[1,1024]{1,0:T(1,128)S(1)}, f32[1,2048]{1,0:T(1,128)}) custom-call(f32[1024,2048]{1,0:T(8,128)S(1)} %get-tuple-element.11.refs_0_.scores_ref, f32[1,2048]{1,0:T(1,128)S(1)} %get-tuple-element.12.refs_1_, f32[1,2048]{1,0:T(1,128)S(1)} %collective-permute-done.refs_2_, f32[1,2048]{1,0:T(1,128)S(1)} %collective-permute-done.1.refs_3_, ...), custom_call_target="tpu_custom_call" | custom-call | tf_op jit(solution)/shard_map/cols/pallas_call | solution.py:313
  19.1 1.2 collective-permute-done.3
  20.3 0.1 broadcast_in_dim.17
  20.4 20.5 %all_to_all.20.refs_1_ = f32[32,1,1024]{2,1,0:T(1,128)S(1)} all-to-all(f32[32,1,1024]{2,1,0:T(1,128)S(1)} %broadcast_in_dim.17), channel_id=1, replica_groups={{0,8,16,24,32,40,48,56,64,72,80,88,96,104,112,120,128,136,144,152,160,1..., dimensions={0} | all-to-all | bytes 262144 | tf_op jit(solution)/shard_map/all_to_all | solution.py:35
  40.9 2.0 %rows.2.refs_1_ = f32[1,2048]{1,0:T(1,128)S(1)} custom-call(f32[1024,2048]{1,0:T(8,128)S(1)} %get-tuple-element.11.refs_0_.scores_ref, f32[32,1,1024]{2,1,0:T(1,128)S(1)} %all_to_all.20.refs_1_), custom_call_target="tpu_custom_call" | custom-call | tf_op jit(solution)/shard_map/rows/pallas_call | solution.py:313
  42.9 0.3 collective-permute-start.4
  43.1 3.8 %collective-permute-start.5 = (f32[1,2048]{1,0:T(1,128)S(1)}, f32[1,2048]{1,0:T(1,128)S(1)}, u32[]{:S(2)}, u32[]{:S(2)}) collective-permute-start(f32[1,2048]{1,0:T(1,128)S(1)} %rows.2.refs_1_), channel_id=1, source_target_pairs={{0,2},{1,3},{2,0},{3,1},{4,6},{5,7},{6,4},{7,5},{8,10},{9,11},{10,... | collective-permute-start | bytes 24584 | tf_op jit(solution)/shard_map/ppermute | solution.py:45
  47.0 0.1 collective-permute-start.6
  47.1 0.7 collective-permute-done.4.refs_2_
  47.8 0.9 collective-permute-done.5.refs_3_
  48.7 1.9 %collective-permute-done.6.refs_4_ = f32[1,2048]{1,0:T(1,128)S(1)} collective-permute-done((f32[1,2048]{1,0:T(1,128)S(1)}, f32[1,2048]{1,0:T(1,128)S(1)}, u32[]{:S(2)}, u32[]{:S(2)}) %collective-permute-start.6) | collective-permute-done | bytes 8224 | tf_op jit(solution)/shard_map/ppermute | solution.py:45
  50.6 2.0 %cols.3 = (f32[1,1024]{1,0:T(1,128)S(1)}, f32[1,2048]{1,0:T(1,128)}) custom-call(f32[1024,2048]{1,0:T(8,128)S(1)} %get-tuple-element.11.refs_0_.scores_ref, f32[1,2048]{1,0:T(1,128)S(1)} %rows.2.refs_1_, f32[1,2048]{1,0:T(1,128)S(1)} %collective-permute-done.4.refs_2_, f32[1,2048]{1,0:T(1,128)S(1)} %collective-permute-done.5.refs_3_, ...), custom_call_target="tpu_custom_call" | custom-call | tf_op jit(solution)/shard_map/cols/pallas_call | solution.py:313
  52.7 1.2 collective-permute-done.7
  53.9 0.1 broadcast_in_dim.19
  53.9 14.1 %all_to_all.21.refs_1_ = f32[32,1,1024]{2,1,0:T(1,128)S(1)} all-to-all(f32[32,1,1024]{2,1,0:T(1,128)S(1)} %broadcast_in_dim.19), channel_id=1, replica_groups={{0,8,16,24,32,40,48,56,64,72,80,88,96,104,112,120,128,136,144,152,160,1..., dimensions={0} | all-to-all | bytes 262144 | tf_op jit(solution)/shard_map/all_to_all | solution.py:35
  68.0 2.0 %rows.3.refs_1_ = f32[1,2048]{1,0:T(1,128)S(1)} custom-call(f32[1024,2048]{1,0:T(8,128)S(1)} %get-tuple-element.11.refs_0_.scores_ref, f32[32,1,1024]{2,1,0:T(1,128)S(1)} %all_to_all.21.refs_1_), custom_call_target="tpu_custom_call" | custom-call | tf_op jit(solution)/shard_map/rows/pallas_call | solution.py:313
  70.0 1.4 collective-permute-start.10
  71.4 0.7 collective-permute-start.8
  72.1 1.5 collective-permute-start.9
  73.6 0.1 collective-permute-done.10.refs_4_
  73.8 2.5 %collective-permute-done.8.refs_2_ = f32[1,2048]{1,0:T(1,128)S(1)} collective-permute-done((f32[1,2048]{1,0:T(1,128)S(1)}, f32[1,2048]{1,0:T(1,128)S(1)}, u32[]{:S(2)}, u32[]{:S(2)}) %collective-permute-start.8) | collective-permute-done | bytes 8224 | tf_op jit(solution)/shard_map/ppermute | solution.py:45
  76.3 1.0 collective-permute-done.9.refs_3_
  77.3 2.5 %give.1 = (f32[512,896]{1,0:T(8,128)S(1)}, f32[1,2048]{1,0:T(1,128)S(1)}) custom-call(f32[1024,2048]{1,0:T(8,128)S(1)} %get-tuple-element.11.refs_0_.scores_ref, f32[1,2048]{1,0:T(1,128)S(1)} %rows.3.refs_1_, f32[1,2048]{1,0:T(1,128)S(1)} %collective-permute-done.8.refs_2_, f32[1,2048]{1,0:T(1,128)S(1)} %collective-permute-done.9.refs_3_, ...), custom_call_target="tpu_custom_call" | custom-call | tf_op jit(solution)/shard_map/give/pallas_call | solution.py:313
  79.8 0.1 collective-permute-start.11
  79.9 2.5 %keep.1.mine_ref = f32[512,896]{1,0:T(8,128)S(1)} custom-call(f32[1024,2048]{1,0:T(8,128)S(1)} %get-tuple-element.11.refs_0_.scores_ref, f32[1,2048]{1,0:T(1,128)S(1)} %get-tuple-element.15.row_ref.refs_1_, bf16[2048,768]{1,0:T(8,128)(2,1)S(1)} %copy-done), custom_call_target="tpu_custom_call" | custom-call | tf_op jit(solution)/shard_map/keep/pallas_call | solution.py:313
  82.4 1.3 collective-permute-done.11.theirs_ref
  83.7 0.6 join.1
  84.3 29.2 %all_to_all.22.refs_0_ = bf16[32,104,128]{2,1,0:T(8,128)(2,1)S(1)} all-to-all(bf16[32,104,128]{2,1,0:T(8,128)(2,1)S(1)} %join.1), channel_id=1, replica_groups={{0,8,16,24,32,40,48,56,64,72,80,88,96,104,112,120,128,136,144,152,160,1..., dimensions={0} | all-to-all | bytes 1703936 | tf_op jit(solution)/shard_map/all_to_all | solution.py:35
  113.4 1.1 own.1
  114.5 28.3 %all_to_all.23.refs_3_ = bf16[32,104,128]{2,1,0:T(8,128)(2,1)S(1)} all-to-all(bf16[32,104,128]{2,1,0:T(8,128)(2,1)S(1)} %get-tuple-element.19), channel_id=1, replica_groups={{0,8,16,24,32,40,48,56,64,72,80,88,96,104,112,120,128,136,144,152,160,1..., dimensions={0} | all-to-all | bytes 1703936 | tf_op jit(solution)/shard_map/all_to_all | solution.py:35
  142.8 2.4 %terms.2 = f32[2,2048]{1,0:T(2,128)S(1)} custom-call(f32[1024,2048]{1,0:T(8,128)S(1)} %get-tuple-element.11.refs_0_.scores_ref, f32[1,2048]{1,0:T(1,128)S(1)} %get-tuple-element.15.row_ref.refs_1_, bf16[768,2048]{1,0:T(8,128)(2,1)S(1)} %get-tuple-element.18.refs_2_, bf16[32,104,128]{2,1,0:T(8,128)(2,1)S(1)} %all_to_all.23.refs_3_), custom_call_target="tpu_custom_call" | custom-call | tf_op jit(solution)/shard_map/terms/pallas_call | solution.py:313
  145.2 0.0 collective-permute-done.12.refs_3_
  145.2 2.3 %terms.3 = f32[2,2048]{1,0:T(2,128)S(1)} custom-call(f32[1024,2048]{1,0:T(8,128)S(1)} %get-tuple-element.11.refs_0_.scores_ref, f32[1,2048]{1,0:T(1,128)S(1)} %get-tuple-element.15.row_ref.refs_1_, bf16[768,2048]{1,0:T(8,128)(2,1)S(1)} %get-tuple-element.18.refs_2_, bf16[32,104,128]{2,1,0:T(8,128)(2,1)S(1)} %collective-permute-done.12.refs_3_), custom_call_target="tpu_custom_call" | custom-call | tf_op jit(solution)/shard_map/terms/pallas_call | solution.py:313
  147.6 1.6 %collective-permute-start.13 = (f32[2,2048]{1,0:T(2,128)S(1)}, f32[2,2048]{1,0:T(2,128)S(1)}, u32[]{:S(2)}, u32[]{:S(2)}) collective-permute-start(f32[2,2048]{1,0:T(2,128)S(1)} %add.33), channel_id=1, source_target_pairs={{0,2},{1,3},{2,0},{3,1},{4,6},{5,7},{6,4},{7,5},{8,10},{9,11},{10,... | collective-permute-start | bytes 49160 | tf_op jit(solution)/shard_map/ppermute | solution.py:45
  149.2 1.9 %collective-permute-start.14 = (f32[2,2048]{1,0:T(2,128)S(1)}, f32[2,2048]{1,0:T(2,128)S(1)}, u32[]{:S(2)}, u32[]{:S(2)}) collective-permute-start(f32[2,2048]{1,0:T(2,128)S(1)} %add.33), channel_id=1, source_target_pairs={{0,1},{1,2},{2,3},{3,0},{4,5},{5,6},{6,7},{7,4},{8,9},{9,10},{10,1... | collective-permute-start | bytes 49160 | tf_op jit(solution)/shard_map/ppermute | solution.py:45
  151.1 1.4 collective-permute-start.15
  152.4 0.5 collective-permute-done.13
  153.0 1.2 collective-permute-done.14
  154.2 0.7 collective-permute-done.15
  154.8 0.6 fusion
  (12 shorter events, 0.1 us)
Async XLA Ops:
  0.6 1.9 %copy-start = (bf16[2048,768]{1,0:T(8,128)(2,1)S(1)}, bf16[2048,768]{1,0:T(8,128)(2,1)}, u32[]{:S(2)}) copy-start(bf16[2048,768]{1,0:T(8,128)(2,1)} %points_ref.1) | copy-start | bytes 9437188
  2.5 1.4 copy-start.1
  8.8 5.9 %collective-permute-start = (f32[1,2048]{1,0:T(1,128)S(1)}, f32[1,2048]{1,0:T(1,128)S(1)}, u32[]{:S(2)}, u32[]{:S(2)}) collective-permute-start(f32[1,2048]{1,0:T(1,128)S(1)} %get-tuple-element.12.refs_1_), channel_id=1, source_target_pairs={{0,1},{1,2},{2,3},{3,0},{4,5},{5,6},{6,7},{7,4},{8,9},{9,10},{10,1... | collective-permute-start | bytes 24584 | tf_op jit(solution)/shard_map/ppermute | solution.py:45
  10.5 5.2 %collective-permute-start.1 = (f32[1,2048]{1,0:T(1,128)S(1)}, f32[1,2048]{1,0:T(1,128)S(1)}, u32[]{:S(2)}, u32[]{:S(2)}) collective-permute-start(f32[1,2048]{1,0:T(1,128)S(1)} %get-tuple-element.12.refs_1_), channel_id=1, source_target_pairs={{0,2},{1,3},{2,0},{3,1},{4,6},{5,7},{6,4},{7,5},{8,10},{9,11},{10,... | collective-permute-start | bytes 24584 | tf_op jit(solution)/shard_map/ppermute | solution.py:45
  13.4 3.7 %collective-permute-start.2 = (f32[1,2048]{1,0:T(1,128)S(1)}, f32[1,2048]{1,0:T(1,128)S(1)}, u32[]{:S(2)}, u32[]{:S(2)}) collective-permute-start(f32[1,2048]{1,0:T(1,128)S(1)} %get-tuple-element.12.refs_1_), channel_id=1, source_target_pairs={{0,3},{1,0},{2,1},{3,2},{4,7},{5,4},{6,5},{7,6},{8,11},{9,8},{10,9... | collective-permute-start | bytes 24584 | tf_op jit(solution)/shard_map/ppermute | solution.py:45
  19.1 1.2 collective-permute-start.3
  42.9 4.9 %collective-permute-start.4 = (f32[1,2048]{1,0:T(1,128)S(1)}, f32[1,2048]{1,0:T(1,128)S(1)}, u32[]{:S(2)}, u32[]{:S(2)}) collective-permute-start(f32[1,2048]{1,0:T(1,128)S(1)} %rows.2.refs_1_), channel_id=1, source_target_pairs={{0,1},{1,2},{2,3},{3,0},{4,5},{5,6},{6,7},{7,4},{8,9},{9,10},{10,1... | collective-permute-start | bytes 24584 | tf_op jit(solution)/shard_map/ppermute | solution.py:45
  43.1 5.6 %collective-permute-start.5 = (f32[1,2048]{1,0:T(1,128)S(1)}, f32[1,2048]{1,0:T(1,128)S(1)}, u32[]{:S(2)}, u32[]{:S(2)}) collective-permute-start(f32[1,2048]{1,0:T(1,128)S(1)} %rows.2.refs_1_), channel_id=1, source_target_pairs={{0,2},{1,3},{2,0},{3,1},{4,6},{5,7},{6,4},{7,5},{8,10},{9,11},{10,... | collective-permute-start | bytes 24584 | tf_op jit(solution)/shard_map/ppermute | solution.py:45
  47.0 3.7 %collective-permute-start.6 = (f32[1,2048]{1,0:T(1,128)S(1)}, f32[1,2048]{1,0:T(1,128)S(1)}, u32[]{:S(2)}, u32[]{:S(2)}) collective-permute-start(f32[1,2048]{1,0:T(1,128)S(1)} %rows.2.refs_1_), channel_id=1, source_target_pairs={{0,3},{1,0},{2,1},{3,2},{4,7},{5,4},{6,5},{7,6},{8,11},{9,8},{10,9... | collective-permute-start | bytes 24584 | tf_op jit(solution)/shard_map/ppermute | solution.py:45
  52.7 1.2 collective-permute-start.7
  70.0 3.7 %collective-permute-start.10 = (f32[1,2048]{1,0:T(1,128)S(1)}, f32[1,2048]{1,0:T(1,128)S(1)}, u32[]{:S(2)}, u32[]{:S(2)}) collective-permute-start(f32[1,2048]{1,0:T(1,128)S(1)} %rows.3.refs_1_), channel_id=1, source_target_pairs={{0,3},{1,0},{2,1},{3,2},{4,7},{5,4},{6,5},{7,6},{8,11},{9,8},{10,9... | collective-permute-start | bytes 24584 | tf_op jit(solution)/shard_map/ppermute | solution.py:45
  71.4 4.9 %collective-permute-start.8 = (f32[1,2048]{1,0:T(1,128)S(1)}, f32[1,2048]{1,0:T(1,128)S(1)}, u32[]{:S(2)}, u32[]{:S(2)}) collective-permute-start(f32[1,2048]{1,0:T(1,128)S(1)} %rows.3.refs_1_), channel_id=1, source_target_pairs={{0,1},{1,2},{2,3},{3,0},{4,5},{5,6},{6,7},{7,4},{8,9},{9,10},{10,1... | collective-permute-start | bytes 24584 | tf_op jit(solution)/shard_map/ppermute | solution.py:45
  72.1 5.2 %collective-permute-start.9 = (f32[1,2048]{1,0:T(1,128)S(1)}, f32[1,2048]{1,0:T(1,128)S(1)}, u32[]{:S(2)}, u32[]{:S(2)}) collective-permute-start(f32[1,2048]{1,0:T(1,128)S(1)} %rows.3.refs_1_), channel_id=1, source_target_pairs={{0,2},{1,3},{2,0},{3,1},{4,6},{5,7},{6,4},{7,5},{8,10},{9,11},{10,... | collective-permute-start | bytes 24584 | tf_op jit(solution)/shard_map/ppermute | solution.py:45
  79.8 3.9 %collective-permute-start.11 = (f32[512,896]{1,0:T(8,128)S(1)}, f32[512,896]{1,0:T(8,128)S(1)}, u32[]{:S(2)}, u32[]{:S(2)}) collective-permute-start(f32[512,896]{1,0:T(8,128)S(1)} %get-tuple-element.16), channel_id=1, source_target_pairs={{0,4},{4,0},{8,12},{12,8},{16,20},{20,16},{24,28},{28,24},{32,36},... | collective-permute-start | bytes 5505032 | tf_op jit(solution)/shard_map/ppermute | solution.py:26
  142.8 2.4 %collective-permute-start.12 = (bf16[32,104,128]{2,1,0:T(8,128)(2,1)S(1)}, bf16[32,104,128]{2,1,0:T(8,128)(2,1)S(1)}, u32[]{:S(2)}, u32[]{:S(2)}) collective-permute-start(bf16[32,104,128]{2,1,0:T(8,128)(2,1)S(1)} %all_to_all.23.refs_3_), channel_id=1, source_target_pairs={{0,4},{4,0},{8,12},{12,8},{16,20},{20,16},{24,28},{28,24},{32,36},... | collective-permute-start | bytes 2555912 | tf_op jit(solution)/shard_map/ppermute | solution.py:26
  147.6 5.4 %collective-permute-start.13 = (f32[2,2048]{1,0:T(2,128)S(1)}, f32[2,2048]{1,0:T(2,128)S(1)}, u32[]{:S(2)}, u32[]{:S(2)}) collective-permute-start(f32[2,2048]{1,0:T(2,128)S(1)} %add.33), channel_id=1, source_target_pairs={{0,2},{1,3},{2,0},{3,1},{4,6},{5,7},{6,4},{7,5},{8,10},{9,11},{10,... | collective-permute-start | bytes 49160 | tf_op jit(solution)/shard_map/ppermute | solution.py:45
  149.2 4.9 %collective-permute-start.14 = (f32[2,2048]{1,0:T(2,128)S(1)}, f32[2,2048]{1,0:T(2,128)S(1)}, u32[]{:S(2)}, u32[]{:S(2)}) collective-permute-start(f32[2,2048]{1,0:T(2,128)S(1)} %add.33), channel_id=1, source_target_pairs={{0,1},{1,2},{2,3},{3,0},{4,5},{5,6},{6,7},{7,4},{8,9},{9,10},{10,1... | collective-permute-start | bytes 49160 | tf_op jit(solution)/shard_map/ppermute | solution.py:45
  151.1 3.7 %collective-permute-start.15 = (f32[2,2048]{1,0:T(2,128)S(1)}, f32[2,2048]{1,0:T(2,128)S(1)}, u32[]{:S(2)}, u32[]{:S(2)}) collective-permute-start(f32[2,2048]{1,0:T(2,128)S(1)} %add.33), channel_id=1, source_target_pairs={{0,3},{1,0},{2,1},{3,2},{4,7},{5,4},{6,5},{7,6},{8,11},{9,8},{10,9... | collective-permute-start | bytes 49160 | tf_op jit(solution)/shard_map/ppermute | solution.py:45

commit v5 on v4

--- a/solution.py
+++ b/solution.py
@@ -12,7 +12,8 @@
 
 sharpness = 4.0
 LOG2E = math.log2(math.e)
-C = 2
+X, C = 4, 2
+PARITIES = 2
 LANES = 128
 SUB = 8
 GROUP = 128
@@ -21,23 +22,37 @@
 BF16 = jnp.bfloat16
 
 
+def place(z, x, core):
+    return (z * X + x) * C + core
+
+
+def partner(value, mask):
+    size = lax.axis_size("pts")
+    return lax.ppermute(value, "pts", [(i, i ^ mask) for i in range(size)])
+
+
 def other_core(value):
-    size = lax.axis_size("pts")
-    return lax.ppermute(value, "pts", [(i, i ^ 1) for i in range(size)])
-
-
-def chip_groups():
-    size = lax.axis_size("pts")
-    return [[chip * C + core for chip in range(size // C)] for core in range(C)]
-
-
-def exchange(value):
-    return lax.all_to_all(value, "pts", 0, 0, axis_index_groups=chip_groups())
+    return partner(value, 1)
+
+
+def other_parity(value):
+    return partner(value, C)
+
+
+def exchange(value, parities):
+    slabs = lax.axis_size("pts") // (X * C)
+    step = PARITIES // parities
+    groups = [
+        [place(z, x, core) for x in range(parity, X, step) for z in range(slabs)]
+        for parity in range(step)
+        for core in range(C)
+    ]
+    return lax.all_to_all(value, "pts", 0, 0, axis_index_groups=groups)
 
 
 def from_chips(value):
     chips = lax.axis_size("pts") // C
-    return exchange(jnp.broadcast_to(value[None], (chips,) + value.shape))
+    return exchange(jnp.broadcast_to(value[None], (chips,) + value.shape), PARITIES)
 
 
 def cen_shift(value, step):
@@ -90,22 +105,24 @@
 
 
 def score_kernel(
-    core_ref, points_ref, centroids_ref, scores_ref, row_ref, turned_ref, split_ref, *, each
+    sides_ref, points_ref, centroids_ref, scores_ref, row_ref, turned_ref, split_ref, *, each
 ):
     count = points_ref.shape[0]
     rows = centroids_ref.shape[0]
-    core = core_ref[0]
-    blocks = rows // each // C
-
-    def order(j, carry):
-        for part in range(C):
-            side = core if part == 0 else 1 - core
-            start = pl.multiple_of((j * C + side) * each, each)
-            here = pl.multiple_of((part * blocks + j) * each, each)
-            split_ref[pl.ds(here, each), :] = centroids_ref[pl.ds(start, each), :]
+    core, parity = sides_ref[0], sides_ref[1]
+    slabs = rows // (each * X * C)
+
+    def order(z, carry):
+        for n in range(X * C):
+            core_side, parity_side, pair = n // X, n // PARITIES % PARITIES, n % PARITIES
+            to_core = core if core_side == 0 else 1 - core
+            to_parity = parity if parity_side == 0 else 1 - parity
+            start = place(z, pair * PARITIES + to_parity, to_core) * each
+            here = pl.ds(pl.multiple_of((n * slabs + z) * each, each), each)
+            split_ref[here, :] = centroids_ref[pl.ds(pl.multiple_of(start, each), each), :]
         return carry
 
-    lax.fori_loop(0, blocks, order, 0, unroll=4)
+    lax.fori_loop(0, slabs, order, 0, unroll=2)
     chunk = 256
     for first in range(0, count, chunk):
         here = slice(first, first + chunk)
@@ -128,8 +145,17 @@
     return level - (highest + jnp.log2(total))
 
 
-def row_kernel(scores_ref, values_ref, row_ref, cols_ref, top_ref, total_ref, *, level):
-    cols_ref[...] = on_lanes(col_potential(values_ref, level))
+def common_order(sides_ref, row):
+    size = row.shape[1] // (C * PARITIES)
+    quarters = [row[:, n * size : (n + 1) * size] for n in range(C * PARITIES)]
+    swapped = jnp.concatenate([quarters[n ^ 1] for n in range(C * PARITIES)], axis=1)
+    return jnp.where(sides_ref[1] == 0, row, swapped)
+
+
+def row_kernel(
+    sides_ref, scores_ref, values_ref, row_ref, cols_ref, top_ref, total_ref, *, level
+):
+    cols_ref[...] = on_lanes(common_order(sides_ref, col_potential(values_ref, level)))
     for group in range(scores_ref.shape[0] // GROUP):
         cols = [
             cols_ref.at[pl.ds(group * GROUP + SUB * j, SUB), :] for j in range(GROUP // SUB)
@@ -147,7 +173,7 @@
 
 
 def col_kernel(
-    scores_ref, own_ref, one_ref, two_ref, three_ref, col_ref, row_ref, top_ref, total_ref, *, level
+    sides_ref, scores_ref, own_ref, one_ref, two_ref, three_ref, col_ref, row_ref, top_ref, total_ref, *, level
 ):
     row_ref[...] = row_potential(own_ref, one_ref, two_ref, three_ref, level)
     rows, count = scores_ref.shape
@@ -161,15 +187,16 @@
         return carry
 
     lax.fori_loop(0, rows // SUB, step, 0, unroll=UNROLL)
-    col_ref[...] = close(top_ref[...].T, total_ref[...].T)
-
-
-def sums_of(scores_ref, row_ref, points_ref, sums_ref, half):
+    col = close(top_ref[...].T, total_ref[...].T)
+    col_ref[...] = common_order(sides_ref, col)
+
+
+def sums_of(scores_ref, row_ref, points_ref, sums_ref, part):
     rows = sums_ref.shape[0]
     width = points_ref.shape[1]
     for first in range(0, rows, GROUP):
         here = slice(first, first + GROUP)
-        far = slice(half * rows + first, half * rows + first + GROUP)
+        far = slice(part * rows + first, part * rows + first + GROUP)
         shifted = scores_ref[far, :] + row_ref[...]
         top = jnp.max(shifted, axis=1, keepdims=True)
         weights = jnp.exp2(shifted - top)
@@ -184,15 +211,15 @@
         sums_ref[here, width:] = jnp.where(lane < LANES // 2, top, total)
 
 
-def give_kernel(
-    scores_ref, own_ref, one_ref, two_ref, three_ref, points_ref, sums_ref, row_ref, *, level
+def first_sums_kernel(
+    scores_ref, own_ref, one_ref, two_ref, three_ref, points_ref, sums_ref, row_ref, *, part, level
 ):
     row_ref[...] = row_potential(own_ref, one_ref, two_ref, three_ref, level)
-    sums_of(scores_ref, row_ref, points_ref, sums_ref, 1)
-
-
-def keep_kernel(scores_ref, row_ref, points_ref, sums_ref):
-    sums_of(scores_ref, row_ref, points_ref, sums_ref, 0)
+    sums_of(scores_ref, row_ref, points_ref, sums_ref, part)
+
+
+def sums_kernel(scores_ref, row_ref, points_ref, sums_ref, *, part):
+    sums_of(scores_ref, row_ref, points_ref, sums_ref, part)
 
 
 def thirds(value):
@@ -225,28 +252,38 @@
     return jnp.concatenate(halves, axis=1)
 
 
-def join_kernel(mine_ref, theirs_ref, pieces_ref):
-    width = mine_ref.shape[1] - LANES
+def join_kernel(mine_ref, theirs_ref, *refs):
+    *near_ref, pieces_ref = refs
+    rows, width = mine_ref.shape
+    width = width - LANES
     chips = pieces_ref.shape[0]
-    each = mine_ref.shape[0] // chips
-    lane = lax.broadcasted_iota(jnp.int32, (mine_ref.shape[0], LANES), 1)
+    each = rows // chips
+    blocks = width // LANES
+    lane = lax.broadcasted_iota(jnp.int32, (rows, LANES), 1)
     tops, totals = [], []
     for ref in (mine_ref, theirs_ref):
         straight = ref[:, width:]
         swapped = pltpu.roll(straight, SPAN, 1)
         tops.append(jnp.where(lane < SPAN, straight, swapped))
         totals.append(jnp.where(lane < SPAN, swapped, straight))
-    top = jnp.maximum(*tops)
+    for ref in near_ref:
+        tiles = ref[:, blocks * each :, :].astype(F32)
+        for n, columns in enumerate((tops, totals)):
+            column = info_column(tiles, n).reshape(rows, 1)
+            columns.append(jnp.broadcast_to(column, (rows, LANES)))
+    top = tree(tops, jnp.maximum)
     scales = [jnp.exp2(t - top) for t in tops]
-    total = totals[0] * scales[0] + totals[1] * scales[1]
-    for b in range(width // LANES):
+    total = tree([t * scale for t, scale in zip(totals, scales)], jnp.add)
+    for b in range(blocks):
         lanes = slice(b * LANES, (b + 1) * LANES)
-        both = mine_ref[:, lanes] * scales[0] + theirs_ref[:, lanes] * scales[1]
         here = slice(b * each, (b + 1) * each)
-        pieces_ref[:, here, :] = both.astype(BF16).reshape(chips, each, LANES)
+        parts = [mine_ref[:, lanes], theirs_ref[:, lanes]]
+        parts += [ref[:, here, :].astype(F32).reshape(rows, LANES) for ref in near_ref]
+        joined = tree([part * scale for part, scale in zip(parts, scales)], jnp.add)
+        pieces_ref[:, here, :] = joined.astype(BF16).reshape(chips, each, LANES)
     shape = (chips, each, LANES)
     tiles = info_tiles([top.reshape(shape), total.reshape(shape)])
-    pieces_ref[:, width // LANES * each :, :] = tiles
+    pieces_ref[:, blocks * each :, :] = tiles
 
 
 def own_kernel(pieces_ref, own_ref, fresh_ref, *, level):
@@ -273,7 +310,7 @@
         fresh_ref[chip, blocks * each :, :] = info
 
 
-def distance_kernel(scores_ref, row_ref, turned_ref, fresh_ref, both_ref, *, half):
+def distance_kernel(scores_ref, row_ref, turned_ref, fresh_ref, both_ref, *, part):
     chips = fresh_ref.shape[0]
     width, count = turned_ref.shape
     blocks = width // LANES
@@ -296,7 +333,7 @@
         cross = lax.dot_general(
             fresh, turned_ref[...], (((1,), (0,)), ((), ())), preferred_element_type=F32
         )
-        first = (half * chips + chip) * each
+        first = (part * chips + chip) * each
         plan = jnp.exp2((scores_ref[first : first + GROUP, :] + row_ref[...]) + col)
         term = plan * (squares - 2.0 * cross)
         numerator = numerator + jnp.sum(term.reshape(GROUP // SUB, SUB, count), axis=0)
@@ -309,7 +346,7 @@
 SCALAR = pl.BlockSpec(memory_space=pltpu.SMEM)
 
 
-def call(kernel, outs, scratch, args, name, limit=24):
+def call(kernel, outs, scratch, args, limit=24):
     return pl.pallas_call(
         kernel,
         out_shape=[jax.ShapeDtypeStruct(shape, dtype) for shape, dtype in outs],
@@ -317,83 +354,90 @@
         out_specs=[VMEM] * len(outs),
         scratch_shapes=[pltpu.VMEM(shape, dtype) for shape, dtype in scratch],
         compiler_params=pltpu.CompilerParams(vmem_limit_bytes=limit << 20),
-        name=name,
     )(*args)
 
 
 def on_device(points, centroids):
     chips = lax.axis_size("pts") // C
-    core = lax.axis_index("pts") % C
+    here = lax.axis_index("pts")
+    sides = jnp.stack([here % C, here // C % PARITIES]).astype(jnp.int32)
     count, width = points.shape
     rows = centroids.shape[0]
-    half = rows // C
+    parts = C * PARITIES
     each = rows // (chips * C)
-    total_centroids = rows * lax.axis_size("cen")
     row_level = -math.log2(count * chips * C)
-    col_level = -math.log2(total_centroids)
+    col_level = -math.log2(rows * lax.axis_size("cen"))
 
     pairs = [((rows // GROUP * SUB, count), F32)] * 2
     strip = ((rows, LANES), F32)
     line = ((1, count), F32)
 
-    scores, part, turned = call(
+    scores, partial, turned = call(
         lambda *refs: score_kernel(*refs, each=each),
         [((rows, count), F32), line, ((width, count), BF16)],
         [((rows, width), BF16)],
-        [core.astype(jnp.int32).reshape(1), points, centroids],
-        "scores",
+        [sides, points, centroids],
     )
     for iteration in range(ITERS):
         if iteration:
-            (part,) = call(
+            (partial,) = call(
                 lambda *refs: row_kernel(*refs, level=col_level),
                 [line],
                 [strip] + pairs,
-                [scores, values],
-                "rows",
+                [sides, scores, values],
             )
-        partial = [part] + [cen_shift(part, step) for step in (1, 2, 3)]
+        lines = [partial] + [cen_shift(partial, step) for step in (1, 2, 3)]
         if iteration < ITERS - 1:
             col, row = call(
                 lambda *refs: col_kernel(*refs, level=row_level),
                 [((1, rows), F32), line],
                 [strip] * 2,
-                [scores] + partial,
-                "cols",
+                [sides, scores] + lines,
             )
             values = spread_cols(col)
 
-    wide = ((half, width + LANES), F32)
-    piece = ((chips, each * width // LANES + SUB, LANES), BF16)
-    give, row = call(
-        lambda *refs: give_kernel(*refs, level=row_level),
+    wide = ((rows // parts, width + LANES), F32)
+    piece = ((chips // PARITIES, each * width // LANES + SUB, LANES), BF16)
+
+    def sums(part):
+        return call(
+            lambda *refs: sums_kernel(*refs, part=part), [wide], [], [scores, row, points]
+        )[0]
+
+    def join(*args):
+        return call(join_kernel, [piece], [], list(args))[0]
+
+    first, row = call(
+        lambda *refs: first_sums_kernel(*refs, part=3, level=row_level),
         [wide, line],
         [],
-        [scores] + partial + [points],
-        "give",
+        [scores] + lines + [points],
     )
-    theirs = other_core(give)
-    (keep,) = call(keep_kernel, [wide], [], [scores, row, points], "keep")
-    (pieces,) = call(join_kernel, [piece], [], [keep, theirs], "join")
+    theirs = other_core(first)
+    near = other_parity(join(sums(1), theirs))
+    theirs = other_core(sums(2))
+    pieces = exchange(join(sums(0), theirs, near), 1)
     own_rows, fresh = call(
         lambda *refs: own_kernel(*refs, level=col_level),
         [((each, width), BF16), piece],
         [],
-        [exchange(pieces)],
-        "own",
+        [pieces],
     )
-    mine = exchange(fresh)
-    terms = [
-        call(
-            lambda *refs: distance_kernel(*refs, half=part),
+
+    def terms(part, new):
+        return call(
+            lambda *refs: distance_kernel(*refs, part=part),
             [((2, count), F32)],
             [],
             [scores, row, turned, new],
-            "terms",
         )[0]
-        for part, new in enumerate((mine, other_core(mine)))
-    ]
-    both = terms[0] + terms[1]
+
+    mine = exchange(fresh, 1)
+    near = other_parity(mine)
+    theirs = other_core(mine)
+    both = terms(0, mine) + terms(2, theirs)
+    theirs = other_core(near)
+    both = both + (terms(1, near) + terms(3, theirs))
     one, two, three = [cen_shift(both, step) for step in (1, 2, 3)]
     total = (both + two) + (one + three)
     distances = total[0] / total[1] / width
@@ -403,6 +447,7 @@
 def solution(mesh):
     in_specs = (P("pts", None), P("cen", None))
     out_specs = (P(("cen", "pts"), None), P("pts"))
+
     return jax.shard_map(
         on_device, mesh=mesh, in_specs=in_specs, out_specs=out_specs, check_vma=False
     )

time: 156 us -> 159 us (1.019)
  blocking collectives: 92.1 us -> 71.1 us
  waiting for transfers between devices: 15.5 us -> 31 us
  Pallas kernels: 24.3 us -> 28.1 us
  starting transfers between devices: 18.7 us -> 22.2 us
    all_to_all x4, blocking collectives: 92.1 us -> 71.1 us  [exchange(): return lax.all_to_all(value, 'pts', 0, 0, axis_index_groups=groups)]
    ppermute x4 -> x8, waiting for transfers between devices: 3.62 us -> 19.2 us  [partner(): return lax.ppermute(value, 'pts', [(i, i ^ mask) for i in range(size)])]
    pallas_call x11 -> x16, Pallas kernels: 24.3 us -> 28.1 us  [call(): pl.pallas_call(kernel, out_shape=[jax.ShapeDtypeStruct(shape, dtype) for...]
    ppermute x4 -> x8, starting transfers between devices: 0.1 us -> 3.69 us  [partner(): return lax.ppermute(value, 'pts', [(i, i ^ mask) for i in range(size)])]
    unnamed x4 -> x6, local copies, waits for them, and re-layouts: 3.29 us -> 3.3 us
  transfers between devices with their start and end apart: 16 -> 20, of which waited for: 14 -> 15; matrix products, arithmetic and copies ran while one was open for 0% -> 0% of each run, Pallas kernels for 3% -> 5%
where the time goes in v5:
time: 159 us; the launch traced here: 158 us
  blocking collectives  71.1 us (45%)
  waiting for transfers between devices  31 us (19%)
  Pallas kernels  28.1 us (18%)
  starting transfers between devices  22.2 us (14%)
  local copies, waits for them, and re-layouts  3.44 us (2%)
    all_to_all x4, blocking collectives, exchange(): return lax.all_to_all(value, 'pts', 0, 0, axis_index_groups=groups)  71.1 us
    pallas_call x16, Pallas kernels, call(): pl.pallas_call(kernel, out_shape=[jax.ShapeDtypeStruct(shape, dtype) for...  28.1 us
    ppermute x8, waiting for transfers between devices, partner(): return lax.ppermute(value, 'pts', [(i, i ^ mask) for i in range(size)])  19.2 us
    ppermute x12, starting transfers between devices, cen_shift(): lax.ppermute(value, 'cen', [(i, (i + step) % size) for i in range(size)])  18.6 us
    ppermute x12, waiting for transfers between devices, cen_shift(): lax.ppermute(value, 'cen', [(i, (i + step) % size) for i in range(size)])  11.9 us
    ppermute x8, starting transfers between devices, partner(): return lax.ppermute(value, 'pts', [(i, i ^ mask) for i in range(size)])  3.69 us
    unnamed x6, local copies, waits for them, and re-layouts  3.3 us
  transfers between devices with their start and end apart: 20, of which 15 were waited for; matrix products, arithmetic and copies ran while one was open for 0% of the time, Pallas kernels for 5%

profile of v5, /device:TPU:2, one launch (start us, length us, event | category | flops | bytes accessed | tf_op | source)
XLA Modules:
  0.0 157.6 jit_solution(1897350103256348515)
XLA Ops:
  0.7 1.9 %copy-done = bf16[2048,768]{1,0:T(8,128)(2,1)S(1)} copy-done((bf16[2048,768]{1,0:T(8,128)(2,1)S(1)}, bf16[2048,768]{1,0:T(8,128)(2,1)}, u32[]{:S(2)}) %copy-start) | copy-done | bytes 3145752
  2.6 1.4 copy-done.2
  4.0 5.5 %shard_map.41 = (f32[1024,2048]{1,0:T(8,128)S(1)}, f32[1,2048]{1,0:T(1,128)S(1)}, bf16[768,2048]{1,0:T(8,128)(2,1)S(1)}) custom-call(s32[2]{0:T(128)S(1)} %pad_add_fusion.refs_0_, bf16[2048,768]{1,0:T(8,128)(2,1)S(1)} %copy-done, bf16[1024,768]{1,0:T(8,128)(2,1)S(1)} %copy-done.2), custom_call_target="tpu_custom_call" | custom-call | tf_op jit(solution)/shard_map/pallas_call | solution.py:350
  9.5 1.7 %collective-permute-start = (f32[1,2048]{1,0:T(1,128)S(1)}, f32[1,2048]{1,0:T(1,128)S(1)}, u32[]{:S(2)}, u32[]{:S(2)}) collective-permute-start(f32[1,2048]{1,0:T(1,128)S(1)} %get-tuple-element.12.refs_2_), channel_id=1, source_target_pairs={{0,1},{1,2},{2,3},{3,0},{4,5},{5,6},{6,7},{7,4},{8,9},{9,10},{10,1... | collective-permute-start | bytes 24584 | tf_op jit(solution)/shard_map/ppermute | solution.py:60
  11.2 2.9 %collective-permute-start.1 = (f32[1,2048]{1,0:T(1,128)S(1)}, f32[1,2048]{1,0:T(1,128)S(1)}, u32[]{:S(2)}, u32[]{:S(2)}) collective-permute-start(f32[1,2048]{1,0:T(1,128)S(1)} %get-tuple-element.12.refs_2_), channel_id=1, source_target_pairs={{0,2},{1,3},{2,0},{3,1},{4,6},{5,7},{6,4},{7,5},{8,10},{9,11},{10,... | collective-permute-start | bytes 24584 | tf_op jit(solution)/shard_map/ppermute | solution.py:60
  14.1 1.3 collective-permute-start.2
  15.4 0.9 collective-permute-done.1.refs_4_
  16.3 1.4 collective-permute-done.2.refs_5_
  17.7 2.7 %shard_map.42 = (f32[1,1024]{1,0:T(1,128)S(1)}, f32[1,2048]{1,0:T(1,128)}) custom-call(s32[2]{0:T(128)S(1)} %pad_add_fusion.refs_0_, f32[1024,2048]{1,0:T(8,128)S(1)} %get-tuple-element.11.refs_1_.refs_0_, f32[1,2048]{1,0:T(1,128)S(1)} %get-tuple-element.12.refs_2_, f32[1,2048]{1,0:T(1,128)S(1)} %collective-permute-done.refs_3_, ...), custom_call_target="tpu_custom_call" | custom-call | tf_op jit(solution)/shard_map/pallas_call | solution.py:350
  20.4 1.2 collective-permute-done.3
  21.7 20.9 %all_to_all.20.refs_2_ = f32[32,1,1024]{2,1,0:T(1,128)S(1)} all-to-all(f32[32,1,1024]{2,1,0:T(1,128)S(1)} %broadcast_in_dim.17), channel_id=1, replica_groups={{0,32,64,96,128,160,192,224,8,40,72,104,136,168,200,232,16,48,80,112,14..., dimensions={0} | all-to-all | bytes 262144 | tf_op jit(solution)/shard_map/all_to_all | solution.py:50
  42.5 2.5 %shard_map.43.refs_2_ = f32[1,2048]{1,0:T(1,128)S(1)} custom-call(s32[2]{0:T(128)S(1)} %pad_add_fusion.refs_0_, f32[1024,2048]{1,0:T(8,128)S(1)} %get-tuple-element.11.refs_1_.refs_0_, f32[32,1,1024]{2,1,0:T(1,128)S(1)} %all_to_all.20.refs_2_), custom_call_target="tpu_custom_call" | custom-call | tf_op jit(solution)/shard_map/pallas_call | solution.py:350
  45.3 3.8 %collective-permute-start.5 = (f32[1,2048]{1,0:T(1,128)S(1)}, f32[1,2048]{1,0:T(1,128)S(1)}, u32[]{:S(2)}, u32[]{:S(2)}) collective-permute-start(f32[1,2048]{1,0:T(1,128)S(1)} %shard_map.43.refs_2_), channel_id=1, source_target_pairs={{0,2},{1,3},{2,0},{3,1},{4,6},{5,7},{6,4},{7,5},{8,10},{9,11},{10,... | collective-permute-start | bytes 24584 | tf_op jit(solution)/shard_map/ppermute | solution.py:60
  49.3 0.7 collective-permute-done.4.refs_3_
  50.0 0.9 collective-permute-done.5.refs_4_
  50.9 1.9 %collective-permute-done.6.refs_5_ = f32[1,2048]{1,0:T(1,128)S(1)} collective-permute-done((f32[1,2048]{1,0:T(1,128)S(1)}, f32[1,2048]{1,0:T(1,128)S(1)}, u32[]{:S(2)}, u32[]{:S(2)}) %collective-permute-start.6) | collective-permute-done | bytes 8224 | tf_op jit(solution)/shard_map/ppermute | solution.py:60
  52.8 2.7 %shard_map.44 = (f32[1,1024]{1,0:T(1,128)S(1)}, f32[1,2048]{1,0:T(1,128)}) custom-call(s32[2]{0:T(128)S(1)} %pad_add_fusion.refs_0_, f32[1024,2048]{1,0:T(8,128)S(1)} %get-tuple-element.11.refs_1_.refs_0_, f32[1,2048]{1,0:T(1,128)S(1)} %shard_map.43.refs_2_, f32[1,2048]{1,0:T(1,128)S(1)} %collective-permute-done.4.refs_3_, ...), custom_call_target="tpu_custom_call" | custom-call | tf_op jit(solution)/shard_map/pallas_call | solution.py:350
  55.5 1.2 collective-permute-done.7
  56.8 14.2 %all_to_all.21.refs_2_ = f32[32,1,1024]{2,1,0:T(1,128)S(1)} all-to-all(f32[32,1,1024]{2,1,0:T(1,128)S(1)} %broadcast_in_dim.19), channel_id=1, replica_groups={{0,32,64,96,128,160,192,224,8,40,72,104,136,168,200,232,16,48,80,112,14..., dimensions={0} | all-to-all | bytes 262144 | tf_op jit(solution)/shard_map/all_to_all | solution.py:50
  70.9 2.5 %shard_map.45.refs_1_ = f32[1,2048]{1,0:T(1,128)S(1)} custom-call(s32[2]{0:T(128)S(1)} %pad_add_fusion.refs_0_, f32[1024,2048]{1,0:T(8,128)S(1)} %get-tuple-element.11.refs_1_.refs_0_, f32[32,1,1024]{2,1,0:T(1,128)S(1)} %all_to_all.21.refs_2_), custom_call_target="tpu_custom_call" | custom-call | tf_op jit(solution)/shard_map/pallas_call | solution.py:350
  73.4 1.4 collective-permute-start.10
  74.8 0.7 collective-permute-start.8
  75.5 1.5 collective-permute-start.9
  77.2 2.5 %collective-permute-done.8.refs_2_ = f32[1,2048]{1,0:T(1,128)S(1)} collective-permute-done((f32[1,2048]{1,0:T(1,128)S(1)}, f32[1,2048]{1,0:T(1,128)S(1)}, u32[]{:S(2)}, u32[]{:S(2)}) %collective-permute-start.8) | collective-permute-done | bytes 8224 | tf_op jit(solution)/shard_map/ppermute | solution.py:60
  79.7 1.0 collective-permute-done.9.refs_3_
  80.7 1.4 shard_map.46
  82.2 1.3 shard_map.48
  83.5 0.6 collective-permute-start.11
  84.1 1.3 shard_map.49.mine_ref
  85.8 1.7 %collective-permute-start.13 = (bf16[16,104,128]{2,1,0:T(8,128)(2,1)S(1)}, bf16[16,104,128]{2,1,0:T(8,128)(2,1)S(1)}, u32[]{:S(2)}, u32[]{:S(2)}) collective-permute-start(bf16[16,104,128]{2,1,0:T(8,128)(2,1)S(1)} %shard_map.50), channel_id=1, source_target_pairs={{0,8},{4,12},{8,0},{12,4},{16,24},{20,28},{24,16},{28,20},{32,40},... | collective-permute-start | bytes 1277960 | tf_op jit(solution)/shard_map/ppermute | solution.py:31
  87.5 1.4 shard_map.47.mine_ref
  88.9 8.9 %collective-permute-done.13.refs_0_ = bf16[16,104,128]{2,1,0:T(8,128)(2,1)S(1)} collective-permute-done((bf16[16,104,128]{2,1,0:T(8,128)(2,1)S(1)}, bf16[16,104,128]{2,1,0:T(8,128)(2,1)S(1)}, u32[]{:S(2)}, u32[]{:S(2)}) %collective-permute-start.13) | collective-permute-done | bytes 426016 | tf_op jit(solution)/shard_map/ppermute | solution.py:31
  98.4 17.5 %all_to_all.22.refs_0_ = bf16[16,104,128]{2,1,0:T(8,128)(2,1)S(1)} all-to-all(bf16[16,104,128]{2,1,0:T(8,128)(2,1)S(1)} %shard_map.51), channel_id=1, replica_groups={{0,32,64,96,128,160,192,224,16,48,80,112,144,176,208,240},{4,36,68,100,..., dimensions={0} | all-to-all | bytes 851968 | tf_op jit(solution)/shard_map/all_to_all | solution.py:50
  115.9 0.9 shard_map.52
  116.8 18.6 %all_to_all.23.refs_3_ = bf16[16,104,128]{2,1,0:T(8,128)(2,1)S(1)} all-to-all(bf16[16,104,128]{2,1,0:T(8,128)(2,1)S(1)} %get-tuple-element.19), channel_id=1, replica_groups={{0,32,64,96,128,160,192,224,16,48,80,112,144,176,208,240},{4,36,68,100,..., dimensions={0} | all-to-all | bytes 851968 | tf_op jit(solution)/shard_map/all_to_all | solution.py:50
  135.4 1.3 collective-permute-start.15
  136.7 7.9 %collective-permute-done.15.refs_3_ = bf16[16,104,128]{2,1,0:T(8,128)(2,1)S(1)} collective-permute-done((bf16[16,104,128]{2,1,0:T(8,128)(2,1)S(1)}, bf16[16,104,128]{2,1,0:T(8,128)(2,1)S(1)}, u32[]{:S(2)}, u32[]{:S(2)}) %collective-permute-start.15) | collective-permute-done | bytes 426016 | tf_op jit(solution)/shard_map/ppermute | solution.py:31
  144.6 1.3 shard_map.53
  145.9 1.3 shard_map.55
  147.2 1.3 shard_map.54
  148.5 1.3 shard_map.56
  149.8 1.6 %collective-permute-start.17 = (f32[2,2048]{1,0:T(2,128)S(1)}, f32[2,2048]{1,0:T(2,128)S(1)}, u32[]{:S(2)}, u32[]{:S(2)}) collective-permute-start(f32[2,2048]{1,0:T(2,128)S(1)} %add_add_fusion.1), channel_id=1, source_target_pairs={{0,2},{1,3},{2,0},{3,1},{4,6},{5,7},{6,4},{7,5},{8,10},{9,11},{10,... | collective-permute-start | bytes 49160 | tf_op jit(solution)/shard_map/ppermute | solution.py:60
  151.4 1.9 %collective-permute-start.18 = (f32[2,2048]{1,0:T(2,128)S(1)}, f32[2,2048]{1,0:T(2,128)S(1)}, u32[]{:S(2)}, u32[]{:S(2)}) collective-permute-start(f32[2,2048]{1,0:T(2,128)S(1)} %add_add_fusion.1), channel_id=1, source_target_pairs={{0,1},{1,2},{2,3},{3,0},{4,5},{5,6},{6,7},{7,4},{8,9},{9,10},{10,1... | collective-permute-start | bytes 49160 | tf_op jit(solution)/shard_map/ppermute | solution.py:60
  153.2 1.4 collective-permute-start.19
  154.6 0.6 collective-permute-done.17
  155.2 1.1 collective-permute-done.18
  156.3 0.7 collective-permute-done.19
  157.0 0.6 fusion
  (28 shorter events, 1.8 us)
Async XLA Ops:
  0.7 1.9 %copy-start = (bf16[2048,768]{1,0:T(8,128)(2,1)S(1)}, bf16[2048,768]{1,0:T(8,128)(2,1)}, u32[]{:S(2)}) copy-start(bf16[2048,768]{1,0:T(8,128)(2,1)} %refs_2_.7) | copy-start | bytes 9437188
  2.6 1.4 copy-start.2
  9.5 5.9 %collective-permute-start = (f32[1,2048]{1,0:T(1,128)S(1)}, f32[1,2048]{1,0:T(1,128)S(1)}, u32[]{:S(2)}, u32[]{:S(2)}) collective-permute-start(f32[1,2048]{1,0:T(1,128)S(1)} %get-tuple-element.12.refs_2_), channel_id=1, source_target_pairs={{0,1},{1,2},{2,3},{3,0},{4,5},{5,6},{6,7},{7,4},{8,9},{9,10},{10,1... | collective-permute-start | bytes 24584 | tf_op jit(solution)/shard_map/ppermute | solution.py:60
  11.2 5.2 %collective-permute-start.1 = (f32[1,2048]{1,0:T(1,128)S(1)}, f32[1,2048]{1,0:T(1,128)S(1)}, u32[]{:S(2)}, u32[]{:S(2)}) collective-permute-start(f32[1,2048]{1,0:T(1,128)S(1)} %get-tuple-element.12.refs_2_), channel_id=1, source_target_pairs={{0,2},{1,3},{2,0},{3,1},{4,6},{5,7},{6,4},{7,5},{8,10},{9,11},{10,... | collective-permute-start | bytes 24584 | tf_op jit(solution)/shard_map/ppermute | solution.py:60
  14.1 3.7 %collective-permute-start.2 = (f32[1,2048]{1,0:T(1,128)S(1)}, f32[1,2048]{1,0:T(1,128)S(1)}, u32[]{:S(2)}, u32[]{:S(2)}) collective-permute-start(f32[1,2048]{1,0:T(1,128)S(1)} %get-tuple-element.12.refs_2_), channel_id=1, source_target_pairs={{0,3},{1,0},{2,1},{3,2},{4,7},{5,4},{6,5},{7,6},{8,11},{9,8},{10,9... | collective-permute-start | bytes 24584 | tf_op jit(solution)/shard_map/ppermute | solution.py:60
  20.4 1.2 collective-permute-start.3
  45.1 4.9 %collective-permute-start.4 = (f32[1,2048]{1,0:T(1,128)S(1)}, f32[1,2048]{1,0:T(1,128)S(1)}, u32[]{:S(2)}, u32[]{:S(2)}) collective-permute-start(f32[1,2048]{1,0:T(1,128)S(1)} %shard_map.43.refs_2_), channel_id=1, source_target_pairs={{0,1},{1,2},{2,3},{3,0},{4,5},{5,6},{6,7},{7,4},{8,9},{9,10},{10,1... | collective-permute-start | bytes 24584 | tf_op jit(solution)/shard_map/ppermute | solution.py:60
  45.3 5.6 %collective-permute-start.5 = (f32[1,2048]{1,0:T(1,128)S(1)}, f32[1,2048]{1,0:T(1,128)S(1)}, u32[]{:S(2)}, u32[]{:S(2)}) collective-permute-start(f32[1,2048]{1,0:T(1,128)S(1)} %shard_map.43.refs_2_), channel_id=1, source_target_pairs={{0,2},{1,3},{2,0},{3,1},{4,6},{5,7},{6,4},{7,5},{8,10},{9,11},{10,... | collective-permute-start | bytes 24584 | tf_op jit(solution)/shard_map/ppermute | solution.py:60
  49.2 3.7 %collective-permute-start.6 = (f32[1,2048]{1,0:T(1,128)S(1)}, f32[1,2048]{1,0:T(1,128)S(1)}, u32[]{:S(2)}, u32[]{:S(2)}) collective-permute-start(f32[1,2048]{1,0:T(1,128)S(1)} %shard_map.43.refs_2_), channel_id=1, source_target_pairs={{0,3},{1,0},{2,1},{3,2},{4,7},{5,4},{6,5},{7,6},{8,11},{9,8},{10,9... | collective-permute-start | bytes 24584 | tf_op jit(solution)/shard_map/ppermute | solution.py:60
  55.5 1.2 collective-permute-start.7
  73.4 3.7 %collective-permute-start.10 = (f32[1,2048]{1,0:T(1,128)S(1)}, f32[1,2048]{1,0:T(1,128)S(1)}, u32[]{:S(2)}, u32[]{:S(2)}) collective-permute-start(f32[1,2048]{1,0:T(1,128)S(1)} %shard_map.45.refs_1_), channel_id=1, source_target_pairs={{0,3},{1,0},{2,1},{3,2},{4,7},{5,4},{6,5},{7,6},{8,11},{9,8},{10,9... | collective-permute-start | bytes 24584 | tf_op jit(solution)/shard_map/ppermute | solution.py:60
  74.8 4.9 %collective-permute-start.8 = (f32[1,2048]{1,0:T(1,128)S(1)}, f32[1,2048]{1,0:T(1,128)S(1)}, u32[]{:S(2)}, u32[]{:S(2)}) collective-permute-start(f32[1,2048]{1,0:T(1,128)S(1)} %shard_map.45.refs_1_), channel_id=1, source_target_pairs={{0,1},{1,2},{2,3},{3,0},{4,5},{5,6},{6,7},{7,4},{8,9},{9,10},{10,1... | collective-permute-start | bytes 24584 | tf_op jit(solution)/shard_map/ppermute | solution.py:60
  75.5 5.2 %collective-permute-start.9 = (f32[1,2048]{1,0:T(1,128)S(1)}, f32[1,2048]{1,0:T(1,128)S(1)}, u32[]{:S(2)}, u32[]{:S(2)}) collective-permute-start(f32[1,2048]{1,0:T(1,128)S(1)} %shard_map.45.refs_1_), channel_id=1, source_target_pairs={{0,2},{1,3},{2,0},{3,1},{4,6},{5,7},{6,4},{7,5},{8,10},{9,11},{10,... | collective-permute-start | bytes 24584 | tf_op jit(solution)/shard_map/ppermute | solution.py:60
  82.1 3.4 %collective-permute-start.12 = (f32[256,896]{1,0:T(8,128)S(1)}, f32[256,896]{1,0:T(8,128)S(1)}, u32[]{:S(2)}, u32[]{:S(2)}) collective-permute-start(f32[256,896]{1,0:T(8,128)S(1)} %get-tuple-element.16), channel_id=1, source_target_pairs={{0,4},{4,0},{8,12},{12,8},{16,20},{20,16},{24,28},{28,24},{32,36},... | collective-permute-start | bytes 2752520 | tf_op jit(solution)/shard_map/ppermute | solution.py:31
  83.5 5.4 %collective-permute-start.11 = (f32[256,896]{1,0:T(8,128)S(1)}, f32[256,896]{1,0:T(8,128)S(1)}, u32[]{:S(2)}, u32[]{:S(2)}) collective-permute-start(f32[256,896]{1,0:T(8,128)S(1)} %shard_map.48), channel_id=1, source_target_pairs={{0,4},{4,0},{8,12},{12,8},{16,20},{20,16},{24,28},{28,24},{32,36},... | collective-permute-start | bytes 2752520 | tf_op jit(solution)/shard_map/ppermute | solution.py:31
  84.1 3.4 %copy-start.1 = (bf16[2048,768]{1,0:T(8,128)(2,1)S(1)}, bf16[2048,768]{1,0:T(8,128)(2,1)}, u32[]{:S(2)}) copy-start(bf16[2048,768]{1,0:T(8,128)(2,1)} %refs_2_.7) | copy-start | bytes 9437188
  85.8 12.1 %collective-permute-start.13 = (bf16[16,104,128]{2,1,0:T(8,128)(2,1)S(1)}, bf16[16,104,128]{2,1,0:T(8,128)(2,1)S(1)}, u32[]{:S(2)}, u32[]{:S(2)}) collective-permute-start(bf16[16,104,128]{2,1,0:T(8,128)(2,1)S(1)} %shard_map.50), channel_id=1, source_target_pairs={{0,8},{4,12},{8,0},{12,4},{16,24},{20,28},{24,16},{28,20},{32,40},... | collective-permute-start | bytes 1277960 | tf_op jit(solution)/shard_map/ppermute | solution.py:31
  135.4 9.2 %collective-permute-start.15 = (bf16[16,104,128]{2,1,0:T(8,128)(2,1)S(1)}, bf16[16,104,128]{2,1,0:T(8,128)(2,1)S(1)}, u32[]{:S(2)}, u32[]{:S(2)}) collective-permute-start(bf16[16,104,128]{2,1,0:T(8,128)(2,1)S(1)} %all_to_all.23.refs_3_), channel_id=1, source_target_pairs={{0,8},{4,12},{8,0},{12,4},{16,24},{20,28},{24,16},{28,20},{32,40},... | collective-permute-start | bytes 1277960 | tf_op jit(solution)/shard_map/ppermute | solution.py:31
  136.7 10.5 %collective-permute-start.14 = (bf16[16,104,128]{2,1,0:T(8,128)(2,1)S(1)}, bf16[16,104,128]{2,1,0:T(8,128)(2,1)S(1)}, u32[]{:S(2)}, u32[]{:S(2)}) collective-permute-start(bf16[16,104,128]{2,1,0:T(8,128)(2,1)S(1)} %all_to_all.23.refs_3_), channel_id=1, source_target_pairs={{0,4},{4,0},{8,12},{12,8},{16,20},{20,16},{24,28},{28,24},{32,36},... | collective-permute-start | bytes 1277960 | tf_op jit(solution)/shard_map/ppermute | solution.py:31
  144.6 3.8 %collective-permute-start.16 = (bf16[16,104,128]{2,1,0:T(8,128)(2,1)S(1)}, bf16[16,104,128]{2,1,0:T(8,128)(2,1)S(1)}, u32[]{:S(2)}, u32[]{:S(2)}) collective-permute-start(bf16[16,104,128]{2,1,0:T(8,128)(2,1)S(1)} %collective-permute-done.15.refs_3_), channel_id=1, source_target_pairs={{0,4},{4,0},{8,12},{12,8},{16,20},{20,16},{24,28},{28,24},{32,36},... | collective-permute-start | bytes 1277960 | tf_op jit(solution)/shard_map/ppermute | solution.py:31
  149.8 5.4 %collective-permute-start.17 = (f32[2,2048]{1,0:T(2,128)S(1)}, f32[2,2048]{1,0:T(2,128)S(1)}, u32[]{:S(2)}, u32[]{:S(2)}) collective-permute-start(f32[2,2048]{1,0:T(2,128)S(1)} %add_add_fusion.1), channel_id=1, source_target_pairs={{0,2},{1,3},{2,0},{3,1},{4,6},{5,7},{6,4},{7,5},{8,10},{9,11},{10,... | collective-permute-start | bytes 49160 | tf_op jit(solution)/shard_map/ppermute | solution.py:60
  151.4 4.9 %collective-permute-start.18 = (f32[2,2048]{1,0:T(2,128)S(1)}, f32[2,2048]{1,0:T(2,128)S(1)}, u32[]{:S(2)}, u32[]{:S(2)}) collective-permute-start(f32[2,2048]{1,0:T(2,128)S(1)} %add_add_fusion.1), channel_id=1, source_target_pairs={{0,1},{1,2},{2,3},{3,0},{4,5},{5,6},{6,7},{7,4},{8,9},{9,10},{10,1... | collective-permute-start | bytes 49160 | tf_op jit(solution)/shard_map/ppermute | solution.py:60
  153.2 3.7 %collective-permute-start.19 = (f32[2,2048]{1,0:T(2,128)S(1)}, f32[2,2048]{1,0:T(2,128)S(1)}, u32[]{:S(2)}, u32[]{:S(2)}) collective-permute-start(f32[2,2048]{1,0:T(2,128)S(1)} %add_add_fusion.1), channel_id=1, source_target_pairs={{0,3},{1,0},{2,1},{3,2},{4,7},{5,4},{6,5},{7,6},{8,11},{9,8},{10,9... | collective-permute-start | bytes 49160 | tf_op jit(solution)/shard_map/ppermute | solution.py:60

commit v6 on v5

--- a/solution.py
+++ b/solution.py
@@ -43,7 +43,7 @@
     slabs = lax.axis_size("pts") // (X * C)
     step = PARITIES // parities
     groups = [
-        [place(z, x, core) for x in range(parity, X, step) for z in range(slabs)]
+        [place(z, x, core) for z in range(slabs) for x in range(parity, X, step)]
         for parity in range(step)
         for core in range(C)
     ]
@@ -105,20 +105,22 @@
 
 
 def score_kernel(
-    sides_ref, points_ref, centroids_ref, scores_ref, row_ref, turned_ref, split_ref, *, each
+    points_ref, centroids_ref, scores_ref, row_ref, turned_ref, split_ref, *, each
 ):
     count = points_ref.shape[0]
     rows = centroids_ref.shape[0]
-    core, parity = sides_ref[0], sides_ref[1]
+    core = lax.axis_index("pts") % C
+    parity = lax.axis_index("pts") // C % PARITIES
     slabs = rows // (each * X * C)
 
     def order(z, carry):
         for n in range(X * C):
-            core_side, parity_side, pair = n // X, n // PARITIES % PARITIES, n % PARITIES
-            to_core = core if core_side == 0 else 1 - core
-            to_parity = parity if parity_side == 0 else 1 - parity
+            side, pair = n // (X // PARITIES), n % (X // PARITIES)
+            to_core = core if side // PARITIES == 0 else 1 - core
+            to_parity = parity if side % PARITIES == 0 else 1 - parity
             start = place(z, pair * PARITIES + to_parity, to_core) * each
-            here = pl.ds(pl.multiple_of((n * slabs + z) * each, each), each)
+            block = (side * slabs + z) * (X // PARITIES) + pair
+            here = pl.ds(pl.multiple_of(block * each, each), each)
             split_ref[here, :] = centroids_ref[pl.ds(pl.multiple_of(start, each), each), :]
         return carry
 
@@ -145,17 +147,15 @@
     return level - (highest + jnp.log2(total))
 
 
-def common_order(sides_ref, row):
+def common_order(row):
     size = row.shape[1] // (C * PARITIES)
     quarters = [row[:, n * size : (n + 1) * size] for n in range(C * PARITIES)]
     swapped = jnp.concatenate([quarters[n ^ 1] for n in range(C * PARITIES)], axis=1)
-    return jnp.where(sides_ref[1] == 0, row, swapped)
-
-
-def row_kernel(
-    sides_ref, scores_ref, values_ref, row_ref, cols_ref, top_ref, total_ref, *, level
-):
-    cols_ref[...] = on_lanes(common_order(sides_ref, col_potential(values_ref, level)))
+    return jnp.where(lax.axis_index("pts") // C % PARITIES == 0, row, swapped)
+
+
+def row_kernel(scores_ref, values_ref, row_ref, cols_ref, top_ref, total_ref, *, level):
+    cols_ref[...] = on_lanes(common_order(col_potential(values_ref, level)))
     for group in range(scores_ref.shape[0] // GROUP):
         cols = [
             cols_ref.at[pl.ds(group * GROUP + SUB * j, SUB), :] for j in range(GROUP // SUB)
@@ -173,7 +173,7 @@
 
 
 def col_kernel(
-    sides_ref, scores_ref, own_ref, one_ref, two_ref, three_ref, col_ref, row_ref, top_ref, total_ref, *, level
+    scores_ref, own_ref, one_ref, two_ref, three_ref, col_ref, row_ref, top_ref, total_ref, *, level
 ):
     row_ref[...] = row_potential(own_ref, one_ref, two_ref, three_ref, level)
     rows, count = scores_ref.shape
@@ -188,7 +188,7 @@
 
     lax.fori_loop(0, rows // SUB, step, 0, unroll=UNROLL)
     col = close(top_ref[...].T, total_ref[...].T)
-    col_ref[...] = common_order(sides_ref, col)
+    col_ref[...] = common_order(col)
 
 
 def sums_of(scores_ref, row_ref, points_ref, sums_ref, part):
@@ -343,14 +343,13 @@
 
 
 VMEM = pl.BlockSpec(memory_space=pltpu.VMEM)
-SCALAR = pl.BlockSpec(memory_space=pltpu.SMEM)
 
 
 def call(kernel, outs, scratch, args, limit=24):
     return pl.pallas_call(
         kernel,
         out_shape=[jax.ShapeDtypeStruct(shape, dtype) for shape, dtype in outs],
-        in_specs=[SCALAR if arg.dtype == jnp.int32 else VMEM for arg in args],
+        in_specs=[VMEM] * len(args),
         out_specs=[VMEM] * len(outs),
         scratch_shapes=[pltpu.VMEM(shape, dtype) for shape, dtype in scratch],
         compiler_params=pltpu.CompilerParams(vmem_limit_bytes=limit << 20),
@@ -359,8 +358,6 @@
 
 def on_device(points, centroids):
     chips = lax.axis_size("pts") // C
-    here = lax.axis_index("pts")
-    sides = jnp.stack([here % C, here // C % PARITIES]).astype(jnp.int32)
     count, width = points.shape
     rows = centroids.shape[0]
     parts = C * PARITIES
@@ -376,7 +373,7 @@
         lambda *refs: score_kernel(*refs, each=each),
         [((rows, count), F32), line, ((width, count), BF16)],
         [((rows, width), BF16)],
-        [sides, points, centroids],
+        [points, centroids],
     )
     for iteration in range(ITERS):
         if iteration:
@@ -384,7 +381,7 @@
                 lambda *refs: row_kernel(*refs, level=col_level),
                 [line],
                 [strip] + pairs,
-                [sides, scores, values],
+                [scores, values],
             )
         lines = [partial] + [cen_shift(partial, step) for step in (1, 2, 3)]
         if iteration < ITERS - 1:
@@ -392,7 +389,7 @@
                 lambda *refs: col_kernel(*refs, level=row_level),
                 [((1, rows), F32), line],
                 [strip] * 2,
-                [sides, scores] + lines,
+                [scores] + lines,
             )
             values = spread_cols(col)
 

time: 159 us -> 157 us (0.987)
  Pallas kernels: 28.1 us -> 24.8 us
    pallas_call x16, Pallas kernels: 28.1 us -> 24.8 us  [call(): pl.pallas_call(kernel, out_shape=[jax.ShapeDtypeStruct(shape, dtype) for...]
where the time goes in v6:
time: 157 us; the launch traced here: 155 us
  blocking collectives  72.6 us (46%)
  waiting for transfers between devices  30.2 us (19%)
  Pallas kernels  24.8 us (16%)
  starting transfers between devices  22.8 us (15%)
  local copies, waits for them, and re-layouts  3.44 us (2%)
    all_to_all x4, blocking collectives, exchange(): return lax.all_to_all(value, 'pts', 0, 0, axis_index_groups=groups)  72.6 us
    pallas_call x16, Pallas kernels, call(): pl.pallas_call(kernel, out_shape=[jax.ShapeDtypeStruct(shape, dtype) for...  24.8 us
    ppermute x12, starting transfers between devices, cen_shift(): lax.ppermute(value, 'cen', [(i, (i + step) % size) for i in range(size)])  18.6 us
    ppermute x8, waiting for transfers between devices, partner(): return lax.ppermute(value, 'pts', [(i, i ^ mask) for i in range(size)])  18.4 us
    ppermute x12, waiting for transfers between devices, cen_shift(): lax.ppermute(value, 'cen', [(i, (i + step) % size) for i in range(size)])  11.8 us
    ppermute x8, starting transfers between devices, partner(): return lax.ppermute(value, 'pts', [(i, i ^ mask) for i in range(size)])  4.23 us
    unnamed x6, local copies, waits for them, and re-layouts  3.3 us
  transfers between devices with their start and end apart: 20, of which 15 were waited for; matrix products, arithmetic and copies ran while one was open for 0% of the time, Pallas kernels for 5%

profile of v6, /device:TPU:2, one launch (start us, length us, event | category | flops | bytes accessed | tf_op | source)
XLA Modules:
  0.0 155.4 jit_solution(9640441141970949703)
XLA Ops:
  0.6 1.9 %copy-done = bf16[2048,768]{1,0:T(8,128)(2,1)S(1)} copy-done((bf16[2048,768]{1,0:T(8,128)(2,1)S(1)}, bf16[2048,768]{1,0:T(8,128)(2,1)}, u32[]{:S(2)}) %copy-start) | copy-done | bytes 3145752
  2.5 1.4 copy-done.2
  3.9 4.9 %shard_map.41 = (f32[1024,2048]{1,0:T(8,128)S(1)}, f32[1,2048]{1,0:T(1,128)S(1)}, bf16[768,2048]{1,0:T(8,128)(2,1)S(1)}) custom-call(bf16[2048,768]{1,0:T(8,128)(2,1)S(1)} %copy-done, bf16[1024,768]{1,0:T(8,128)(2,1)S(1)} %copy-done.2), custom_call_target="tpu_custom_call" | custom-call | tf_op jit(solution)/shard_map/pallas_call | solution.py:349
  8.8 1.7 %collective-permute-start = (f32[1,2048]{1,0:T(1,128)S(1)}, f32[1,2048]{1,0:T(1,128)S(1)}, u32[]{:S(2)}, u32[]{:S(2)}) collective-permute-start(f32[1,2048]{1,0:T(1,128)S(1)} %get-tuple-element.12.refs_1_), channel_id=1, source_target_pairs={{0,1},{1,2},{2,3},{3,0},{4,5},{5,6},{6,7},{7,4},{8,9},{9,10},{10,1... | collective-permute-start | bytes 24584 | tf_op jit(solution)/shard_map/ppermute | solution.py:60
  10.5 2.9 %collective-permute-start.1 = (f32[1,2048]{1,0:T(1,128)S(1)}, f32[1,2048]{1,0:T(1,128)S(1)}, u32[]{:S(2)}, u32[]{:S(2)}) collective-permute-start(f32[1,2048]{1,0:T(1,128)S(1)} %get-tuple-element.12.refs_1_), channel_id=1, source_target_pairs={{0,2},{1,3},{2,0},{3,1},{4,6},{5,7},{6,4},{7,5},{8,10},{9,11},{10,... | collective-permute-start | bytes 24584 | tf_op jit(solution)/shard_map/ppermute | solution.py:60
  13.4 1.3 collective-permute-start.2
  14.7 0.9 collective-permute-done.1.refs_3_
  15.6 1.4 collective-permute-done.2.refs_4_
  17.0 2.1 %shard_map.42 = (f32[1,1024]{1,0:T(1,128)S(1)}, f32[1,2048]{1,0:T(1,128)}) custom-call(f32[1024,2048]{1,0:T(8,128)S(1)} %get-tuple-element.11.refs_0_, f32[1,2048]{1,0:T(1,128)S(1)} %get-tuple-element.12.refs_1_, f32[1,2048]{1,0:T(1,128)S(1)} %collective-permute-done.refs_2_, f32[1,2048]{1,0:T(1,128)S(1)} %collective-permute-done.1.refs_3_, ...), custom_call_target="tpu_custom_call" | custom-call | tf_op jit(solution)/shard_map/pallas_call | solution.py:349
  19.1 1.2 collective-permute-done.3
  20.4 20.5 %all_to_all.20.refs_1_ = f32[32,1,1024]{2,1,0:T(1,128)S(1)} all-to-all(f32[32,1,1024]{2,1,0:T(1,128)S(1)} %broadcast_in_dim.17), channel_id=1, replica_groups={{0,8,16,24,32,40,48,56,64,72,80,88,96,104,112,120,128,136,144,152,160,1..., dimensions={0} | all-to-all | bytes 262144 | tf_op jit(solution)/shard_map/all_to_all | solution.py:50
  40.9 1.9 %shard_map.43.refs_1_ = f32[1,2048]{1,0:T(1,128)S(1)} custom-call(f32[1024,2048]{1,0:T(8,128)S(1)} %get-tuple-element.11.refs_0_, f32[32,1,1024]{2,1,0:T(1,128)S(1)} %all_to_all.20.refs_1_), custom_call_target="tpu_custom_call" | custom-call | tf_op jit(solution)/shard_map/pallas_call | solution.py:349
  43.1 3.8 %collective-permute-start.5 = (f32[1,2048]{1,0:T(1,128)S(1)}, f32[1,2048]{1,0:T(1,128)S(1)}, u32[]{:S(2)}, u32[]{:S(2)}) collective-permute-start(f32[1,2048]{1,0:T(1,128)S(1)} %shard_map.43.refs_1_), channel_id=1, source_target_pairs={{0,2},{1,3},{2,0},{3,1},{4,6},{5,7},{6,4},{7,5},{8,10},{9,11},{10,... | collective-permute-start | bytes 24584 | tf_op jit(solution)/shard_map/ppermute | solution.py:60
  47.1 0.7 collective-permute-done.4.refs_2_
  47.8 0.9 collective-permute-done.5.refs_3_
  48.7 1.9 %collective-permute-done.6.refs_4_ = f32[1,2048]{1,0:T(1,128)S(1)} collective-permute-done((f32[1,2048]{1,0:T(1,128)S(1)}, f32[1,2048]{1,0:T(1,128)S(1)}, u32[]{:S(2)}, u32[]{:S(2)}) %collective-permute-start.6) | collective-permute-done | bytes 8224 | tf_op jit(solution)/shard_map/ppermute | solution.py:60
  50.6 2.1 %shard_map.44 = (f32[1,1024]{1,0:T(1,128)S(1)}, f32[1,2048]{1,0:T(1,128)}) custom-call(f32[1024,2048]{1,0:T(8,128)S(1)} %get-tuple-element.11.refs_0_, f32[1,2048]{1,0:T(1,128)S(1)} %shard_map.43.refs_1_, f32[1,2048]{1,0:T(1,128)S(1)} %collective-permute-done.4.refs_2_, f32[1,2048]{1,0:T(1,128)S(1)} %collective-permute-done.5.refs_3_, ...), custom_call_target="tpu_custom_call" | custom-call | tf_op jit(solution)/shard_map/pallas_call | solution.py:349
  52.7 1.2 collective-permute-done.7
  54.0 14.1 %all_to_all.21.refs_1_ = f32[32,1,1024]{2,1,0:T(1,128)S(1)} all-to-all(f32[32,1,1024]{2,1,0:T(1,128)S(1)} %broadcast_in_dim.19), channel_id=1, replica_groups={{0,8,16,24,32,40,48,56,64,72,80,88,96,104,112,120,128,136,144,152,160,1..., dimensions={0} | all-to-all | bytes 262144 | tf_op jit(solution)/shard_map/all_to_all | solution.py:50
  68.1 1.9 %shard_map.45.refs_1_ = f32[1,2048]{1,0:T(1,128)S(1)} custom-call(f32[1024,2048]{1,0:T(8,128)S(1)} %get-tuple-element.11.refs_0_, f32[32,1,1024]{2,1,0:T(1,128)S(1)} %all_to_all.21.refs_1_), custom_call_target="tpu_custom_call" | custom-call | tf_op jit(solution)/shard_map/pallas_call | solution.py:349
  70.1 1.4 collective-permute-start.10
  71.5 0.7 collective-permute-start.8
  72.2 1.5 collective-permute-start.9
  73.8 2.5 %collective-permute-done.8.refs_2_ = f32[1,2048]{1,0:T(1,128)S(1)} collective-permute-done((f32[1,2048]{1,0:T(1,128)S(1)}, f32[1,2048]{1,0:T(1,128)S(1)}, u32[]{:S(2)}, u32[]{:S(2)}) %collective-permute-start.8) | collective-permute-done | bytes 8224 | tf_op jit(solution)/shard_map/ppermute | solution.py:60
  76.3 1.0 collective-permute-done.9.refs_3_
  77.3 1.3 shard_map.46
  78.7 1.3 shard_map.48
  80.0 0.6 collective-permute-start.11
  80.6 1.3 shard_map.49.mine_ref
  82.2 2.3 %collective-permute-start.13 = (bf16[16,104,128]{2,1,0:T(8,128)(2,1)S(1)}, bf16[16,104,128]{2,1,0:T(8,128)(2,1)S(1)}, u32[]{:S(2)}, u32[]{:S(2)}) collective-permute-start(bf16[16,104,128]{2,1,0:T(8,128)(2,1)S(1)} %shard_map.50), channel_id=1, source_target_pairs={{0,8},{4,12},{8,0},{12,4},{16,24},{20,28},{24,16},{28,20},{32,40},... | collective-permute-start | bytes 1277960 | tf_op jit(solution)/shard_map/ppermute | solution.py:31
  84.4 1.4 shard_map.47.mine_ref
  85.9 8.6 %collective-permute-done.13.refs_0_ = bf16[16,104,128]{2,1,0:T(8,128)(2,1)S(1)} collective-permute-done((bf16[16,104,128]{2,1,0:T(8,128)(2,1)S(1)}, bf16[16,104,128]{2,1,0:T(8,128)(2,1)S(1)}, u32[]{:S(2)}, u32[]{:S(2)}) %collective-permute-start.13) | collective-permute-done | bytes 426016 | tf_op jit(solution)/shard_map/ppermute | solution.py:31
  95.0 19.5 %all_to_all.22.refs_0_ = bf16[16,104,128]{2,1,0:T(8,128)(2,1)S(1)} all-to-all(bf16[16,104,128]{2,1,0:T(8,128)(2,1)S(1)} %shard_map.51), channel_id=1, replica_groups={{0,16,32,48,64,80,96,112,128,144,160,176,192,208,224,240},{4,20,36,52,6..., dimensions={0} | all-to-all | bytes 851968 | tf_op jit(solution)/shard_map/all_to_all | solution.py:50
  114.5 0.9 shard_map.52
  115.5 18.5 %all_to_all.23.refs_3_ = bf16[16,104,128]{2,1,0:T(8,128)(2,1)S(1)} all-to-all(bf16[16,104,128]{2,1,0:T(8,128)(2,1)S(1)} %get-tuple-element.19), channel_id=1, replica_groups={{0,16,32,48,64,80,96,112,128,144,160,176,192,208,224,240},{4,20,36,52,6..., dimensions={0} | all-to-all | bytes 851968 | tf_op jit(solution)/shard_map/all_to_all | solution.py:50
  133.9 1.3 collective-permute-start.15
  135.2 7.5 %collective-permute-done.15.refs_3_ = bf16[16,104,128]{2,1,0:T(8,128)(2,1)S(1)} collective-permute-done((bf16[16,104,128]{2,1,0:T(8,128)(2,1)S(1)}, bf16[16,104,128]{2,1,0:T(8,128)(2,1)S(1)}, u32[]{:S(2)}, u32[]{:S(2)}) %collective-permute-start.15) | collective-permute-done | bytes 426016 | tf_op jit(solution)/shard_map/ppermute | solution.py:31
  142.7 1.2 shard_map.53
  143.9 1.2 shard_map.55
  145.1 1.2 shard_map.54
  146.4 1.2 shard_map.56
  147.6 1.6 %collective-permute-start.17 = (f32[2,2048]{1,0:T(2,128)S(1)}, f32[2,2048]{1,0:T(2,128)S(1)}, u32[]{:S(2)}, u32[]{:S(2)}) collective-permute-start(f32[2,2048]{1,0:T(2,128)S(1)} %add_add_fusion.1), channel_id=1, source_target_pairs={{0,2},{1,3},{2,0},{3,1},{4,6},{5,7},{6,4},{7,5},{8,10},{9,11},{10,... | collective-permute-start | bytes 49160 | tf_op jit(solution)/shard_map/ppermute | solution.py:60
  149.2 1.8 %collective-permute-start.18 = (f32[2,2048]{1,0:T(2,128)S(1)}, f32[2,2048]{1,0:T(2,128)S(1)}, u32[]{:S(2)}, u32[]{:S(2)}) collective-permute-start(f32[2,2048]{1,0:T(2,128)S(1)} %add_add_fusion.1), channel_id=1, source_target_pairs={{0,1},{1,2},{2,3},{3,0},{4,5},{5,6},{6,7},{7,4},{8,9},{9,10},{10,1... | collective-permute-start | bytes 49160 | tf_op jit(solution)/shard_map/ppermute | solution.py:60
  151.1 1.4 collective-permute-start.19
  152.5 0.6 collective-permute-done.17
  153.0 1.1 collective-permute-done.18
  154.2 0.6 collective-permute-done.19
  154.8 0.6 fusion
  (27 shorter events, 1.7 us)
Async XLA Ops:
  0.6 1.9 %copy-start = (bf16[2048,768]{1,0:T(8,128)(2,1)S(1)}, bf16[2048,768]{1,0:T(8,128)(2,1)}, u32[]{:S(2)}) copy-start(bf16[2048,768]{1,0:T(8,128)(2,1)} %refs_2_.5) | copy-start | bytes 9437188
  2.5 1.4 copy-start.2
  8.8 5.9 %collective-permute-start = (f32[1,2048]{1,0:T(1,128)S(1)}, f32[1,2048]{1,0:T(1,128)S(1)}, u32[]{:S(2)}, u32[]{:S(2)}) collective-permute-start(f32[1,2048]{1,0:T(1,128)S(1)} %get-tuple-element.12.refs_1_), channel_id=1, source_target_pairs={{0,1},{1,2},{2,3},{3,0},{4,5},{5,6},{6,7},{7,4},{8,9},{9,10},{10,1... | collective-permute-start | bytes 24584 | tf_op jit(solution)/shard_map/ppermute | solution.py:60
  10.5 5.2 %collective-permute-start.1 = (f32[1,2048]{1,0:T(1,128)S(1)}, f32[1,2048]{1,0:T(1,128)S(1)}, u32[]{:S(2)}, u32[]{:S(2)}) collective-permute-start(f32[1,2048]{1,0:T(1,128)S(1)} %get-tuple-element.12.refs_1_), channel_id=1, source_target_pairs={{0,2},{1,3},{2,0},{3,1},{4,6},{5,7},{6,4},{7,5},{8,10},{9,11},{10,... | collective-permute-start | bytes 24584 | tf_op jit(solution)/shard_map/ppermute | solution.py:60
  13.4 3.7 %collective-permute-start.2 = (f32[1,2048]{1,0:T(1,128)S(1)}, f32[1,2048]{1,0:T(1,128)S(1)}, u32[]{:S(2)}, u32[]{:S(2)}) collective-permute-start(f32[1,2048]{1,0:T(1,128)S(1)} %get-tuple-element.12.refs_1_), channel_id=1, source_target_pairs={{0,3},{1,0},{2,1},{3,2},{4,7},{5,4},{6,5},{7,6},{8,11},{9,8},{10,9... | collective-permute-start | bytes 24584 | tf_op jit(solution)/shard_map/ppermute | solution.py:60
  19.1 1.2 collective-permute-start.3
  42.9 4.9 %collective-permute-start.4 = (f32[1,2048]{1,0:T(1,128)S(1)}, f32[1,2048]{1,0:T(1,128)S(1)}, u32[]{:S(2)}, u32[]{:S(2)}) collective-permute-start(f32[1,2048]{1,0:T(1,128)S(1)} %shard_map.43.refs_1_), channel_id=1, source_target_pairs={{0,1},{1,2},{2,3},{3,0},{4,5},{5,6},{6,7},{7,4},{8,9},{9,10},{10,1... | collective-permute-start | bytes 24584 | tf_op jit(solution)/shard_map/ppermute | solution.py:60
  43.1 5.6 %collective-permute-start.5 = (f32[1,2048]{1,0:T(1,128)S(1)}, f32[1,2048]{1,0:T(1,128)S(1)}, u32[]{:S(2)}, u32[]{:S(2)}) collective-permute-start(f32[1,2048]{1,0:T(1,128)S(1)} %shard_map.43.refs_1_), channel_id=1, source_target_pairs={{0,2},{1,3},{2,0},{3,1},{4,6},{5,7},{6,4},{7,5},{8,10},{9,11},{10,... | collective-permute-start | bytes 24584 | tf_op jit(solution)/shard_map/ppermute | solution.py:60
  47.0 3.7 %collective-permute-start.6 = (f32[1,2048]{1,0:T(1,128)S(1)}, f32[1,2048]{1,0:T(1,128)S(1)}, u32[]{:S(2)}, u32[]{:S(2)}) collective-permute-start(f32[1,2048]{1,0:T(1,128)S(1)} %shard_map.43.refs_1_), channel_id=1, source_target_pairs={{0,3},{1,0},{2,1},{3,2},{4,7},{5,4},{6,5},{7,6},{8,11},{9,8},{10,9... | collective-permute-start | bytes 24584 | tf_op jit(solution)/shard_map/ppermute | solution.py:60
  52.7 1.2 collective-permute-start.7
  70.1 3.7 %collective-permute-start.10 = (f32[1,2048]{1,0:T(1,128)S(1)}, f32[1,2048]{1,0:T(1,128)S(1)}, u32[]{:S(2)}, u32[]{:S(2)}) collective-permute-start(f32[1,2048]{1,0:T(1,128)S(1)} %shard_map.45.refs_1_), channel_id=1, source_target_pairs={{0,3},{1,0},{2,1},{3,2},{4,7},{5,4},{6,5},{7,6},{8,11},{9,8},{10,9... | collective-permute-start | bytes 24584 | tf_op jit(solution)/shard_map/ppermute | solution.py:60
  71.5 4.9 %collective-permute-start.8 = (f32[1,2048]{1,0:T(1,128)S(1)}, f32[1,2048]{1,0:T(1,128)S(1)}, u32[]{:S(2)}, u32[]{:S(2)}) collective-permute-start(f32[1,2048]{1,0:T(1,128)S(1)} %shard_map.45.refs_1_), channel_id=1, source_target_pairs={{0,1},{1,2},{2,3},{3,0},{4,5},{5,6},{6,7},{7,4},{8,9},{9,10},{10,1... | collective-permute-start | bytes 24584 | tf_op jit(solution)/shard_map/ppermute | solution.py:60
  72.2 5.2 %collective-permute-start.9 = (f32[1,2048]{1,0:T(1,128)S(1)}, f32[1,2048]{1,0:T(1,128)S(1)}, u32[]{:S(2)}, u32[]{:S(2)}) collective-permute-start(f32[1,2048]{1,0:T(1,128)S(1)} %shard_map.45.refs_1_), channel_id=1, source_target_pairs={{0,2},{1,3},{2,0},{3,1},{4,6},{5,7},{6,4},{7,5},{8,10},{9,11},{10,... | collective-permute-start | bytes 24584 | tf_op jit(solution)/shard_map/ppermute | solution.py:60
  78.6 3.2 %collective-permute-start.12 = (f32[256,896]{1,0:T(8,128)S(1)}, f32[256,896]{1,0:T(8,128)S(1)}, u32[]{:S(2)}, u32[]{:S(2)}) collective-permute-start(f32[256,896]{1,0:T(8,128)S(1)} %get-tuple-element.16), channel_id=1, source_target_pairs={{0,4},{4,0},{8,12},{12,8},{16,20},{20,16},{24,28},{28,24},{32,36},... | collective-permute-start | bytes 2752520 | tf_op jit(solution)/shard_map/ppermute | solution.py:31
  80.0 5.9 %collective-permute-start.11 = (f32[256,896]{1,0:T(8,128)S(1)}, f32[256,896]{1,0:T(8,128)S(1)}, u32[]{:S(2)}, u32[]{:S(2)}) collective-permute-start(f32[256,896]{1,0:T(8,128)S(1)} %shard_map.48), channel_id=1, source_target_pairs={{0,4},{4,0},{8,12},{12,8},{16,20},{20,16},{24,28},{28,24},{32,36},... | collective-permute-start | bytes 2752520 | tf_op jit(solution)/shard_map/ppermute | solution.py:31
  80.6 3.9 %copy-start.1 = (bf16[2048,768]{1,0:T(8,128)(2,1)S(1)}, bf16[2048,768]{1,0:T(8,128)(2,1)}, u32[]{:S(2)}) copy-start(bf16[2048,768]{1,0:T(8,128)(2,1)} %refs_2_.5) | copy-start | bytes 9437188
  82.2 12.3 %collective-permute-start.13 = (bf16[16,104,128]{2,1,0:T(8,128)(2,1)S(1)}, bf16[16,104,128]{2,1,0:T(8,128)(2,1)S(1)}, u32[]{:S(2)}, u32[]{:S(2)}) collective-permute-start(bf16[16,104,128]{2,1,0:T(8,128)(2,1)S(1)} %shard_map.50), channel_id=1, source_target_pairs={{0,8},{4,12},{8,0},{12,4},{16,24},{20,28},{24,16},{28,20},{32,40},... | collective-permute-start | bytes 1277960 | tf_op jit(solution)/shard_map/ppermute | solution.py:31
  133.9 8.7 %collective-permute-start.15 = (bf16[16,104,128]{2,1,0:T(8,128)(2,1)S(1)}, bf16[16,104,128]{2,1,0:T(8,128)(2,1)S(1)}, u32[]{:S(2)}, u32[]{:S(2)}) collective-permute-start(bf16[16,104,128]{2,1,0:T(8,128)(2,1)S(1)} %all_to_all.23.refs_3_), channel_id=1, source_target_pairs={{0,8},{4,12},{8,0},{12,4},{16,24},{20,28},{24,16},{28,20},{32,40},... | collective-permute-start | bytes 1277960 | tf_op jit(solution)/shard_map/ppermute | solution.py:31
  135.2 9.9 %collective-permute-start.14 = (bf16[16,104,128]{2,1,0:T(8,128)(2,1)S(1)}, bf16[16,104,128]{2,1,0:T(8,128)(2,1)S(1)}, u32[]{:S(2)}, u32[]{:S(2)}) collective-permute-start(bf16[16,104,128]{2,1,0:T(8,128)(2,1)S(1)} %all_to_all.23.refs_3_), channel_id=1, source_target_pairs={{0,4},{4,0},{8,12},{12,8},{16,20},{20,16},{24,28},{28,24},{32,36},... | collective-permute-start | bytes 1277960 | tf_op jit(solution)/shard_map/ppermute | solution.py:31
  142.7 3.7 %collective-permute-start.16 = (bf16[16,104,128]{2,1,0:T(8,128)(2,1)S(1)}, bf16[16,104,128]{2,1,0:T(8,128)(2,1)S(1)}, u32[]{:S(2)}, u32[]{:S(2)}) collective-permute-start(bf16[16,104,128]{2,1,0:T(8,128)(2,1)S(1)} %collective-permute-done.15.refs_3_), channel_id=1, source_target_pairs={{0,4},{4,0},{8,12},{12,8},{16,20},{20,16},{24,28},{28,24},{32,36},... | collective-permute-start | bytes 1277960 | tf_op jit(solution)/shard_map/ppermute | solution.py:31
  147.6 5.4 %collective-permute-start.17 = (f32[2,2048]{1,0:T(2,128)S(1)}, f32[2,2048]{1,0:T(2,128)S(1)}, u32[]{:S(2)}, u32[]{:S(2)}) collective-permute-start(f32[2,2048]{1,0:T(2,128)S(1)} %add_add_fusion.1), channel_id=1, source_target_pairs={{0,2},{1,3},{2,0},{3,1},{4,6},{5,7},{6,4},{7,5},{8,10},{9,11},{10,... | collective-permute-start | bytes 49160 | tf_op jit(solution)/shard_map/ppermute | solution.py:60
  149.2 4.9 %collective-permute-start.18 = (f32[2,2048]{1,0:T(2,128)S(1)}, f32[2,2048]{1,0:T(2,128)S(1)}, u32[]{:S(2)}, u32[]{:S(2)}) collective-permute-start(f32[2,2048]{1,0:T(2,128)S(1)} %add_add_fusion.1), channel_id=1, source_target_pairs={{0,1},{1,2},{2,3},{3,0},{4,5},{5,6},{6,7},{7,4},{8,9},{9,10},{10,1... | collective-permute-start | bytes 49160 | tf_op jit(solution)/shard_map/ppermute | solution.py:60
  151.1 3.7 %collective-permute-start.19 = (f32[2,2048]{1,0:T(2,128)S(1)}, f32[2,2048]{1,0:T(2,128)S(1)}, u32[]{:S(2)}, u32[]{:S(2)}) collective-permute-start(f32[2,2048]{1,0:T(2,128)S(1)} %add_add_fusion.1), channel_id=1, source_target_pairs={{0,3},{1,0},{2,1},{3,2},{4,7},{5,4},{6,5},{7,6},{8,11},{9,8},{10,9... | collective-permute-start | bytes 49160 | tf_op jit(solution)/shard_map/ppermute | solution.py:60

commit v7 on v6

--- a/solution.py
+++ b/solution.py
@@ -35,18 +35,38 @@
     return partner(value, 1)
 
 
+def parity_of(core):
+    here = lax.axis_index("pts") // C
+    return jnp.where(core == 0, here % PARITIES, here // X % PARITIES)
+
+
 def other_parity(value):
-    return partner(value, C)
-
-
-def exchange(value, parities):
-    slabs = lax.axis_size("pts") // (X * C)
-    step = PARITIES // parities
-    groups = [
-        [place(z, x, core) for z in range(slabs) for x in range(parity, X, step)]
-        for parity in range(step)
+    size = lax.axis_size("pts")
+    flip = (C, C * X)
+    return lax.ppermute(value, "pts", [(i, i ^ flip[i % C]) for i in range(size)])
+
+
+def sorted_by_parity(chips):
+    slabs = chips // X
+    return [
+        [
+            [(z, x) for z in range(slabs) for x in range(X) if (z if core else x) % PARITIES == p]
+            for p in range(PARITIES)
+        ]
         for core in range(C)
     ]
+
+
+def exchange(value, parities):
+    chips = lax.axis_size("pts") // C
+    if parities == PARITIES:
+        groups = [[chip * C + core for chip in range(chips)] for core in range(C)]
+    else:
+        groups = [
+            [place(z, x, core) for z, x in some]
+            for core, parts in enumerate(sorted_by_parity(chips))
+            for some in parts
+        ]
     return lax.all_to_all(value, "pts", 0, 0, axis_index_groups=groups)
 
 
@@ -110,21 +130,22 @@
     count = points_ref.shape[0]
     rows = centroids_ref.shape[0]
     core = lax.axis_index("pts") % C
-    parity = lax.axis_index("pts") // C % PARITIES
-    slabs = rows // (each * X * C)
-
-    def order(z, carry):
-        for n in range(X * C):
-            side, pair = n // (X // PARITIES), n % (X // PARITIES)
+    chips = rows // (each * C)
+
+    def order(block, carry):
+        for side in range(C * PARITIES):
             to_core = core if side // PARITIES == 0 else 1 - core
-            to_parity = parity if side % PARITIES == 0 else 1 - parity
-            start = place(z, pair * PARITIES + to_parity, to_core) * each
-            block = (side * slabs + z) * (X // PARITIES) + pair
-            here = pl.ds(pl.multiple_of(block * each, each), each)
+            parity = parity_of(to_core)
+            parity = parity if side % PARITIES == 0 else 1 - parity
+            along_x = place(block // PARITIES, block % PARITIES * PARITIES + parity, 0)
+            along_z = place(block // X * PARITIES + parity, block % X, 1)
+            start = jnp.where(to_core == 0, along_x, along_z) * each
+            here = (side * (chips // PARITIES) + block) * each
+            here = pl.ds(pl.multiple_of(here, each), each)
             split_ref[here, :] = centroids_ref[pl.ds(pl.multiple_of(start, each), each), :]
         return carry
 
-    lax.fori_loop(0, slabs, order, 0, unroll=2)
+    lax.fori_loop(0, chips // PARITIES, order, 0, unroll=2)
     chunk = 256
     for first in range(0, count, chunk):
         here = slice(first, first + chunk)
@@ -148,10 +169,15 @@
 
 
 def common_order(row):
+    core = lax.axis_index("pts") % C
     size = row.shape[1] // (C * PARITIES)
     quarters = [row[:, n * size : (n + 1) * size] for n in range(C * PARITIES)]
-    swapped = jnp.concatenate([quarters[n ^ 1] for n in range(C * PARITIES)], axis=1)
-    return jnp.where(lax.axis_index("pts") // C % PARITIES == 0, row, swapped)
+    out = []
+    for half in range(C):
+        straight = parity_of(core if half == 0 else 1 - core) == 0
+        pair = quarters[half * PARITIES : (half + 1) * PARITIES]
+        out += [jnp.where(straight, *pair), jnp.where(straight, *pair[::-1])]
+    return jnp.concatenate(out, axis=1)
 
 
 def row_kernel(scores_ref, values_ref, row_ref, cols_ref, top_ref, total_ref, *, level):

time: 157 us -> 153 us (0.975)
  waiting for transfers between devices: 30.2 us -> 25.6 us
    ppermute x8 -> x6, waiting for transfers between devices: 18.4 us -> 2.34 us  [partner(): return lax.ppermute(value, 'pts', [(i, i ^ mask) for i in range(size)])]
    ppermute x0 -> x2, waiting for transfers between devices: none -> 11.4 us  [other_parity(): lax.ppermute(value, 'pts', [(i, i ^ flip[i % C]) for i in range(size)])]
    ppermute x0 -> x2, starting transfers between devices: none -> 3.7 us  [other_parity(): lax.ppermute(value, 'pts', [(i, i ^ flip[i % C]) for i in range(size)])]
    ppermute x8 -> x6, starting transfers between devices: 4.23 us -> 0.69 us  [partner(): return lax.ppermute(value, 'pts', [(i, i ^ mask) for i in range(size)])]
where the time goes in v7:
time: 153 us; the launch traced here: 152 us
  blocking collectives  73.2 us (48%)
  waiting for transfers between devices  25.6 us (17%)
  Pallas kernels  25.3 us (17%)
  starting transfers between devices  23 us (15%)
  local copies, waits for them, and re-layouts  3.44 us (2%)
    all_to_all x4, blocking collectives, exchange(): return lax.all_to_all(value, 'pts', 0, 0, axis_index_groups=groups)  73.2 us
    pallas_call x16, Pallas kernels, call(): pl.pallas_call(kernel, out_shape=[jax.ShapeDtypeStruct(shape, dtype) for...  25.3 us
    ppermute x12, starting transfers between devices, cen_shift(): lax.ppermute(value, 'cen', [(i, (i + step) % size) for i in range(size)])  18.6 us
    ppermute x12, waiting for transfers between devices, cen_shift(): lax.ppermute(value, 'cen', [(i, (i + step) % size) for i in range(size)])  11.9 us
    ppermute x2, waiting for transfers between devices, other_parity(): lax.ppermute(value, 'pts', [(i, i ^ flip[i % C]) for i in range(size)])  11.4 us
    ppermute x2, starting transfers between devices, other_parity(): lax.ppermute(value, 'pts', [(i, i ^ flip[i % C]) for i in range(size)])  3.7 us
    unnamed x6, local copies, waits for them, and re-layouts  3.3 us
  transfers between devices with their start and end apart: 20, of which 15 were waited for; matrix products, arithmetic and copies ran while one was open for 0% of the time, Pallas kernels for 5%

profile of v7, /device:TPU:2, one launch (start us, length us, event | category | flops | bytes accessed | tf_op | source)
XLA Modules:
  0.0 152.1 jit_solution(10475124226957001987)
XLA Ops:
  0.6 1.9 %copy-done = bf16[2048,768]{1,0:T(8,128)(2,1)S(1)} copy-done((bf16[2048,768]{1,0:T(8,128)(2,1)S(1)}, bf16[2048,768]{1,0:T(8,128)(2,1)}, u32[]{:S(2)}) %copy-start) | copy-done | bytes 3145752
  2.5 1.4 copy-done.2
  3.9 5.2 %shard_map.41 = (f32[1024,2048]{1,0:T(8,128)S(1)}, f32[1,2048]{1,0:T(1,128)S(1)}, bf16[768,2048]{1,0:T(8,128)(2,1)S(1)}) custom-call(bf16[2048,768]{1,0:T(8,128)(2,1)S(1)} %copy-done, bf16[1024,768]{1,0:T(8,128)(2,1)S(1)} %copy-done.2), custom_call_target="tpu_custom_call" | custom-call | tf_op jit(solution)/shard_map/pallas_call | solution.py:375
  9.2 1.7 %collective-permute-start = (f32[1,2048]{1,0:T(1,128)S(1)}, f32[1,2048]{1,0:T(1,128)S(1)}, u32[]{:S(2)}, u32[]{:S(2)}) collective-permute-start(f32[1,2048]{1,0:T(1,128)S(1)} %get-tuple-element.12.refs_1_), channel_id=1, source_target_pairs={{0,1},{1,2},{2,3},{3,0},{4,5},{5,6},{6,7},{7,4},{8,9},{9,10},{10,1... | collective-permute-start | bytes 24584 | tf_op jit(solution)/shard_map/ppermute | solution.py:80
  10.8 2.9 %collective-permute-start.1 = (f32[1,2048]{1,0:T(1,128)S(1)}, f32[1,2048]{1,0:T(1,128)S(1)}, u32[]{:S(2)}, u32[]{:S(2)}) collective-permute-start(f32[1,2048]{1,0:T(1,128)S(1)} %get-tuple-element.12.refs_1_), channel_id=1, source_target_pairs={{0,2},{1,3},{2,0},{3,1},{4,6},{5,7},{6,4},{7,5},{8,10},{9,11},{10,... | collective-permute-start | bytes 24584 | tf_op jit(solution)/shard_map/ppermute | solution.py:80
  13.7 1.3 collective-permute-start.2
  15.1 0.9 collective-permute-done.1.refs_3_
  16.0 1.4 collective-permute-done.2.refs_4_
  17.4 2.2 %shard_map.42 = (f32[1,1024]{1,0:T(1,128)S(1)}, f32[1,2048]{1,0:T(1,128)}) custom-call(f32[1024,2048]{1,0:T(8,128)S(1)} %get-tuple-element.11.refs_0_, f32[1,2048]{1,0:T(1,128)S(1)} %get-tuple-element.12.refs_1_, f32[1,2048]{1,0:T(1,128)S(1)} %collective-permute-done.refs_2_, f32[1,2048]{1,0:T(1,128)S(1)} %collective-permute-done.1.refs_3_, ...), custom_call_target="tpu_custom_call" | custom-call | tf_op jit(solution)/shard_map/pallas_call | solution.py:375
  19.5 1.2 collective-permute-done.3
  20.8 20.5 %all_to_all.20.refs_1_ = f32[32,1,1024]{2,1,0:T(1,128)S(1)} all-to-all(f32[32,1,1024]{2,1,0:T(1,128)S(1)} %broadcast_in_dim.17), channel_id=1, replica_groups={{0,8,16,24,32,40,48,56,64,72,80,88,96,104,112,120,128,136,144,152,160,1..., dimensions={0} | all-to-all | bytes 262144 | tf_op jit(solution)/shard_map/all_to_all | solution.py:70
  41.3 1.9 %shard_map.43.refs_1_ = f32[1,2048]{1,0:T(1,128)S(1)} custom-call(f32[1024,2048]{1,0:T(8,128)S(1)} %get-tuple-element.11.refs_0_, f32[32,1,1024]{2,1,0:T(1,128)S(1)} %all_to_all.20.refs_1_), custom_call_target="tpu_custom_call" | custom-call | tf_op jit(solution)/shard_map/pallas_call | solution.py:375
  43.5 3.8 %collective-permute-start.5 = (f32[1,2048]{1,0:T(1,128)S(1)}, f32[1,2048]{1,0:T(1,128)S(1)}, u32[]{:S(2)}, u32[]{:S(2)}) collective-permute-start(f32[1,2048]{1,0:T(1,128)S(1)} %shard_map.43.refs_1_), channel_id=1, source_target_pairs={{0,2},{1,3},{2,0},{3,1},{4,6},{5,7},{6,4},{7,5},{8,10},{9,11},{10,... | collective-permute-start | bytes 24584 | tf_op jit(solution)/shard_map/ppermute | solution.py:80
  47.5 0.7 collective-permute-done.4.refs_2_
  48.2 0.9 collective-permute-done.5.refs_3_
  49.1 1.9 %collective-permute-done.6.refs_4_ = f32[1,2048]{1,0:T(1,128)S(1)} collective-permute-done((f32[1,2048]{1,0:T(1,128)S(1)}, f32[1,2048]{1,0:T(1,128)S(1)}, u32[]{:S(2)}, u32[]{:S(2)}) %collective-permute-start.6) | collective-permute-done | bytes 8224 | tf_op jit(solution)/shard_map/ppermute | solution.py:80
  51.0 2.2 %shard_map.44 = (f32[1,1024]{1,0:T(1,128)S(1)}, f32[1,2048]{1,0:T(1,128)}) custom-call(f32[1024,2048]{1,0:T(8,128)S(1)} %get-tuple-element.11.refs_0_, f32[1,2048]{1,0:T(1,128)S(1)} %shard_map.43.refs_1_, f32[1,2048]{1,0:T(1,128)S(1)} %collective-permute-done.4.refs_2_, f32[1,2048]{1,0:T(1,128)S(1)} %collective-permute-done.5.refs_3_, ...), custom_call_target="tpu_custom_call" | custom-call | tf_op jit(solution)/shard_map/pallas_call | solution.py:375
  53.2 1.2 collective-permute-done.7
  54.5 14.1 %all_to_all.21.refs_1_ = f32[32,1,1024]{2,1,0:T(1,128)S(1)} all-to-all(f32[32,1,1024]{2,1,0:T(1,128)S(1)} %broadcast_in_dim.19), channel_id=1, replica_groups={{0,8,16,24,32,40,48,56,64,72,80,88,96,104,112,120,128,136,144,152,160,1..., dimensions={0} | all-to-all | bytes 262144 | tf_op jit(solution)/shard_map/all_to_all | solution.py:70
  68.6 1.9 %shard_map.45.refs_1_ = f32[1,2048]{1,0:T(1,128)S(1)} custom-call(f32[1024,2048]{1,0:T(8,128)S(1)} %get-tuple-element.11.refs_0_, f32[32,1,1024]{2,1,0:T(1,128)S(1)} %all_to_all.21.refs_1_), custom_call_target="tpu_custom_call" | custom-call | tf_op jit(solution)/shard_map/pallas_call | solution.py:375
  70.5 1.4 collective-permute-start.10
  71.9 0.7 collective-permute-start.8
  72.6 1.5 collective-permute-start.9
  74.2 2.5 %collective-permute-done.8.refs_2_ = f32[1,2048]{1,0:T(1,128)S(1)} collective-permute-done((f32[1,2048]{1,0:T(1,128)S(1)}, f32[1,2048]{1,0:T(1,128)S(1)}, u32[]{:S(2)}, u32[]{:S(2)}) %collective-permute-start.8) | collective-permute-done | bytes 8224 | tf_op jit(solution)/shard_map/ppermute | solution.py:80
  76.8 1.0 collective-permute-done.9.refs_3_
  77.8 1.3 shard_map.46
  79.2 1.3 shard_map.48
  80.4 0.6 collective-permute-start.11
  81.0 1.3 shard_map.49.mine_ref
  82.6 2.3 %collective-permute-start.13 = (bf16[16,104,128]{2,1,0:T(8,128)(2,1)S(1)}, bf16[16,104,128]{2,1,0:T(8,128)(2,1)S(1)}, u32[]{:S(2)}, u32[]{:S(2)}) collective-permute-start(bf16[16,104,128]{2,1,0:T(8,128)(2,1)S(1)} %shard_map.50), channel_id=1, source_target_pairs={{0,8},{4,36},{8,0},{12,44},{16,24},{20,52},{24,16},{28,60},{32,40}... | collective-permute-start | bytes 1277960 | tf_op jit(solution)/shard_map/ppermute | solution.py:46
  84.9 1.4 shard_map.47.mine_ref
  86.3 4.7 %collective-permute-done.13.refs_0_ = bf16[16,104,128]{2,1,0:T(8,128)(2,1)S(1)} collective-permute-done((bf16[16,104,128]{2,1,0:T(8,128)(2,1)S(1)}, bf16[16,104,128]{2,1,0:T(8,128)(2,1)S(1)}, u32[]{:S(2)}, u32[]{:S(2)}) %collective-permute-start.13) | collective-permute-done | bytes 426016 | tf_op jit(solution)/shard_map/ppermute | solution.py:46
  91.6 19.9 %all_to_all.22.refs_0_ = bf16[16,104,128]{2,1,0:T(8,128)(2,1)S(1)} all-to-all(bf16[16,104,128]{2,1,0:T(8,128)(2,1)S(1)} %shard_map.51), channel_id=1, replica_groups={{0,16,32,48,64,80,96,112,128,144,160,176,192,208,224,240},{8,24,40,56,7..., dimensions={0} | all-to-all | bytes 851968 | tf_op jit(solution)/shard_map/all_to_all | solution.py:70
  111.5 0.9 shard_map.52
  112.4 18.8 %all_to_all.23.refs_3_ = bf16[16,104,128]{2,1,0:T(8,128)(2,1)S(1)} all-to-all(bf16[16,104,128]{2,1,0:T(8,128)(2,1)S(1)} %get-tuple-element.19), channel_id=1, replica_groups={{0,16,32,48,64,80,96,112,128,144,160,176,192,208,224,240},{8,24,40,56,7..., dimensions={0} | all-to-all | bytes 851968 | tf_op jit(solution)/shard_map/all_to_all | solution.py:70
  131.2 1.4 collective-permute-start.15
  132.6 6.7 %collective-permute-done.15.refs_3_ = bf16[16,104,128]{2,1,0:T(8,128)(2,1)S(1)} collective-permute-done((bf16[16,104,128]{2,1,0:T(8,128)(2,1)S(1)}, bf16[16,104,128]{2,1,0:T(8,128)(2,1)S(1)}, u32[]{:S(2)}, u32[]{:S(2)}) %collective-permute-start.15) | collective-permute-done | bytes 426016 | tf_op jit(solution)/shard_map/ppermute | solution.py:46
  139.3 1.2 shard_map.53
  140.5 1.2 shard_map.55
  141.8 1.2 shard_map.54
  143.0 1.2 shard_map.56
  144.3 1.6 %collective-permute-start.17 = (f32[2,2048]{1,0:T(2,128)S(1)}, f32[2,2048]{1,0:T(2,128)S(1)}, u32[]{:S(2)}, u32[]{:S(2)}) collective-permute-start(f32[2,2048]{1,0:T(2,128)S(1)} %add_add_fusion.1), channel_id=1, source_target_pairs={{0,2},{1,3},{2,0},{3,1},{4,6},{5,7},{6,4},{7,5},{8,10},{9,11},{10,... | collective-permute-start | bytes 49160 | tf_op jit(solution)/shard_map/ppermute | solution.py:80
  145.9 1.9 %collective-permute-start.18 = (f32[2,2048]{1,0:T(2,128)S(1)}, f32[2,2048]{1,0:T(2,128)S(1)}, u32[]{:S(2)}, u32[]{:S(2)}) collective-permute-start(f32[2,2048]{1,0:T(2,128)S(1)} %add_add_fusion.1), channel_id=1, source_target_pairs={{0,1},{1,2},{2,3},{3,0},{4,5},{5,6},{6,7},{7,4},{8,9},{9,10},{10,1... | collective-permute-start | bytes 49160 | tf_op jit(solution)/shard_map/ppermute | solution.py:80
  147.7 1.4 collective-permute-start.19
  149.1 0.6 collective-permute-done.17
  149.7 1.1 collective-permute-done.18
  150.8 0.7 collective-permute-done.19
  151.5 0.6 fusion
  (27 shorter events, 1.7 us)
Async XLA Ops:
  0.6 1.9 %copy-start = (bf16[2048,768]{1,0:T(8,128)(2,1)S(1)}, bf16[2048,768]{1,0:T(8,128)(2,1)}, u32[]{:S(2)}) copy-start(bf16[2048,768]{1,0:T(8,128)(2,1)} %refs_2_.5) | copy-start | bytes 9437188
  2.5 1.4 copy-start.2
  9.2 5.9 %collective-permute-start = (f32[1,2048]{1,0:T(1,128)S(1)}, f32[1,2048]{1,0:T(1,128)S(1)}, u32[]{:S(2)}, u32[]{:S(2)}) collective-permute-start(f32[1,2048]{1,0:T(1,128)S(1)} %get-tuple-element.12.refs_1_), channel_id=1, source_target_pairs={{0,1},{1,2},{2,3},{3,0},{4,5},{5,6},{6,7},{7,4},{8,9},{9,10},{10,1... | collective-permute-start | bytes 24584 | tf_op jit(solution)/shard_map/ppermute | solution.py:80
  10.8 5.2 %collective-permute-start.1 = (f32[1,2048]{1,0:T(1,128)S(1)}, f32[1,2048]{1,0:T(1,128)S(1)}, u32[]{:S(2)}, u32[]{:S(2)}) collective-permute-start(f32[1,2048]{1,0:T(1,128)S(1)} %get-tuple-element.12.refs_1_), channel_id=1, source_target_pairs={{0,2},{1,3},{2,0},{3,1},{4,6},{5,7},{6,4},{7,5},{8,10},{9,11},{10,... | collective-permute-start | bytes 24584 | tf_op jit(solution)/shard_map/ppermute | solution.py:80
  13.7 3.7 %collective-permute-start.2 = (f32[1,2048]{1,0:T(1,128)S(1)}, f32[1,2048]{1,0:T(1,128)S(1)}, u32[]{:S(2)}, u32[]{:S(2)}) collective-permute-start(f32[1,2048]{1,0:T(1,128)S(1)} %get-tuple-element.12.refs_1_), channel_id=1, source_target_pairs={{0,3},{1,0},{2,1},{3,2},{4,7},{5,4},{6,5},{7,6},{8,11},{9,8},{10,9... | collective-permute-start | bytes 24584 | tf_op jit(solution)/shard_map/ppermute | solution.py:80
  19.5 1.2 collective-permute-start.3
  43.3 4.9 %collective-permute-start.4 = (f32[1,2048]{1,0:T(1,128)S(1)}, f32[1,2048]{1,0:T(1,128)S(1)}, u32[]{:S(2)}, u32[]{:S(2)}) collective-permute-start(f32[1,2048]{1,0:T(1,128)S(1)} %shard_map.43.refs_1_), channel_id=1, source_target_pairs={{0,1},{1,2},{2,3},{3,0},{4,5},{5,6},{6,7},{7,4},{8,9},{9,10},{10,1... | collective-permute-start | bytes 24584 | tf_op jit(solution)/shard_map/ppermute | solution.py:80
  43.5 5.6 %collective-permute-start.5 = (f32[1,2048]{1,0:T(1,128)S(1)}, f32[1,2048]{1,0:T(1,128)S(1)}, u32[]{:S(2)}, u32[]{:S(2)}) collective-permute-start(f32[1,2048]{1,0:T(1,128)S(1)} %shard_map.43.refs_1_), channel_id=1, source_target_pairs={{0,2},{1,3},{2,0},{3,1},{4,6},{5,7},{6,4},{7,5},{8,10},{9,11},{10,... | collective-permute-start | bytes 24584 | tf_op jit(solution)/shard_map/ppermute | solution.py:80
  47.4 3.7 %collective-permute-start.6 = (f32[1,2048]{1,0:T(1,128)S(1)}, f32[1,2048]{1,0:T(1,128)S(1)}, u32[]{:S(2)}, u32[]{:S(2)}) collective-permute-start(f32[1,2048]{1,0:T(1,128)S(1)} %shard_map.43.refs_1_), channel_id=1, source_target_pairs={{0,3},{1,0},{2,1},{3,2},{4,7},{5,4},{6,5},{7,6},{8,11},{9,8},{10,9... | collective-permute-start | bytes 24584 | tf_op jit(solution)/shard_map/ppermute | solution.py:80
  53.2 1.2 collective-permute-start.7
  70.5 3.7 %collective-permute-start.10 = (f32[1,2048]{1,0:T(1,128)S(1)}, f32[1,2048]{1,0:T(1,128)S(1)}, u32[]{:S(2)}, u32[]{:S(2)}) collective-permute-start(f32[1,2048]{1,0:T(1,128)S(1)} %shard_map.45.refs_1_), channel_id=1, source_target_pairs={{0,3},{1,0},{2,1},{3,2},{4,7},{5,4},{6,5},{7,6},{8,11},{9,8},{10,9... | collective-permute-start | bytes 24584 | tf_op jit(solution)/shard_map/ppermute | solution.py:80
  71.9 4.9 %collective-permute-start.8 = (f32[1,2048]{1,0:T(1,128)S(1)}, f32[1,2048]{1,0:T(1,128)S(1)}, u32[]{:S(2)}, u32[]{:S(2)}) collective-permute-start(f32[1,2048]{1,0:T(1,128)S(1)} %shard_map.45.refs_1_), channel_id=1, source_target_pairs={{0,1},{1,2},{2,3},{3,0},{4,5},{5,6},{6,7},{7,4},{8,9},{9,10},{10,1... | collective-permute-start | bytes 24584 | tf_op jit(solution)/shard_map/ppermute | solution.py:80
  72.6 5.2 %collective-permute-start.9 = (f32[1,2048]{1,0:T(1,128)S(1)}, f32[1,2048]{1,0:T(1,128)S(1)}, u32[]{:S(2)}, u32[]{:S(2)}) collective-permute-start(f32[1,2048]{1,0:T(1,128)S(1)} %shard_map.45.refs_1_), channel_id=1, source_target_pairs={{0,2},{1,3},{2,0},{3,1},{4,6},{5,7},{6,4},{7,5},{8,10},{9,11},{10,... | collective-permute-start | bytes 24584 | tf_op jit(solution)/shard_map/ppermute | solution.py:80
  79.1 3.2 %collective-permute-start.12 = (f32[256,896]{1,0:T(8,128)S(1)}, f32[256,896]{1,0:T(8,128)S(1)}, u32[]{:S(2)}, u32[]{:S(2)}) collective-permute-start(f32[256,896]{1,0:T(8,128)S(1)} %get-tuple-element.16), channel_id=1, source_target_pairs={{0,4},{4,0},{8,12},{12,8},{16,20},{20,16},{24,28},{28,24},{32,36},... | collective-permute-start | bytes 2752520 | tf_op jit(solution)/shard_map/ppermute | solution.py:31
  80.4 5.9 %collective-permute-start.11 = (f32[256,896]{1,0:T(8,128)S(1)}, f32[256,896]{1,0:T(8,128)S(1)}, u32[]{:S(2)}, u32[]{:S(2)}) collective-permute-start(f32[256,896]{1,0:T(8,128)S(1)} %shard_map.48), channel_id=1, source_target_pairs={{0,4},{4,0},{8,12},{12,8},{16,20},{20,16},{24,28},{28,24},{32,36},... | collective-permute-start | bytes 2752520 | tf_op jit(solution)/shard_map/ppermute | solution.py:31
  81.0 3.9 %copy-start.1 = (bf16[2048,768]{1,0:T(8,128)(2,1)S(1)}, bf16[2048,768]{1,0:T(8,128)(2,1)}, u32[]{:S(2)}) copy-start(bf16[2048,768]{1,0:T(8,128)(2,1)} %refs_2_.5) | copy-start | bytes 9437188
  82.6 8.4 %collective-permute-start.13 = (bf16[16,104,128]{2,1,0:T(8,128)(2,1)S(1)}, bf16[16,104,128]{2,1,0:T(8,128)(2,1)S(1)}, u32[]{:S(2)}, u32[]{:S(2)}) collective-permute-start(bf16[16,104,128]{2,1,0:T(8,128)(2,1)S(1)} %shard_map.50), channel_id=1, source_target_pairs={{0,8},{4,36},{8,0},{12,44},{16,24},{20,52},{24,16},{28,60},{32,40}... | collective-permute-start | bytes 1277960 | tf_op jit(solution)/shard_map/ppermute | solution.py:46
  131.2 8.1 %collective-permute-start.15 = (bf16[16,104,128]{2,1,0:T(8,128)(2,1)S(1)}, bf16[16,104,128]{2,1,0:T(8,128)(2,1)S(1)}, u32[]{:S(2)}, u32[]{:S(2)}) collective-permute-start(bf16[16,104,128]{2,1,0:T(8,128)(2,1)S(1)} %all_to_all.23.refs_3_), channel_id=1, source_target_pairs={{0,8},{4,36},{8,0},{12,44},{16,24},{20,52},{24,16},{28,60},{32,40}... | collective-permute-start | bytes 1277960 | tf_op jit(solution)/shard_map/ppermute | solution.py:46
  132.6 9.2 %collective-permute-start.14 = (bf16[16,104,128]{2,1,0:T(8,128)(2,1)S(1)}, bf16[16,104,128]{2,1,0:T(8,128)(2,1)S(1)}, u32[]{:S(2)}, u32[]{:S(2)}) collective-permute-start(bf16[16,104,128]{2,1,0:T(8,128)(2,1)S(1)} %all_to_all.23.refs_3_), channel_id=1, source_target_pairs={{0,4},{4,0},{8,12},{12,8},{16,20},{20,16},{24,28},{28,24},{32,36},... | collective-permute-start | bytes 1277960 | tf_op jit(solution)/shard_map/ppermute | solution.py:31
  139.3 3.7 %collective-permute-start.16 = (bf16[16,104,128]{2,1,0:T(8,128)(2,1)S(1)}, bf16[16,104,128]{2,1,0:T(8,128)(2,1)S(1)}, u32[]{:S(2)}, u32[]{:S(2)}) collective-permute-start(bf16[16,104,128]{2,1,0:T(8,128)(2,1)S(1)} %collective-permute-done.15.refs_3_), channel_id=1, source_target_pairs={{0,4},{4,0},{8,12},{12,8},{16,20},{20,16},{24,28},{28,24},{32,36},... | collective-permute-start | bytes 1277960 | tf_op jit(solution)/shard_map/ppermute | solution.py:31
  144.3 5.4 %collective-permute-start.17 = (f32[2,2048]{1,0:T(2,128)S(1)}, f32[2,2048]{1,0:T(2,128)S(1)}, u32[]{:S(2)}, u32[]{:S(2)}) collective-permute-start(f32[2,2048]{1,0:T(2,128)S(1)} %add_add_fusion.1), channel_id=1, source_target_pairs={{0,2},{1,3},{2,0},{3,1},{4,6},{5,7},{6,4},{7,5},{8,10},{9,11},{10,... | collective-permute-start | bytes 49160 | tf_op jit(solution)/shard_map/ppermute | solution.py:80
  145.9 4.9 %collective-permute-start.18 = (f32[2,2048]{1,0:T(2,128)S(1)}, f32[2,2048]{1,0:T(2,128)S(1)}, u32[]{:S(2)}, u32[]{:S(2)}) collective-permute-start(f32[2,2048]{1,0:T(2,128)S(1)} %add_add_fusion.1), channel_id=1, source_target_pairs={{0,1},{1,2},{2,3},{3,0},{4,5},{5,6},{6,7},{7,4},{8,9},{9,10},{10,1... | collective-permute-start | bytes 49160 | tf_op jit(solution)/shard_map/ppermute | solution.py:80
  147.7 3.7 %collective-permute-start.19 = (f32[2,2048]{1,0:T(2,128)S(1)}, f32[2,2048]{1,0:T(2,128)S(1)}, u32[]{:S(2)}, u32[]{:S(2)}) collective-permute-start(f32[2,2048]{1,0:T(2,128)S(1)} %add_add_fusion.1), channel_id=1, source_target_pairs={{0,3},{1,0},{2,1},{3,2},{4,7},{5,4},{6,5},{7,6},{8,11},{9,8},{10,9... | collective-permute-start | bytes 49160 | tf_op jit(solution)/shard_map/ppermute | solution.py:80

commit v8 on v7

--- a/solution.py
+++ b/solution.py
@@ -85,6 +85,13 @@
     top = jnp.maximum(value, theirs)
     value = top + jnp.log2(jnp.exp2(value - top) + jnp.exp2(theirs - top))
     return from_chips(value)
+
+
+def cen_others(value):
+    out = []
+    for step in (1, 2, 3):
+        out.append(cen_shift(value, step))
+    return out
 
 
 def on_lanes(row):
@@ -368,6 +375,11 @@
     both_ref[1:2, :] = jnp.sum(mass, axis=0, keepdims=True)
 
 
+def finish_kernel(own_ref, one_ref, two_ref, three_ref, distances_ref, *, width):
+    total = (own_ref[...] + two_ref[...]) + (one_ref[...] + three_ref[...])
+    distances_ref[...] = total[0:1] / total[1:2] / width
+
+
 VMEM = pl.BlockSpec(memory_space=pltpu.VMEM)
 
 
@@ -409,7 +421,7 @@
                 [strip] + pairs,
                 [scores, values],
             )
-        lines = [partial] + [cen_shift(partial, step) for step in (1, 2, 3)]
+        lines = [partial] + cen_others(partial)
         if iteration < ITERS - 1:
             col, row = call(
                 lambda *refs: col_kernel(*refs, level=row_level),
@@ -461,10 +473,10 @@
     both = terms(0, mine) + terms(2, theirs)
     theirs = other_core(near)
     both = both + (terms(1, near) + terms(3, theirs))
-    one, two, three = [cen_shift(both, step) for step in (1, 2, 3)]
-    total = (both + two) + (one + three)
-    distances = total[0] / total[1] / width
-    return (own_rows, distances)
+    (distances,) = call(
+        lambda *refs: finish_kernel(*refs, width=width), [line], [], [both] + cen_others(both)
+    )
+    return (own_rows, distances.reshape(count))
 
 
 def solution(mesh):

time: 153 us -> 154 us (level)
    pallas_call x16 -> x17, Pallas kernels: 25.3 us -> 25.9 us  [call(): pl.pallas_call(kernel, out_shape=[jax.ShapeDtypeStruct(shape, dtype) for...]
where the time goes in v8:
time: 154 us; the launch traced here: 153 us
  blocking collectives  73.2 us (48%)
  waiting for transfers between devices  26.9 us (17%)
  Pallas kernels  25.9 us (17%)
  starting transfers between devices  22.3 us (14%)
  local copies, waits for them, and re-layouts  3.44 us (2%)
    all_to_all x4, blocking collectives, exchange(): return lax.all_to_all(value, 'pts', 0, 0, axis_index_groups=groups)  73.2 us
    pallas_call x17, Pallas kernels, call(): pl.pallas_call(kernel, out_shape=[jax.ShapeDtypeStruct(shape, dtype) for...  25.9 us
    ppermute x12, starting transfers between devices, cen_shift(): lax.ppermute(value, 'cen', [(i, (i + step) % size) for i in range(size)])  18 us
    ppermute x12, waiting for transfers between devices, cen_shift(): lax.ppermute(value, 'cen', [(i, (i + step) % size) for i in range(size)])  13.1 us
    ppermute x2, waiting for transfers between devices, other_parity(): lax.ppermute(value, 'pts', [(i, i ^ flip[i % C]) for i in range(size)])  11.4 us
    ppermute x2, starting transfers between devices, other_parity(): lax.ppermute(value, 'pts', [(i, i ^ flip[i % C]) for i in range(size)])  3.7 us
    unnamed x6, local copies, waits for them, and re-layouts  3.3 us
  transfers between devices with their start and end apart: 20, of which 15 were waited for; matrix products, arithmetic and copies ran while one was open for 0% of the time, Pallas kernels for 5%

profile of v8, /device:TPU:2, one launch (start us, length us, event | category | flops | bytes accessed | tf_op | source)
XLA Modules:
  0.0 152.7 jit_solution(2328646304937103475)
XLA Ops:
  0.6 1.9 %copy-done = bf16[2048,768]{1,0:T(8,128)(2,1)S(1)} copy-done((bf16[2048,768]{1,0:T(8,128)(2,1)S(1)}, bf16[2048,768]{1,0:T(8,128)(2,1)}, u32[]{:S(2)}) %copy-start) | copy-done | bytes 3145752
  2.5 1.4 copy-done.2
  3.9 5.2 %shard_map.41 = (f32[1024,2048]{1,0:T(8,128)S(1)}, f32[1,2048]{1,0:T(1,128)S(1)}, bf16[768,2048]{1,0:T(8,128)(2,1)S(1)}) custom-call(bf16[2048,768]{1,0:T(8,128)(2,1)S(1)} %copy-done, bf16[1024,768]{1,0:T(8,128)(2,1)S(1)} %copy-done.2), custom_call_target="tpu_custom_call" | custom-call | tf_op jit(solution)/shard_map/pallas_call | solution.py:387
  9.2 1.7 %collective-permute-start = (f32[1,2048]{1,0:T(1,128)S(1)}, f32[1,2048]{1,0:T(1,128)S(1)}, u32[]{:S(2)}, u32[]{:S(2)}) collective-permute-start(f32[1,2048]{1,0:T(1,128)S(1)} %get-tuple-element.12.refs_1_), channel_id=1, source_target_pairs={{0,1},{1,2},{2,3},{3,0},{4,5},{5,6},{6,7},{7,4},{8,9},{9,10},{10,1... | collective-permute-start | bytes 24584 | tf_op jit(solution)/shard_map/ppermute | solution.py:80
  10.8 2.9 %collective-permute-start.1 = (f32[1,2048]{1,0:T(1,128)S(1)}, f32[1,2048]{1,0:T(1,128)S(1)}, u32[]{:S(2)}, u32[]{:S(2)}) collective-permute-start(f32[1,2048]{1,0:T(1,128)S(1)} %get-tuple-element.12.refs_1_), channel_id=1, source_target_pairs={{0,2},{1,3},{2,0},{3,1},{4,6},{5,7},{6,4},{7,5},{8,10},{9,11},{10,... | collective-permute-start | bytes 24584 | tf_op jit(solution)/shard_map/ppermute | solution.py:80
  13.7 1.3 collective-permute-start.2
  15.1 0.9 collective-permute-done.1.refs_3_
  16.0 1.4 collective-permute-done.2.refs_4_
  17.4 2.2 %shard_map.42 = (f32[1,1024]{1,0:T(1,128)S(1)}, f32[1,2048]{1,0:T(1,128)}) custom-call(f32[1024,2048]{1,0:T(8,128)S(1)} %get-tuple-element.11.refs_0_, f32[1,2048]{1,0:T(1,128)S(1)} %get-tuple-element.12.refs_1_, f32[1,2048]{1,0:T(1,128)S(1)} %collective-permute-done.refs_2_, f32[1,2048]{1,0:T(1,128)S(1)} %collective-permute-done.1.refs_3_, ...), custom_call_target="tpu_custom_call" | custom-call | tf_op jit(solution)/shard_map/pallas_call | solution.py:387
  19.5 1.2 collective-permute-done.3
  20.8 20.5 %all_to_all.20.refs_1_ = f32[32,1,1024]{2,1,0:T(1,128)S(1)} all-to-all(f32[32,1,1024]{2,1,0:T(1,128)S(1)} %broadcast_in_dim.17), channel_id=1, replica_groups={{0,8,16,24,32,40,48,56,64,72,80,88,96,104,112,120,128,136,144,152,160,1..., dimensions={0} | all-to-all | bytes 262144 | tf_op jit(solution)/shard_map/all_to_all | solution.py:70
  41.3 1.9 %shard_map.43.refs_1_ = f32[1,2048]{1,0:T(1,128)S(1)} custom-call(f32[1024,2048]{1,0:T(8,128)S(1)} %get-tuple-element.11.refs_0_, f32[32,1,1024]{2,1,0:T(1,128)S(1)} %all_to_all.20.refs_1_), custom_call_target="tpu_custom_call" | custom-call | tf_op jit(solution)/shard_map/pallas_call | solution.py:387
  43.5 3.8 %collective-permute-start.5 = (f32[1,2048]{1,0:T(1,128)S(1)}, f32[1,2048]{1,0:T(1,128)S(1)}, u32[]{:S(2)}, u32[]{:S(2)}) collective-permute-start(f32[1,2048]{1,0:T(1,128)S(1)} %shard_map.43.refs_1_), channel_id=1, source_target_pairs={{0,2},{1,3},{2,0},{3,1},{4,6},{5,7},{6,4},{7,5},{8,10},{9,11},{10,... | collective-permute-start | bytes 24584 | tf_op jit(solution)/shard_map/ppermute | solution.py:80
  47.5 0.7 collective-permute-done.4.refs_2_
  48.2 0.9 collective-permute-done.5.refs_3_
  49.1 1.9 %collective-permute-done.6.refs_4_ = f32[1,2048]{1,0:T(1,128)S(1)} collective-permute-done((f32[1,2048]{1,0:T(1,128)S(1)}, f32[1,2048]{1,0:T(1,128)S(1)}, u32[]{:S(2)}, u32[]{:S(2)}) %collective-permute-start.6) | collective-permute-done | bytes 8224 | tf_op jit(solution)/shard_map/ppermute | solution.py:80
  51.0 2.2 %shard_map.44 = (f32[1,1024]{1,0:T(1,128)S(1)}, f32[1,2048]{1,0:T(1,128)}) custom-call(f32[1024,2048]{1,0:T(8,128)S(1)} %get-tuple-element.11.refs_0_, f32[1,2048]{1,0:T(1,128)S(1)} %shard_map.43.refs_1_, f32[1,2048]{1,0:T(1,128)S(1)} %collective-permute-done.4.refs_2_, f32[1,2048]{1,0:T(1,128)S(1)} %collective-permute-done.5.refs_3_, ...), custom_call_target="tpu_custom_call" | custom-call | tf_op jit(solution)/shard_map/pallas_call | solution.py:387
  53.2 1.2 collective-permute-done.7
  54.5 14.1 %all_to_all.21.refs_1_ = f32[32,1,1024]{2,1,0:T(1,128)S(1)} all-to-all(f32[32,1,1024]{2,1,0:T(1,128)S(1)} %broadcast_in_dim.19), channel_id=1, replica_groups={{0,8,16,24,32,40,48,56,64,72,80,88,96,104,112,120,128,136,144,152,160,1..., dimensions={0} | all-to-all | bytes 262144 | tf_op jit(solution)/shard_map/all_to_all | solution.py:70
  68.6 1.9 %shard_map.45.refs_1_ = f32[1,2048]{1,0:T(1,128)S(1)} custom-call(f32[1024,2048]{1,0:T(8,128)S(1)} %get-tuple-element.11.refs_0_, f32[32,1,1024]{2,1,0:T(1,128)S(1)} %all_to_all.21.refs_1_), custom_call_target="tpu_custom_call" | custom-call | tf_op jit(solution)/shard_map/pallas_call | solution.py:387
  70.5 1.4 collective-permute-start.10
  71.9 0.7 collective-permute-start.8
  72.6 1.5 collective-permute-start.9
  74.2 2.5 %collective-permute-done.8.refs_2_ = f32[1,2048]{1,0:T(1,128)S(1)} collective-permute-done((f32[1,2048]{1,0:T(1,128)S(1)}, f32[1,2048]{1,0:T(1,128)S(1)}, u32[]{:S(2)}, u32[]{:S(2)}) %collective-permute-start.8) | collective-permute-done | bytes 8224 | tf_op jit(solution)/shard_map/ppermute | solution.py:80
  76.8 1.0 collective-permute-done.9.refs_3_
  77.8 1.3 shard_map.46
  79.2 1.3 shard_map.48
  80.4 0.6 collective-permute-start.11
  81.0 1.3 shard_map.49.mine_ref
  82.3 0.3 shard_map.50
  82.6 2.3 %collective-permute-start.13 = (bf16[16,104,128]{2,1,0:T(8,128)(2,1)S(1)}, bf16[16,104,128]{2,1,0:T(8,128)(2,1)S(1)}, u32[]{:S(2)}, u32[]{:S(2)}) collective-permute-start(bf16[16,104,128]{2,1,0:T(8,128)(2,1)S(1)} %shard_map.50), channel_id=1, source_target_pairs={{0,8},{4,36},{8,0},{12,44},{16,24},{20,52},{24,16},{28,60},{32,40}... | collective-permute-start | bytes 1277960 | tf_op jit(solution)/shard_map/ppermute | solution.py:46
  84.9 1.4 shard_map.47.mine_ref
  86.3 4.7 %collective-permute-done.13.refs_0_ = bf16[16,104,128]{2,1,0:T(8,128)(2,1)S(1)} collective-permute-done((bf16[16,104,128]{2,1,0:T(8,128)(2,1)S(1)}, bf16[16,104,128]{2,1,0:T(8,128)(2,1)S(1)}, u32[]{:S(2)}, u32[]{:S(2)}) %collective-permute-start.13) | collective-permute-done | bytes 426016 | tf_op jit(solution)/shard_map/ppermute | solution.py:46
  91.0 0.5 shard_map.51
  91.6 19.9 %all_to_all.22.refs_0_ = bf16[16,104,128]{2,1,0:T(8,128)(2,1)S(1)} all-to-all(bf16[16,104,128]{2,1,0:T(8,128)(2,1)S(1)} %shard_map.51), channel_id=1, replica_groups={{0,16,32,48,64,80,96,112,128,144,160,176,192,208,224,240},{8,24,40,56,7..., dimensions={0} | all-to-all | bytes 851968 | tf_op jit(solution)/shard_map/all_to_all | solution.py:70
  111.5 0.9 shard_map.52
  112.4 18.8 %all_to_all.23.refs_3_ = bf16[16,104,128]{2,1,0:T(8,128)(2,1)S(1)} all-to-all(bf16[16,104,128]{2,1,0:T(8,128)(2,1)S(1)} %get-tuple-element.19), channel_id=1, replica_groups={{0,16,32,48,64,80,96,112,128,144,160,176,192,208,224,240},{8,24,40,56,7..., dimensions={0} | all-to-all | bytes 851968 | tf_op jit(solution)/shard_map/all_to_all | solution.py:70
  131.2 1.4 collective-permute-start.15
  132.6 6.7 %collective-permute-done.15.refs_3_ = bf16[16,104,128]{2,1,0:T(8,128)(2,1)S(1)} collective-permute-done((bf16[16,104,128]{2,1,0:T(8,128)(2,1)S(1)}, bf16[16,104,128]{2,1,0:T(8,128)(2,1)S(1)}, u32[]{:S(2)}, u32[]{:S(2)}) %collective-permute-start.15) | collective-permute-done | bytes 426016 | tf_op jit(solution)/shard_map/ppermute | solution.py:46
  139.3 1.2 shard_map.53
  140.5 1.2 shard_map.55
  141.8 1.2 shard_map.54
  143.0 1.2 shard_map.56
  144.4 3.9 %collective-permute-start.18 = (f32[2,2048]{1,0:T(2,128)S(1)}, f32[2,2048]{1,0:T(2,128)S(1)}, u32[]{:S(2)}, u32[]{:S(2)}) collective-permute-start(f32[2,2048]{1,0:T(2,128)S(1)} %add_add_fusion.refs_0_), channel_id=1, source_target_pairs={{0,2},{1,3},{2,0},{3,1},{4,6},{5,7},{6,4},{7,5},{8,10},{9,11},{10,... | collective-permute-start | bytes 49160 | tf_op jit(solution)/shard_map/ppermute | solution.py:80
  148.5 0.8 collective-permute-done.17.refs_1_
  149.3 0.9 collective-permute-done.18.refs_2_
  150.2 1.9 %collective-permute-done.19.refs_3_ = f32[2,2048]{1,0:T(2,128)S(1)} collective-permute-done((f32[2,2048]{1,0:T(2,128)S(1)}, f32[2,2048]{1,0:T(2,128)S(1)}, u32[]{:S(2)}, u32[]{:S(2)}) %collective-permute-start.19) | collective-permute-done | bytes 16416 | tf_op jit(solution)/shard_map/ppermute | solution.py:80
  152.1 0.6 shard_map.57
  (26 shorter events, 1.1 us)
Async XLA Ops:
  0.6 1.9 %copy-start = (bf16[2048,768]{1,0:T(8,128)(2,1)S(1)}, bf16[2048,768]{1,0:T(8,128)(2,1)}, u32[]{:S(2)}) copy-start(bf16[2048,768]{1,0:T(8,128)(2,1)} %refs_2_.5) | copy-start | bytes 9437188
  2.5 1.4 copy-start.2
  9.2 5.9 %collective-permute-start = (f32[1,2048]{1,0:T(1,128)S(1)}, f32[1,2048]{1,0:T(1,128)S(1)}, u32[]{:S(2)}, u32[]{:S(2)}) collective-permute-start(f32[1,2048]{1,0:T(1,128)S(1)} %get-tuple-element.12.refs_1_), channel_id=1, source_target_pairs={{0,1},{1,2},{2,3},{3,0},{4,5},{5,6},{6,7},{7,4},{8,9},{9,10},{10,1... | collective-permute-start | bytes 24584 | tf_op jit(solution)/shard_map/ppermute | solution.py:80
  10.8 5.2 %collective-permute-start.1 = (f32[1,2048]{1,0:T(1,128)S(1)}, f32[1,2048]{1,0:T(1,128)S(1)}, u32[]{:S(2)}, u32[]{:S(2)}) collective-permute-start(f32[1,2048]{1,0:T(1,128)S(1)} %get-tuple-element.12.refs_1_), channel_id=1, source_target_pairs={{0,2},{1,3},{2,0},{3,1},{4,6},{5,7},{6,4},{7,5},{8,10},{9,11},{10,... | collective-permute-start | bytes 24584 | tf_op jit(solution)/shard_map/ppermute | solution.py:80
  13.7 3.7 %collective-permute-start.2 = (f32[1,2048]{1,0:T(1,128)S(1)}, f32[1,2048]{1,0:T(1,128)S(1)}, u32[]{:S(2)}, u32[]{:S(2)}) collective-permute-start(f32[1,2048]{1,0:T(1,128)S(1)} %get-tuple-element.12.refs_1_), channel_id=1, source_target_pairs={{0,3},{1,0},{2,1},{3,2},{4,7},{5,4},{6,5},{7,6},{8,11},{9,8},{10,9... | collective-permute-start | bytes 24584 | tf_op jit(solution)/shard_map/ppermute | solution.py:80
  19.5 1.2 collective-permute-start.3
  43.3 4.9 %collective-permute-start.4 = (f32[1,2048]{1,0:T(1,128)S(1)}, f32[1,2048]{1,0:T(1,128)S(1)}, u32[]{:S(2)}, u32[]{:S(2)}) collective-permute-start(f32[1,2048]{1,0:T(1,128)S(1)} %shard_map.43.refs_1_), channel_id=1, source_target_pairs={{0,1},{1,2},{2,3},{3,0},{4,5},{5,6},{6,7},{7,4},{8,9},{9,10},{10,1... | collective-permute-start | bytes 24584 | tf_op jit(solution)/shard_map/ppermute | solution.py:80
  43.5 5.6 %collective-permute-start.5 = (f32[1,2048]{1,0:T(1,128)S(1)}, f32[1,2048]{1,0:T(1,128)S(1)}, u32[]{:S(2)}, u32[]{:S(2)}) collective-permute-start(f32[1,2048]{1,0:T(1,128)S(1)} %shard_map.43.refs_1_), channel_id=1, source_target_pairs={{0,2},{1,3},{2,0},{3,1},{4,6},{5,7},{6,4},{7,5},{8,10},{9,11},{10,... | collective-permute-start | bytes 24584 | tf_op jit(solution)/shard_map/ppermute | solution.py:80
  47.4 3.7 %collective-permute-start.6 = (f32[1,2048]{1,0:T(1,128)S(1)}, f32[1,2048]{1,0:T(1,128)S(1)}, u32[]{:S(2)}, u32[]{:S(2)}) collective-permute-start(f32[1,2048]{1,0:T(1,128)S(1)} %shard_map.43.refs_1_), channel_id=1, source_target_pairs={{0,3},{1,0},{2,1},{3,2},{4,7},{5,4},{6,5},{7,6},{8,11},{9,8},{10,9... | collective-permute-start | bytes 24584 | tf_op jit(solution)/shard_map/ppermute | solution.py:80
  53.2 1.2 collective-permute-start.7
  70.5 3.7 %collective-permute-start.10 = (f32[1,2048]{1,0:T(1,128)S(1)}, f32[1,2048]{1,0:T(1,128)S(1)}, u32[]{:S(2)}, u32[]{:S(2)}) collective-permute-start(f32[1,2048]{1,0:T(1,128)S(1)} %shard_map.45.refs_1_), channel_id=1, source_target_pairs={{0,3},{1,0},{2,1},{3,2},{4,7},{5,4},{6,5},{7,6},{8,11},{9,8},{10,9... | collective-permute-start | bytes 24584 | tf_op jit(solution)/shard_map/ppermute | solution.py:80
  71.9 4.9 %collective-permute-start.8 = (f32[1,2048]{1,0:T(1,128)S(1)}, f32[1,2048]{1,0:T(1,128)S(1)}, u32[]{:S(2)}, u32[]{:S(2)}) collective-permute-start(f32[1,2048]{1,0:T(1,128)S(1)} %shard_map.45.refs_1_), channel_id=1, source_target_pairs={{0,1},{1,2},{2,3},{3,0},{4,5},{5,6},{6,7},{7,4},{8,9},{9,10},{10,1... | collective-permute-start | bytes 24584 | tf_op jit(solution)/shard_map/ppermute | solution.py:80
  72.6 5.2 %collective-permute-start.9 = (f32[1,2048]{1,0:T(1,128)S(1)}, f32[1,2048]{1,0:T(1,128)S(1)}, u32[]{:S(2)}, u32[]{:S(2)}) collective-permute-start(f32[1,2048]{1,0:T(1,128)S(1)} %shard_map.45.refs_1_), channel_id=1, source_target_pairs={{0,2},{1,3},{2,0},{3,1},{4,6},{5,7},{6,4},{7,5},{8,10},{9,11},{10,... | collective-permute-start | bytes 24584 | tf_op jit(solution)/shard_map/ppermute | solution.py:80
  79.1 3.2 %collective-permute-start.12 = (f32[256,896]{1,0:T(8,128)S(1)}, f32[256,896]{1,0:T(8,128)S(1)}, u32[]{:S(2)}, u32[]{:S(2)}) collective-permute-start(f32[256,896]{1,0:T(8,128)S(1)} %get-tuple-element.16), channel_id=1, source_target_pairs={{0,4},{4,0},{8,12},{12,8},{16,20},{20,16},{24,28},{28,24},{32,36},... | collective-permute-start | bytes 2752520 | tf_op jit(solution)/shard_map/ppermute | solution.py:31
  80.4 5.9 %collective-permute-start.11 = (f32[256,896]{1,0:T(8,128)S(1)}, f32[256,896]{1,0:T(8,128)S(1)}, u32[]{:S(2)}, u32[]{:S(2)}) collective-permute-start(f32[256,896]{1,0:T(8,128)S(1)} %shard_map.48), channel_id=1, source_target_pairs={{0,4},{4,0},{8,12},{12,8},{16,20},{20,16},{24,28},{28,24},{32,36},... | collective-permute-start | bytes 2752520 | tf_op jit(solution)/shard_map/ppermute | solution.py:31
  81.0 3.9 %copy-start.1 = (bf16[2048,768]{1,0:T(8,128)(2,1)S(1)}, bf16[2048,768]{1,0:T(8,128)(2,1)}, u32[]{:S(2)}) copy-start(bf16[2048,768]{1,0:T(8,128)(2,1)} %refs_2_.5) | copy-start | bytes 9437188
  82.6 8.4 %collective-permute-start.13 = (bf16[16,104,128]{2,1,0:T(8,128)(2,1)S(1)}, bf16[16,104,128]{2,1,0:T(8,128)(2,1)S(1)}, u32[]{:S(2)}, u32[]{:S(2)}) collective-permute-start(bf16[16,104,128]{2,1,0:T(8,128)(2,1)S(1)} %shard_map.50), channel_id=1, source_target_pairs={{0,8},{4,36},{8,0},{12,44},{16,24},{20,52},{24,16},{28,60},{32,40}... | collective-permute-start | bytes 1277960 | tf_op jit(solution)/shard_map/ppermute | solution.py:46
  131.2 8.1 %collective-permute-start.15 = (bf16[16,104,128]{2,1,0:T(8,128)(2,1)S(1)}, bf16[16,104,128]{2,1,0:T(8,128)(2,1)S(1)}, u32[]{:S(2)}, u32[]{:S(2)}) collective-permute-start(bf16[16,104,128]{2,1,0:T(8,128)(2,1)S(1)} %all_to_all.23.refs_3_), channel_id=1, source_target_pairs={{0,8},{4,36},{8,0},{12,44},{16,24},{20,52},{24,16},{28,60},{32,40}... | collective-permute-start | bytes 1277960 | tf_op jit(solution)/shard_map/ppermute | solution.py:46
  132.6 9.2 %collective-permute-start.14 = (bf16[16,104,128]{2,1,0:T(8,128)(2,1)S(1)}, bf16[16,104,128]{2,1,0:T(8,128)(2,1)S(1)}, u32[]{:S(2)}, u32[]{:S(2)}) collective-permute-start(bf16[16,104,128]{2,1,0:T(8,128)(2,1)S(1)} %all_to_all.23.refs_3_), channel_id=1, source_target_pairs={{0,4},{4,0},{8,12},{12,8},{16,20},{20,16},{24,28},{28,24},{32,36},... | collective-permute-start | bytes 1277960 | tf_op jit(solution)/shard_map/ppermute | solution.py:31
  139.3 3.7 %collective-permute-start.16 = (bf16[16,104,128]{2,1,0:T(8,128)(2,1)S(1)}, bf16[16,104,128]{2,1,0:T(8,128)(2,1)S(1)}, u32[]{:S(2)}, u32[]{:S(2)}) collective-permute-start(bf16[16,104,128]{2,1,0:T(8,128)(2,1)S(1)} %collective-permute-done.15.refs_3_), channel_id=1, source_target_pairs={{0,4},{4,0},{8,12},{12,8},{16,20},{20,16},{24,28},{28,24},{32,36},... | collective-permute-start | bytes 1277960 | tf_op jit(solution)/shard_map/ppermute | solution.py:31
  144.3 5.0 %collective-permute-start.17 = (f32[2,2048]{1,0:T(2,128)S(1)}, f32[2,2048]{1,0:T(2,128)S(1)}, u32[]{:S(2)}, u32[]{:S(2)}) collective-permute-start(f32[2,2048]{1,0:T(2,128)S(1)} %add_add_fusion.refs_0_), channel_id=1, source_target_pairs={{0,1},{1,2},{2,3},{3,0},{4,5},{5,6},{6,7},{7,4},{8,9},{9,10},{10,1... | collective-permute-start | bytes 49160 | tf_op jit(solution)/shard_map/ppermute | solution.py:80
  144.4 5.8 %collective-permute-start.18 = (f32[2,2048]{1,0:T(2,128)S(1)}, f32[2,2048]{1,0:T(2,128)S(1)}, u32[]{:S(2)}, u32[]{:S(2)}) collective-permute-start(f32[2,2048]{1,0:T(2,128)S(1)} %add_add_fusion.refs_0_), channel_id=1, source_target_pairs={{0,2},{1,3},{2,0},{3,1},{4,6},{5,7},{6,4},{7,5},{8,10},{9,11},{10,... | collective-permute-start | bytes 49160 | tf_op jit(solution)/shard_map/ppermute | solution.py:80
  148.3 3.7 %collective-permute-start.19 = (f32[2,2048]{1,0:T(2,128)S(1)}, f32[2,2048]{1,0:T(2,128)S(1)}, u32[]{:S(2)}, u32[]{:S(2)}) collective-permute-start(f32[2,2048]{1,0:T(2,128)S(1)} %add_add_fusion.refs_0_), channel_id=1, source_target_pairs={{0,3},{1,0},{2,1},{3,2},{4,7},{5,4},{6,5},{7,6},{8,11},{9,8},{10,9... | collective-permute-start | bytes 49160 | tf_op jit(solution)/shard_map/ppermute | solution.py:80
